TPU v7x, 32 devices: a whole 2x2x4 slice. The times are simulated.
32 devices in a mesh: dp: 8 (over z, y), mp: 4 (over x, core).
Axes of the slice: x: 2, y: 2, z: 4, core: 2. Of those that a mesh axis runs over, the one named last changes fastest.
Arguments:
- tokens: bfloat16 [32768, 512], P(('dp', 'mp')), may hold values from -6 to 6
- segment_ids: int32 [32, 1024], P('dp'), may hold values from 0 to 22, as said below
- cotangent: bfloat16 [32768, 512], P(('dp', 'mp')), may hold values from -6 to 6
- step_count: int32 [1], replicated, may hold values from 2 to 20
- mixer_weights: float32 [512, 4, 512], P('dp', None, 'mp')
- mixer_moment: float32 [512, 4, 512], P('dp', None, 'mp')
- mixer_second: float32 [512, 4, 512], P('dp', None, 'mp')
- feed_weights: float32 [512, 2, 2048], P('dp', None, 'mp')
- feed_moment: float32 [512, 2, 2048], P('dp', None, 'mp')
- feed_second: float32 [512, 2, 2048], P('dp', None, 'mp')
- sorter_weights: float32 [512, 256], P('dp', 'mp'), may hold values from -1.5 to 1.5
- sorter_moment: float32 [512, 256], P('dp', 'mp')
- sorter_second: float32 [512, 256], P('dp', 'mp')
- norm_gains: float32 [2, 512], P(None, ('dp', 'mp')), may hold values from 0.5 to 1.5
- gain_moment: float32 [2, 512], P(None, ('dp', 'mp'))
- gain_second: float32 [2, 512], P(None, ('dp', 'mp'))
Outputs:
- block_output: bfloat16 [32768, 512], P(('dp', 'mp'))
- token_grad: float32 [32768, 512], P(('dp', 'mp'))
- penalty: float32 [1], replicated
- mixer_momentum: float32 [512, 4, 512], P('dp', None, 'mp')
- mixer_variance: float32 [512, 4, 512], P('dp', None, 'mp')
- mixer_master: float32 [512, 4, 512], P('dp', None, 'mp')
- feed_momentum: float32 [512, 2, 2048], P('dp', None, 'mp')
- feed_variance: float32 [512, 2, 2048], P('dp', None, 'mp')
- feed_master: float32 [512, 2, 2048], P('dp', None, 'mp')
- sorter_momentum: float32 [512, 256], P('dp', 'mp')
- sorter_variance: float32 [512, 256], P('dp', 'mp')
- sorter_master: float32 [512, 256], P('dp', 'mp')
- gain_momentum: float32 [2, 512], P(None, ('dp', 'mp'))
- gain_variance: float32 [2, 512], P(None, ('dp', 'mp'))
- gain_master: float32 [2, 512], P(None, ('dp', 'mp'))
Inputs may be any that keep to these rules, and one draw needn't show every extreme that they name: `segment_ids`: 0 marks padding, which only follows the sentences at the end of a sequence; nonzero ids never fall along a sequence.
All inputs are finite; a program needn't handle non-finite values.
Results may differ from a plain program's by a relative error of at most 0.028.
The roundings to bfloat16 on the way count: a program that leaves them out, or rounds other values in their place, can miss the bound.
Values may be sent and summed in bfloat16 or wider, within the bound.
A program may use at most 192 MiB of HBM per device.

v0:
```python
import jax
import jax.numpy as jnp
from jax import lax
from jax.sharding import PartitionSpec as P

WIDTH = 512
HEADS = 8
HEAD_DIM = 64
BLOCK = 32
SINK_ITERS = 8
SEQ_LEN = 1024
BLOCKS = 32


norm_eps = 1e-05
softness_factor = 0.75
excluded_fill = -1000000000.0
penalty_weight = 0.1
beta_first = 0.9
beta_second = 0.95
adam_eps = 1e-08
weight_decay = 0.1
rate_mixer = 0.2
rate_feed = 0.1
rate_sorter = 0.6
rate_gains = 1.0


def cross(left_rows, right_rows):
    return lax.dot_general(
        left_rows, right_rows, (((0,), (0,)), ((), ())), preferred_element_type=jnp.float32
    )


def times_t(left_rows, right_rows):
    return lax.dot_general(
        left_rows, right_rows, (((1,), (1,)), ((), ())), preferred_element_type=jnp.float32
    )


def normalize(block_rows, gain):
    centred = block_rows - jnp.mean(block_rows, axis=-1, keepdims=True)
    inverse = lax.rsqrt(jnp.mean(centred * centred, axis=-1, keepdims=True) + norm_eps)
    normed = centred * inverse
    return (normed, inverse, normed * gain)


def norm_back(grad_out, normed, inverse, gain):
    scaled = grad_out * gain
    grad_in = inverse * (
        scaled
        - jnp.mean(scaled, axis=-1, keepdims=True)
        - normed * jnp.mean(scaled * normed, axis=-1, keepdims=True)
    )
    return (grad_in, jnp.sum(grad_out * normed, axis=0))


def balancing_terms(logit_matrix, permitted_pairs, genuine_rows):
    present_iterate = jnp.where(permitted_pairs, logit_matrix / softness_factor, excluded_fill)
    for sweep in range(SINK_ITERS):
        present_iterate = present_iterate - jax.nn.logsumexp(
            present_iterate, axis=-1, keepdims=True
        )
        present_iterate = present_iterate - jax.nn.logsumexp(
            present_iterate, axis=-2, keepdims=True
        )
    weights = jnp.exp(present_iterate)
    sorting_entropy = -jnp.sum(jnp.where(genuine_rows, weights * present_iterate, 0.0))
    return (weights, sorting_entropy)


def block_masks(segments):
    real_blocks = segments[:, ::BLOCK] > 0
    diagonal = jnp.arange(BLOCKS)[:, None] == jnp.arange(BLOCKS)[None, :]
    permitted_pairs = real_blocks[:, None, :, None] & real_blocks[:, None, None, :] | diagonal
    return (real_blocks, permitted_pairs, real_blocks[:, None, :, None])


def token_masks(segments):
    groups = segments.shape[0]
    token_ids = segments.reshape(groups, BLOCKS, BLOCK)
    near_mask = token_ids[:, :, :, None] == token_ids[:, :, None, :]
    far_mask = jnp.broadcast_to(token_ids[:, :, :, None] > 0, near_mask.shape)
    return jnp.concatenate([near_mask, far_mask], axis=-1)[:, None]


def gather_rows(block_rows):
    return lax.all_gather(block_rows, "mp", axis=0, tiled=True)


def scatter_rows(term_fn, local_rows):
    return lax.psum_scatter(
        term_fn(jnp.int32(0), local_rows * lax.axis_size("mp")),
        "mp",
        scatter_dimension=0,
        tiled=True,
    )


def adamw(master, moment, second, grad, rate, step_value):
    moment_new = beta_first * moment + (1.0 - beta_first) * grad
    second_new = beta_second * second + (1.0 - beta_second) * grad * grad
    first_hat = moment_new / (1.0 - beta_first**step_value)
    second_hat = second_new / (1.0 - beta_second**step_value)
    master_new = master - rate * (
        first_hat / (jnp.sqrt(second_hat) + adam_eps) + weight_decay * master
    )
    return (moment_new, second_new, master_new)


def local(
    tokens,
    segment_ids,
    cotangent,
    step_count,
    mixer_weights,
    mixer_moment,
    mixer_second,
    feed_weights,
    feed_moment,
    feed_second,
    sorter_weights,
    sorter_moment,
    sorter_second,
    norm_gains,
    gain_moment,
    gain_second,
):
    local_rows = tokens.shape[0]
    tile_size = BLOCK * HEAD_DIM
    total_tokens = lax.axis_size("dp") * segment_ids.shape[0] * SEQ_LEN
    score_scale = HEAD_DIM ** (-0.5)
    mixer_low, feed_split, sorter_low = (
        lax.all_gather(mixer_weights.astype(jnp.bfloat16), "dp", axis=0, tiled=True),
        lax.all_gather(feed_weights.astype(jnp.bfloat16), "dp", axis=0, tiled=True),
        lax.all_gather(sorter_weights.astype(jnp.bfloat16), "dp", axis=0, tiled=True),
    )
    gain_rows = lax.all_gather(norm_gains, ("dp", "mp"), axis=1, tiled=True)

    def spread_rows(block_rows):
        return gather_rows(block_rows)

    def sum_rows(term_fn):
        return scatter_rows(term_fn, local_rows)

    groups = segment_ids.shape[0]
    group_rows = groups * SEQ_LEN
    width_here = mixer_low.shape[2]
    heads_here = width_here // HEAD_DIM

    def to_blocks(flat):
        return flat.reshape(groups, BLOCKS, BLOCK, heads_here, HEAD_DIM).transpose(0, 3, 1, 2, 4)

    def from_blocks(blocked):
        return blocked.transpose(0, 2, 3, 1, 4).reshape(group_rows, heads_here * HEAD_DIM)

    inputs_f = tokens.astype(jnp.float32)
    normed_first, inverse_first, scaled_first = normalize(inputs_f, gain_rows[0])
    first_all = spread_rows(scaled_first.astype(jnp.bfloat16))
    proj_weights = mixer_low[:, :3, :].reshape(WIDTH, 3 * width_here)
    projected = jnp.dot(first_all, proj_weights, preferred_element_type=jnp.float32).astype(
        jnp.bfloat16
    )
    query_blocks = to_blocks(projected[:, :width_here])
    key_blocks = to_blocks(projected[:, width_here : 2 * width_here])
    value_blocks = to_blocks(projected[:, 2 * width_here :])
    block_means = (
        jnp.sum(first_all.reshape(groups * BLOCKS, BLOCK, WIDTH), axis=1, dtype=jnp.float32) / BLOCK
    ).astype(jnp.bfloat16)
    sorting_logit_rows = jnp.dot(block_means, sorter_low, preferred_element_type=jnp.float32)
    sorting_logit_rows = sorting_logit_rows.reshape(groups, BLOCKS, heads_here, BLOCKS).transpose(
        0, 2, 1, 3
    )
    real_blocks, permitted_pairs, genuine_rows = block_masks(segment_ids)
    (sorting_probabilities, entropy_local), sink_pull = jax.vjp(
        lambda logit_matrix: balancing_terms(logit_matrix, permitted_pairs, genuine_rows),
        sorting_logit_rows,
    )
    count_local = jnp.sum((segment_ids[:, ::BLOCK] > 0).astype(jnp.float32))
    block_count = lax.psum(count_local, "dp")
    entropy_total = lax.psum(entropy_local, ("dp", "mp"))
    penalty = entropy_total / (block_count * HEADS)
    probs_low = sorting_probabilities.astype(jnp.bfloat16)
    pair_blocks = jnp.concatenate(
        [
            key_blocks.reshape(groups, heads_here, BLOCKS, tile_size),
            value_blocks.reshape(groups, heads_here, BLOCKS, tile_size),
        ],
        axis=-1,
    )
    sorted_pair = jnp.einsum(
        "ghbc,ghcf->ghbf", probs_low, pair_blocks, preferred_element_type=jnp.float32
    ).astype(jnp.bfloat16)
    sorted_keys = sorted_pair[..., :tile_size].reshape(groups, heads_here, BLOCKS, BLOCK, HEAD_DIM)
    sorted_values = sorted_pair[..., tile_size:].reshape(
        groups, heads_here, BLOCKS, BLOCK, HEAD_DIM
    )
    all_keys = jnp.concatenate([key_blocks, sorted_keys], axis=3)
    all_values = jnp.concatenate([value_blocks, sorted_values], axis=3)
    key_mask = token_masks(segment_ids)

    def scored(query_part):
        raw_scores = jnp.einsum(
            "ghnie,ghnje->ghnij", query_part, all_keys, preferred_element_type=jnp.float32
        )
        return jnp.where(key_mask, raw_scores * score_scale, excluded_fill)

    scores = scored(query_blocks)
    row_max = jnp.max(scores, axis=-1, keepdims=True)
    shifted = jnp.exp(scores - row_max)
    row_total = jnp.sum(shifted, axis=-1, keepdims=True)
    attention = shifted / row_total
    log_total = row_max + jnp.log(row_total)
    mixed_blocks = jnp.einsum(
        "ghnij,ghnje->ghnie",
        attention.astype(jnp.bfloat16),
        all_values,
        preferred_element_type=jnp.float32,
    ).astype(jnp.bfloat16)
    mixed_rows = from_blocks(mixed_blocks)
    out_weights = mixer_low[:, 3, :]
    branch = sum_rows(lambda row_start, row_count: times_t(mixed_rows, out_weights))
    middle = inputs_f + branch
    normed_second, inverse_second, scaled_second = normalize(middle, gain_rows[1])
    second_in = scaled_second.astype(jnp.bfloat16)
    up_weights = feed_split[:, 0, :]
    down_weights = feed_split[:, 1, :]
    feed_rows = spread_rows(second_in)
    pre_act = jnp.dot(feed_rows, up_weights, preferred_element_type=jnp.float32)
    activated = jnp.maximum(pre_act, 0.0).astype(jnp.bfloat16)
    feed_out = sum_rows(lambda row_start, row_count: times_t(activated, down_weights))
    block_output = (middle + feed_out).astype(jnp.bfloat16)
    grad_feed = spread_rows(cotangent)
    down_grad = cross(grad_feed, activated)
    act_grad = jnp.dot(grad_feed, down_weights, preferred_element_type=jnp.float32)
    pre_grad = jnp.where(pre_act > 0, act_grad, 0.0).astype(jnp.bfloat16)
    up_grad = cross(feed_rows, pre_grad)
    second_grad = sum_rows(lambda row_start, row_count: times_t(pre_grad, up_weights))
    middle_back, gain_second_grad = norm_back(
        second_grad, normed_second, inverse_second, gain_rows[1]
    )
    middle_grad = cotangent.astype(jnp.float32) + middle_back
    branch_all = spread_rows(middle_grad.astype(jnp.bfloat16))
    out_grad = cross(branch_all, mixed_rows)
    mixed_grad = to_blocks(
        jnp.dot(branch_all, out_weights, preferred_element_type=jnp.float32).astype(jnp.bfloat16)
    )
    attention_again = jnp.exp(scored(query_blocks) - log_total)
    prob_grad = jnp.einsum(
        "ghnie,ghnje->ghnij", mixed_grad, all_values, preferred_element_type=jnp.float32
    )
    score_grad = attention_again * (
        prob_grad - jnp.sum(attention_again * prob_grad, axis=-1, keepdims=True)
    )
    raw_grad = jnp.where(key_mask, score_grad * score_scale, 0.0).astype(jnp.bfloat16)
    query_grad = jnp.einsum(
        "ghnij,ghnje->ghnie", raw_grad, all_keys, preferred_element_type=jnp.float32
    ).astype(jnp.bfloat16)
    key_grad_all = jnp.einsum(
        "ghnij,ghnie->ghnje", raw_grad, query_blocks, preferred_element_type=jnp.float32
    )
    value_grad_all = jnp.einsum(
        "ghnij,ghnie->ghnje",
        attention_again.astype(jnp.bfloat16),
        mixed_grad,
        preferred_element_type=jnp.float32,
    )
    sorted_grad = jnp.concatenate(
        [
            key_grad_all[:, :, :, BLOCK:].reshape(groups, heads_here, BLOCKS, tile_size),
            value_grad_all[:, :, :, BLOCK:].reshape(groups, heads_here, BLOCKS, tile_size),
        ],
        axis=-1,
    ).astype(jnp.bfloat16)
    pair_back = jnp.einsum(
        "ghbc,ghbf->ghcf", probs_low, sorted_grad, preferred_element_type=jnp.float32
    )
    probs_grad = jnp.einsum(
        "ghbf,ghcf->ghbc", sorted_grad, pair_blocks, preferred_element_type=jnp.float32
    )
    key_grad = (
        key_grad_all[:, :, :, :BLOCK]
        + pair_back[..., :tile_size].reshape(groups, heads_here, BLOCKS, BLOCK, HEAD_DIM)
    ).astype(jnp.bfloat16)
    value_grad = (
        value_grad_all[:, :, :, :BLOCK]
        + pair_back[..., tile_size:].reshape(groups, heads_here, BLOCKS, BLOCK, HEAD_DIM)
    ).astype(jnp.bfloat16)
    entropy_weight = penalty_weight * total_tokens / (block_count * HEADS)
    (logit_grad,) = sink_pull((probs_grad, entropy_weight))
    logit_rows = (
        logit_grad.transpose(0, 2, 1, 3)
        .reshape(groups * BLOCKS, heads_here * BLOCKS)
        .astype(jnp.bfloat16)
    )
    sorter_grad = cross(block_means, logit_rows)
    mean_grad = times_t(logit_rows, sorter_low) / BLOCK
    proj_grad = jnp.concatenate(
        [from_blocks(query_grad), from_blocks(key_grad), from_blocks(value_grad)], axis=1
    )

    def first_term(row_start, row_count):
        part_sum = times_t(proj_grad, proj_weights)
        spread = mean_grad
        spread = jnp.broadcast_to(spread[:, None, :], (row_count // BLOCK, BLOCK, WIDTH)).reshape(
            row_count, WIDTH
        )
        return part_sum + spread

    first_grad = sum_rows(first_term)
    input_back, gain_first_grad = norm_back(first_grad, normed_first, inverse_first, gain_rows[0])
    token_grad = middle_grad + input_back
    mixer_grad = jnp.concatenate(
        [cross(first_all, proj_grad).reshape(WIDTH, 3, width_here), out_grad[:, None, :]], axis=1
    )
    feed_grad = jnp.stack([up_grad, down_grad], axis=1)
    mixer_sum, feed_sum, sorter_sum = (
        lax.psum_scatter(
            mixer_grad.astype(jnp.bfloat16), "dp", scatter_dimension=0, tiled=True
        ).astype(jnp.float32),
        lax.psum_scatter(
            feed_grad.astype(jnp.bfloat16), "dp", scatter_dimension=0, tiled=True
        ).astype(jnp.float32),
        lax.psum_scatter(
            sorter_grad.astype(jnp.bfloat16), "dp", scatter_dimension=0, tiled=True
        ).astype(jnp.float32),
    )
    gain_sum = lax.psum_scatter(
        jnp.stack([gain_first_grad, gain_second_grad]),
        ("dp", "mp"),
        scatter_dimension=1,
        tiled=True,
    )
    step_value = step_count[0].astype(jnp.float32)
    mixer_new = adamw(mixer_weights, mixer_moment, mixer_second, mixer_sum, rate_mixer, step_value)
    feed_new = adamw(feed_weights, feed_moment, feed_second, feed_sum, rate_feed, step_value)
    sorter_new = adamw(
        sorter_weights, sorter_moment, sorter_second, sorter_sum, rate_sorter, step_value
    )
    gain_new = adamw(norm_gains, gain_moment, gain_second, gain_sum, rate_gains, step_value)
    return (
        block_output,
        token_grad,
        penalty.reshape(1),
        mixer_new[0],
        mixer_new[1],
        mixer_new[2],
        feed_new[0],
        feed_new[1],
        feed_new[2],
        sorter_new[0],
        sorter_new[1],
        sorter_new[2],
        gain_new[0],
        gain_new[1],
        gain_new[2],
    )


def solution(mesh):
    return jax.shard_map(
        local,
        mesh=mesh,
        in_specs=(
            P(("dp", "mp"), None),
            P("dp", None),
            P(("dp", "mp"), None),
            P(),
            P("dp", None, "mp"),
            P("dp", None, "mp"),
            P("dp", None, "mp"),
            P("dp", None, "mp"),
            P("dp", None, "mp"),
            P("dp", None, "mp"),
            P("dp", "mp"),
            P("dp", "mp"),
            P("dp", "mp"),
            P(None, ("dp", "mp")),
            P(None, ("dp", "mp")),
            P(None, ("dp", "mp")),
        ),
        out_specs=(
            P(("dp", "mp"), None),
            P(("dp", "mp"), None),
            P(),
            P("dp", None, "mp"),
            P("dp", None, "mp"),
            P("dp", None, "mp"),
            P("dp", None, "mp"),
            P("dp", None, "mp"),
            P("dp", None, "mp"),
            P("dp", "mp"),
            P("dp", "mp"),
            P("dp", "mp"),
            P(None, ("dp", "mp")),
            P(None, ("dp", "mp")),
            P(None, ("dp", "mp")),
        ),
        check_vma=False,
    )
```

profile of v0, /device:TPU:0, one launch (start us, length us, event | category | flops | bytes accessed | tf_op | source)
XLA Modules:
  0.0 1113.7 jit_solution(4015465283017380022)
XLA Ops:
  11.3 43.5 %all-gather = f32[32,16,2]{1,2,0:T(2,128)S(1)} all-gather(f32[1,16,2]{1,2,0:T(2,128)} %bitcast.270), channel_id=1, replica_groups=mesh['dp'=8,'mp'=4] {'dp','mp'}, dimensions={0}, use_global_device_ids=true | all-gather | bytes 4224 | tf_op jit(solution)/shard_map/all_gather | solution.py:138
  58.5 31.3 %all_gather.26 = bf16[512,4,128]{2,1,0:T(4,128)(2,1)S(1)} all-gather(bf16[64,4,128]{2,1,0:T(4,128)(2,1)S(1)} %convert_element_type.113), channel_id=1, replica_groups=mesh['dp'=8,'mp'=4] {'dp'}, dimensions={0}, use_global_device_ids=true | all-gather | bytes 589824 | tf_op jit(solution)/shard_map/all_gather | solution.py:134
  91.1 30.7 %all_gather.27 = bf16[512,64]{1,0:T(8,128)(2,1)S(1)} all-gather(bf16[64,64]{1,0:T(8,128)(2,1)S(1)} %convert_element_type.118), channel_id=1, replica_groups=mesh['dp'=8,'mp'=4] {'dp'}, dimensions={0}, use_global_device_ids=true | all-gather | bytes 73728 | tf_op jit(solution)/shard_map/all_gather | solution.py:136
  125.8 3.7 convert_reduce_fusion
  152.9 5.4 reshape.617
  158.2 3.3 copy.140
  161.6 4.2 reshape.618
  169.7 4.4 reshape.621
  174.1 3.1 reshape.622
  177.2 5.3 fusion.156
  182.6 6.3 fusion.4
  188.9 3.8 convert_bitcast_fusion.1
  192.7 3.3 copy.78
  197.0 5.6 fusion.111
  204.4 66.5 %reduce-scatter.10.cloned.1.call-done = f32[1024,512]{1,0:T(8,128)} async-done(((f32[4096,512]{1,0:T(8,128)}), f32[1024,512]{1,0:T(8,128)}) %reduce-scatter.10.cloned.1.call-update) | async-done | bytes 2097168 | tf_op jit(solution)/shard_map/reduce_scatter | solution.py:92
  276.6 33.6 %all-gather.9.cloned.1.call-done = bf16[4096,512]{1,0:T(8,128)(2,1)} async-done(((bf16[1024,512]{1,0:T(8,128)(2,1)}), bf16[4096,512]{1,0:T(8,128)(2,1)}) %all-gather.9.cloned.1.call-update) | async-done | bytes 4194320 | tf_op jit(solution)/shard_map/all_gather | solution.py:88
  310.2 7.9 fusion.57
  318.1 28.0 %all-gather.13.cloned.1.call-done = bf16[4096,512]{1,0:T(8,128)(2,1)} async-done(((bf16[1024,512]{1,0:T(8,128)(2,1)}), bf16[4096,512]{1,0:T(8,128)(2,1)}) %all-gather.13.cloned.1.call-update) | async-done | bytes 4194320 | tf_op jit(solution)/shard_map/all_gather | solution.py:88
  346.1 7.2 select_convert_fusion
  355.2 5.8 fusion.56
  361.1 10.0 fusion.51
  371.2 61.6 %reduce-scatter.14.cloned.1.call-done = f32[1024,512]{1,0:T(8,128)} async-done(((f32[4096,512]{1,0:T(8,128)}), f32[1024,512]{1,0:T(8,128)}) %reduce-scatter.14.cloned.1.call-update) | async-done | bytes 2097168 | tf_op jit(solution)/shard_map/reduce_scatter | solution.py:92
  436.5 70.6 %reduce-scatter.12.cloned.1.call-done = f32[1024,512]{1,0:T(8,128)} async-done(((f32[4096,512]{1,0:T(8,128)}), f32[1024,512]{1,0:T(8,128)}) %reduce-scatter.12.cloned.1.call-update) | async-done | bytes 2097168 | tf_op jit(solution)/shard_map/reduce_scatter | solution.py:92
  507.1 4.3 fusion.146
  511.5 22.4 %psum.14 = f32[]{:T(128)} all-reduce(f32[]{:T(128)} %get-tuple-element.86), channel_id=1, replica_groups=mesh['dp'=8,'mp'=4] {'dp'}, use_global_device_ids=true, to_apply=%region_46.47 | all-reduce | flops 1 | bytes 8 | tf_op jit(solution)/shard_map/psum | solution.py:180
  544.0 6.0 fusion.53
  550.0 5.8 fusion.54
  557.0 4.5 convolution_convert_fusion.2
  561.5 3.9 reshape.624
  565.4 6.5 fusion.8
  571.9 52.8 %convert_bitcast_fusion = bf16[4,32,32,2,64]{4,2,1,3,0:T(8,128)(2,1)} fusion(bf16[4,2,32,32,64]{4,3,2,1,0:T(8,128)(2,1)} %reshape.621, bf16[4,2,32,32,64]{4,3,2,1,0:T(8,128)(2,1)} %bitcast.247, f32[4,2,32,32,64]{4,3,2,1,0:T(8,128)} %fusion.8, f32[4,2,32,32,64]{4,3,2,1,0:T(8,128)} %copy-done.2, f32[4,2,32,32]{3,2,1,0:T(8,128)} %log_add_fusion, ...), kind=kOutput, calls=%fused_computation.56 | convolution fusion | flops 76030016 | bytes 7634944 | tf_op jit(solution)/shard_map/ghnij,ghnje->ghnie/dot_general | solution.py:256
  624.7 55.8 %fusion.31 = f32[4,2,32,64,64]{4,3,2,1,0:T(8,128)} fusion(f32[4,2,32,32,64]{4,3,2,1,0:T(8,128)} %fusion.8, f32[4,2,32,32,64]{4,3,2,1,0:T(8,128)} %copy-done.2, f32[4,2,32,32]{3,2,1,0:T(8,128)} %log_add_fusion, pred[4,32,32,64]{3,2,1,0:T(8,128)(4,1)} %pad_add_fusion, bf16[4,32,32,2,64]{4,3,2,1,0:T(2,128)(2,1)} %reshape.616), kind=kOutput, calls=%fused_computation.50 | convolution fusion | flops 71311424 | bytes 9732096 | tf_op jit(solution)/shard_map/ghnij,ghnie->ghnje/dot_general | solution.py:259
  680.5 7.5 fusion.25
  688.0 3.3 copy.82
  721.3 3.9 fusion.152
  725.3 5.2 reshape.630
  730.5 4.5 fusion.28
  735.1 4.6 copy.85
  739.6 4.8 reshape.631
  747.4 4.5 fusion.27
  752.0 3.3 copy.84
  762.7 5.2 convolution_convert_fusion.4
  771.4 7.5 bitcast_add_fusion
  785.7 36.8 %psum.15 = f32[]{:T(128)} all-reduce(f32[]{:T(128)S(6)} %neg.223), channel_id=1, replica_groups=mesh['dp'=8,'mp'=4] {'dp','mp'}, use_global_device_ids=true, to_apply=%region_67.68 | all-reduce | flops 1 | bytes 8 | tf_op jit(solution)/shard_map/psum | solution.py:181
  824.7 68.1 %all-reduce.3.cloned.1.call-done = bf16[512,4,128]{2,1,0:T(4,128)(2,1)} async-done(((bf16[512,4,128]{2,1,0:T(4,128)(2,1)}), bf16[512,4,128]{2,1,0:T(4,128)(2,1)}) %all-reduce.3.cloned.1.call-update) | async-done | bytes 524304
  894.7 71.4 %reduce-scatter.16.cloned.1.call-done = f32[1024,512]{1,0:T(8,128)} async-done(((f32[4096,512]{1,0:T(8,128)}), f32[1024,512]{1,0:T(8,128)}) %reduce-scatter.16.cloned.1.call-update) | async-done | bytes 2097168 | tf_op jit(solution)/shard_map/reduce_scatter | solution.py:92
  969.7 3.1 fusion.22
  972.8 130.9 %reduce-scatter.22.cloned.1.call-done = f32[16,2]{1,0:T(8,128)} async-done(((f32[512,2]{1,0:T(8,128)}), f32[16,2]{1,0:T(8,128)}) %reduce-scatter.22.cloned.1.call-update) | async-done | bytes 144
  (534 shorter events, 118.7 us)
Async XLA Ops:
  8.0 50.2 %copy-start.137 = (s32[4,1024]{1,0:T(4,128)S(1)}, s32[4,1024]{1,0:T(4,128)}, u32[]{:S(2)}) copy-start(s32[4,1024]{1,0:T(4,128)} %param.17) | copy-start | bytes 49156
  8.0 50.4 %copy-start.76 = (f32[64,64]{1,0:T(8,128)S(1)}, f32[64,64]{1,0:T(8,128)}, u32[]{:S(2)}) copy-start(f32[64,64]{1,0:T(8,128)} %param.26) | copy-start | bytes 49156
  8.0 50.4 %copy-start.43 = (f32[64,4,128]{2,1,0:T(4,128)S(1)}, f32[64,4,128]{2,1,0:T(4,128)}, u32[]{:S(2)}) copy-start(f32[64,4,128]{2,1,0:T(4,128)} %param.20) | copy-start | bytes 393220
  8.0 117.8 %all-gather.7.cloned.1.call-start = ((), (), s32[]{:S(2)}) async-start(), calls=%async_computation.7 | async-start | bytes 5242880 | tf_op jit(solution)/shard_map/all_gather | solution.py:88
  9.6 81.5 %copy-start.77 = (f32[1024]{0:T(1024)}, f32[1024]{0:T(1024)S(1)}, u32[]{:S(2)}) copy-start(f32[1024]{0:T(1024)S(1)} %broadcast_multiply_fusion.5) | copy-start | bytes 12292
  11.3 110.5 %copy-start.80 = (f32[1024]{0:T(1024)}, f32[1024]{0:T(1024)S(1)}, u32[]{:S(2)}) copy-start(f32[1024]{0:T(1024)S(1)} %add_rsqrt_fusion.1) | copy-start | bytes 12292
  58.1 212.7 %reduce-scatter.10.cloned.1.call-start = ((), (), s32[]{:S(2)}) async-start(), calls=%async_computation.8 | async-start | bytes 10485760 | tf_op jit(solution)/shard_map/reduce_scatter | solution.py:92
  91.1 50.5 %copy-start.21 = (bf16[512,3,128]{0,2,1:T(8,128)(2,1)}, bf16[512,3,128]{0,2,1:T(8,128)(2,1)S(1)}, u32[]{:S(2)}) copy-start(bf16[512,3,128]{0,2,1:T(8,128)(2,1)S(1)} %copy.101) | copy-start | bytes 1179652
  130.5 13.5 %copy-start.4 = (f32[4,32,2,32]{3,1,2,0:T(8,128)}, f32[4,32,2,32]{3,1,2,0:T(8,128)S(1)}, u32[]{:S(2)}) copy-start(f32[4,32,2,32]{3,1,2,0:T(8,128)S(1)} %copy.76) | copy-start | bytes 98308
  130.5 11.1 copy-start.16
  151.2 37.7 %copy-start.3 = (bf16[4,32,32,2,64]{4,2,1,3,0:T(8,128)(2,1)}, bf16[4,32,32,2,64]{4,2,1,3,0:T(8,128)(2,1)S(1)}, u32[]{:S(2)}) copy-start(bf16[4,32,32,2,64]{4,2,1,3,0:T(8,128)(2,1)S(1)} %copy.139) | copy-start | bytes 3145732
  182.5 10.2 copy-start.2
  182.5 10.2 copy-start.41
  202.6 68.2 %copy-start = (bf16[1024,512]{1,0:T(8,128)(2,1)S(1)}, bf16[1024,512]{1,0:T(8,128)(2,1)}, u32[]{:S(2)}) copy-start(bf16[1024,512]{1,0:T(8,128)(2,1)} %param.16) | copy-start | bytes 3145732
  202.7 73.9 %all-gather.11.cloned.1.call-start = ((), (), s32[]{:S(2)}) async-start(), calls=%async_computation.10 | async-start | bytes 1179648 | tf_op jit(solution)/shard_map/all_gather | solution.py:135
  204.3 105.9 %all-gather.9.cloned.1.call-start = ((), (), s32[]{:S(2)}) async-start(), calls=%async_computation.9 | async-start | bytes 5242880 | tf_op jit(solution)/shard_map/all_gather | solution.py:88
  275.8 70.3 %all-gather.13.cloned.1.call-start = ((), (), s32[]{:S(2)}) async-start(), calls=%async_computation.12 | async-start | bytes 5242880 | tf_op jit(solution)/shard_map/all_gather | solution.py:88
  276.4 156.4 %reduce-scatter.14.cloned.1.call-start = ((), (), s32[]{:S(2)}) async-start(), calls=%async_computation.13 | async-start | bytes 10485760 | tf_op jit(solution)/shard_map/reduce_scatter | solution.py:92
  346.1 9.2 copy-start.17
  361.1 146.0 %reduce-scatter.12.cloned.1.call-start = ((), (), s32[]{:S(2)}) async-start(), calls=%async_computation.11 | async-start | bytes 10485760 | tf_op jit(solution)/shard_map/reduce_scatter | solution.py:92
  371.2 185.8 %all-gather.15.cloned.1.call-start = ((), (), s32[]{:S(2)}) async-start(), calls=%async_computation.14 | async-start | bytes 5242880 | tf_op jit(solution)/shard_map/all_gather | solution.py:88
  511.4 269.7 %reduce-scatter.18.cloned.1.call-start = ((), (), s32[]{:S(2)}) async-start(), calls=%async_computation.16 | async-start | bytes 1179648 | tf_op jit(solution)/shard_map/reduce_scatter | solution.py:321
  556.9 266.3 %reduce-scatter.20.cloned.1.call-start = ((), (), s32[]{:S(2)}) async-start(), calls=%async_computation.17 | async-start | bytes 147456 | tf_op jit(solution)/shard_map/reduce_scatter | solution.py:324
  709.2 9.3 copy-start.108
  709.3 9.3 copy-start.92
  710.0 9.2 copy-start.106
  710.1 9.2 copy-start.5
  710.1 9.2 copy-start.59
  710.1 9.2 copy-start.65
  710.1 9.2 copy-start.88
  710.1 9.4 copy-start.125
  710.1 9.4 copy-start.84
  710.1 9.7 copy-start.100
  710.1 9.7 copy-start.138
  710.1 9.7 copy-start.139
  710.1 9.7 copy-start.140
  760.4 132.4 %all-reduce.3.cloned.1.call-start = ((), (), s32[]{:S(2)}) async-start(), calls=%async_computation.19 | async-start | bytes 1048576
  771.1 195.0 %reduce-scatter.16.cloned.1.call-start = ((), (), s32[]{:S(2)}) async-start(), calls=%async_computation.15 | async-start | bytes 10485760 | tf_op jit(solution)/shard_map/reduce_scatter | solution.py:92
  779.0 113.8 %copy-start.44 = (f32[64,4,128]{2,1,0:T(4,128)S(1)}, f32[64,4,128]{2,1,0:T(4,128)}, u32[]{:S(2)}) copy-start(f32[64,4,128]{2,1,0:T(4,128)} %param.20) | copy-start | bytes 393220
  779.0 187.1 %copy-start.78 = (f32[1024]{0:T(1024)S(1)}, f32[1024]{0:T(1024)}, u32[]{:S(2)}) copy-start(f32[1024]{0:T(1024)} %copy-done.77) | copy-start | bytes 12292
  779.0 187.1 %copy-start.81 = (f32[1024]{0:T(1024)S(1)}, f32[1024]{0:T(1024)}, u32[]{:S(2)}) copy-start(f32[1024]{0:T(1024)} %copy-done.80) | copy-start | bytes 12292
  779.0 187.1 %copy-start.136 = (f32[1,512]{1,0:T(1,128)S(1)}, f32[1,512]{1,0:T(1,128)}, u32[]{:S(2)}) copy-start(f32[1,512]{1,0:T(1,128)} %copy-done.135) | copy-start | bytes 6148
  779.0 324.6 %reduce-scatter.22.cloned.1.call-start = ((), (), s32[]{:S(2)}) async-start(), calls=%async_computation.18 | async-start | bytes 270336
  782.3 186.4 %copy-start.155 = (f32[512]{0:T(512)S(1)}, f32[512]{0:T(512)}, u32[]{:S(2)}) copy-start(f32[512]{0:T(512)} %get-tuple-element.60) | copy-start | bytes 6148
  782.3 187.3 %copy-start.10 = (f32[1024,512]{1,0:T(8,128)S(1)}, f32[1024,512]{1,0:T(8,128)}, u32[]{:S(2)}) copy-start(f32[1024,512]{1,0:T(8,128)} %get-tuple-element.89) | copy-start | bytes 6291460
  969.6 134.8 %copy-start.156 = (f32[2,16]{1,0:T(2,128)S(1)}, f32[2,16]{1,0:T(2,128)}, u32[]{:S(2)}) copy-start(f32[2,16]{1,0:T(2,128)} %param.29) | copy-start | bytes 388
  969.7 134.8 %copy-start.157 = (f32[2,16]{1,0:T(2,128)S(1)}, f32[2,16]{1,0:T(2,128)}, u32[]{:S(2)}) copy-start(f32[2,16]{1,0:T(2,128)} %param.31) | copy-start | bytes 388
  969.7 134.8 %copy-start.158 = (f32[2,16]{1,0:T(2,128)S(1)}, f32[2,16]{1,0:T(2,128)}, u32[]{:S(2)}) copy-start(f32[2,16]{1,0:T(2,128)} %param.30) | copy-start | bytes 388
  (125 other events, 449.1 us)
Sparse Core Ops, SparseCore 0:
  58.3 30.5 all-gather.6
  202.8 68.0 reduce-scatter.9
  511.6 34.4 all-gather.14
  969.8 133.8 reduce-scatter.21
Sparse Core Ops, SparseCore 1:
  205.9 36.7 all-gather.10
  275.9 34.3 all-gather.8
  311.7 34.3 all-gather.12
  361.1 71.6 reduce-scatter.13
  435.4 71.6 reduce-scatter.11
  557.0 60.0 reduce-scatter.17
  760.5 57.3 reduce-scatter.19
  821.7 71.1 all-reduce.2
  895.4 70.6 reduce-scatter.15
where the time goes:
time: 1120 us; the launch traced here: 1110 us
  waiting for transfers between devices  531 us (47%)
  matrix products  206 us (18%)
  blocking collectives  165 us (15%)
  local copies, waits for them, and re-layouts  109 us (10%)
  other arithmetic  78.5 us (7%)
  between operations  23.3 us (2%)
    reduce_scatter x4, waiting for transfers between devices, scatter_rows(): lax.psum_scatter(term_fn(jnp.int32(0), local_rows * lax.axis_size('mp')),...  270 us
    unnamed x15, waiting for transfers between devices  200 us
    all_gather x4, waiting for transfers between devices, gather_rows(): return lax.all_gather(block_rows, 'mp', axis=0, tiled=True)  61.6 us
    dot_general x1, matrix products, local(): jnp.einsum('ghnij,ghnie->ghnje', raw_grad, query_blocks, preferred_elemen...  55.8 us
    dot_general x1, matrix products, local(): jnp.einsum('ghnij,ghnje->ghnie', raw_grad, all_keys, preferred_element_ty...  52.8 us
    all_gather x1, blocking collectives, local(): gain_rows = lax.all_gather(norm_gains, ('dp', 'mp'), axis=1, tiled=True)  43.5 us
    psum x1, blocking collectives, local(): entropy_total = lax.psum(entropy_local, ('dp', 'mp'))  36.8 us
    all_gather x1, blocking collectives, local(): lax.all_gather(mixer_weights.astype(jnp.bfloat16), 'dp', axis=0, tiled=True)  31.3 us
  transfers between devices with their start and end apart: 13, of which 8 were waited for; matrix products, arithmetic and copies ran while one was open for 26% of the time, Pallas kernels for 0%

commit v1 on v0

v1 whole, which is shorter than its diff:
```python
import functools
import jax
import jax.numpy as jnp
from jax import lax
from jax.sharding import PartitionSpec as P
from jax.experimental import pallas as pl
from jax.experimental.pallas import tpu as pltpu

WIDTH = 512
HEADS = 8
HEAD_DIM = 64
HIDDEN = 2048
BLOCK = 32
SINK_ITERS = 8
SEQ_LEN = 1024
BLOCKS = 32
LOGITS = HEADS * BLOCKS
ROWS = 256
TILES = SEQ_LEN // ROWS
PACK = 4
GROUPS = HEADS // PACK
LANES = PACK * HEAD_DIM
PAIRS = PACK * BLOCK

norm_eps = 1e-05
softness_factor = 0.75
excluded_fill = -1000000000.0
penalty_weight = 0.1
bf16 = jnp.bfloat16
f32 = jnp.float32


def mm(a, b, ca=1, cb=0):
    return lax.dot_general(a, b, (((ca,), (cb,)), ((), ())), preferred_element_type=f32)


def iota(shape, dim):
    return lax.broadcasted_iota(jnp.int32, shape, dim)


def normalize(rows):
    centred = rows - jnp.mean(rows, axis=-1, keepdims=True)
    inverse = lax.rsqrt(jnp.mean(centred * centred, axis=-1, keepdims=True) + norm_eps)
    return centred * inverse, inverse


def norm_back(grad_out, normed, inverse, gain):
    scaled = grad_out * gain
    return inverse * (
        scaled
        - jnp.mean(scaled, axis=-1, keepdims=True)
        - normed * jnp.mean(scaled * normed, axis=-1, keepdims=True)
    )


def three_parts(value):
    high = value.astype(bf16)
    rest = value - high.astype(f32)
    mid = rest.astype(bf16)
    low = (rest - mid.astype(f32)).astype(bf16)
    return high, mid, low


def group_matrix():
    return (iota((LOGITS, LOGITS), 0) // BLOCKS == iota((LOGITS, LOGITS), 1) // BLOCKS).astype(bf16)


def exact_dot(value, matrix):
    rows = value.shape[0]
    out = mm(jnp.concatenate(three_parts(value), axis=0), matrix)
    return out[:rows] + out[rows : 2 * rows] + out[2 * rows :]


def head_max(value):
    lane_head = iota(value.shape, 1) // BLOCKS
    out = jnp.zeros_like(value)
    for head in range(HEADS):
        here = lane_head == head
        top = jnp.max(jnp.where(here, value, -jnp.inf), axis=1, keepdims=True)
        out = jnp.where(here, top, out)
    return out


def permitted(real_col, real_row):
    col = iota((BLOCKS, LOGITS), 1) % BLOCKS
    return ((real_col * real_row) > 0) | (iota((BLOCKS, LOGITS), 0) == col)


def sinkhorn(logits, allowed, groups, store):
    logs = jnp.where(allowed, logits / softness_factor, excluded_fill)
    top = head_max(logs)
    logs = logs - (top + jnp.log(exact_dot(jnp.exp(logs - top), groups)))
    store(0, jnp.exp(logs))
    top = jnp.max(logs, axis=0, keepdims=True)
    logs = logs - (top + jnp.log(jnp.sum(jnp.exp(logs - top), axis=0, keepdims=True)))
    weights = jnp.exp(logs)
    store(1, weights)
    for sweep in range(1, SINK_ITERS):
        logs = logs - jnp.log(exact_dot(weights, groups))
        weights = jnp.exp(logs)
        store(2 * sweep, weights)
        logs = logs - jnp.log(jnp.sum(weights, axis=0, keepdims=True))
        weights = jnp.exp(logs)
        store(2 * sweep + 1, weights)
    return logs, weights


def sinkhorn_back(grad, groups, load):
    for sweep in reversed(range(SINK_ITERS)):
        grad = grad - load(2 * sweep + 1) * jnp.sum(grad, axis=0, keepdims=True)
        grad = grad - load(2 * sweep) * exact_dot(grad, groups)
    return grad


def by_head(tile):
    rows = jnp.concatenate([tile] * HEADS, axis=0)
    keep = iota((LOGITS, WIDTH), 0) // BLOCKS == iota((LOGITS, WIDTH), 1) // HEAD_DIM
    return jnp.where(keep, rows, jnp.zeros_like(rows))


def by_pack(tile):
    rows = jnp.concatenate([tile] * PACK, axis=0)
    keep = iota((PAIRS, LANES), 0) // BLOCK == iota((PAIRS, LANES), 1) // HEAD_DIM
    return jnp.where(keep, rows, jnp.zeros_like(rows))


def own_heads(product):
    lane_head = iota((BLOCK, LANES), 1) // HEAD_DIM
    out = product[:BLOCK]
    for head in range(1, PACK):
        out = jnp.where(lane_head == head, product[head * BLOCK : (head + 1) * BLOCK], out)
    return out


CHUNK = 128
CHUNKS = WIDTH // CHUNK


def take(ref, rows, low=0, count=CHUNKS):
    return jnp.concatenate([ref[part, rows, :] for part in range(low, low + count)], axis=1)


def put(ref, rows, value, low=0):
    for part in range(value.shape[1] // CHUNK):
        ref[low + part, rows, :] = value[:, part * CHUNK : (part + 1) * CHUNK]


MESH = pl.DeviceIdType.MESH


class Layout:
    def __init__(self, mesh_dp, mesh_mp):
        self.dp, self.mp = mesh_dp, mesh_mp
        self.C = 2 if mesh_mp % 2 == 0 else 1
        self.X = mesh_mp // self.C
        self.L = 2 if mesh_dp % 2 == 0 else 1
        self.H = mesh_dp // self.L

    def here(self):
        dp, mp = lax.axis_index("dp"), lax.axis_index("mp")
        return dp // self.L, dp % self.L, mp // self.C, mp % self.C


class Item:
    def __init__(self, lay, J, r, c):
        self.lay, self.J, self.r, self.c = lay, J, r, c
        self.direct = c % 128 == 0
        self.half = r // 2

    def shard(self):
        return (self.J, self.r, self.c)

    def dims(self, *lead, rows=None, wide=None):
        rows = self.r if rows is None else rows
        wide = self.lay.mp if wide is None else wide
        if self.direct:
            return (self.J, *lead, rows, wide * self.c)
        return (self.J, *lead, wide, rows, self.c)

    def full(self):
        return self.dims(self.lay.H, self.lay.L)

    def at(self, lead, m, rows=slice(None)):
        if self.direct:
            cols = slice(None) if m is None else pl.ds(pl.multiple_of(m * self.c, 128), self.c)
            return (slice(None), *lead, rows, cols)
        return (slice(None), *lead, slice(None) if m is None else m, rows, slice(None))

    def rows_a(self):
        return slice(0, self.half)

    def rows_b(self):
        return slice(self.half, self.r)


ALLR = slice(None)


class Sems:
    def __init__(self, send, recv):
        self.send, self.recv, self.used = send, recv, 0

    def copy(self, src, dst, device):
        index = self.used
        self.used += 1
        return pltpu.make_async_remote_copy(
            src_ref=src,
            dst_ref=dst,
            send_sem=self.send.at[index],
            recv_sem=self.recv.at[index],
            device_id=device,
            device_id_type=MESH,
        )


def begin(copies):
    for copy in copies:
        copy.start()
    return copies


def arrive(copies):
    for copy in copies:
        copy.wait_recv()


class Gather:
    def __init__(self, item, shard, full, sems):
        self.item, self.shard, self.full, self.sems = item, shard, full, sems
        self.sent = []

    def stage(self, number):
        item, lay, full = self.item, self.item.lay, self.full
        h, l, x, c = lay.here()
        mp = x * lay.C + c
        copies = []

        def to(hh, ll, xx, cc):
            return (hh * lay.L + ll, xx * lay.C + cc)

        def same(index, device):
            copies.append(self.sems.copy(full.at[index], full.at[index], device))

        if number == 0:
            for k in range(1, lay.H):
                copies.append(
                    self.sems.copy(self.shard, full.at[item.at((h, l), mp)], to((h + k) % lay.H, l, x, c))
                )
        if number == 1:
            for k in range(1, lay.L):
                same(item.at((ALLR, l), mp, item.rows_a()), to(h, (l + k) % lay.L, x, c))
            for k in range(1, lay.X):
                same(item.at((ALLR, l), mp, item.rows_b()), to(h, l, (x + k) % lay.X, c))
        if number == 2:
            for k in range(1, lay.X):
                same(item.at((ALLR, ALLR), mp, item.rows_a()), to(h, l, (x + k) % lay.X, c))
            for k in range(1, lay.L):
                for part in range(lay.X):
                    same(item.at((ALLR, l), part * lay.C + c, item.rows_b()), to(h, (l + k) % lay.L, x, c))
        if number == 3:
            for k in range(1, lay.C):
                for part in range(lay.X):
                    same(item.at((ALLR, ALLR), part * lay.C + c), to(h, l, x, (c + k) % lay.C))
        self.sent += begin(copies)
        self.flying = copies

    def place(self):
        h, l, x, c = self.item.lay.here()
        self.full[self.item.at((h, l), x * self.item.lay.C + c)] = self.shard[...]

    def landed(self):
        arrive(self.flying)

    def close(self):
        for copy in self.sent:
            copy.wait_send()

    @staticmethod
    def count(lay):
        return (lay.H - 1) + (lay.L - 1) + (lay.X - 1) * 2 + (lay.L - 1) * lay.X + (lay.C - 1) * lay.X


class Scatter:
    def __init__(self, item, full, buffers, out, sems):
        self.item, self.full, self.out, self.sems = item, full, out, sems
        self.core, self.one_a, self.one_b, self.two_a, self.two_b, self.top_a, self.top_b = buffers
        self.sent = []

    @staticmethod
    def buffers(item):
        lay = item.lay
        half = item.half
        return [
            pltpu.VMEM((lay.C - 1, *item.dims(lay.H, lay.L, wide=lay.X)), bf16),
            pltpu.VMEM((lay.X - 1, *item.dims(lay.H, lay.L, rows=half, wide=1)), bf16),
            pltpu.VMEM((lay.L - 1, *item.dims(lay.H, rows=half, wide=lay.X)), bf16),
            pltpu.VMEM((lay.L - 1, *item.dims(lay.H, rows=half, wide=1)), bf16),
            pltpu.VMEM((lay.X - 1, *item.dims(lay.H, rows=half, wide=1)), bf16),
            pltpu.VMEM((lay.H - 1, *item.dims(rows=half, wide=1)), bf16),
            pltpu.VMEM((lay.H - 1, *item.dims(rows=half, wide=1)), bf16),
        ]

    def stage(self, number):
        item, lay = self.item, self.item.lay
        h, l, x, c = lay.here()
        copies = []

        def to(hh, ll, xx, cc):
            return (hh * lay.L + ll, xx * lay.C + cc)

        def send(src, src_index, dst, dst_index, device):
            copies.append(self.sems.copy(src.at[src_index], dst.at[dst_index], device))

        if number == 0:
            for k in range(1, lay.C):
                cc = (c + k) % lay.C
                for part in range(lay.X):
                    send(
                        self.full, item.at((ALLR, ALLR), part * lay.C + cc),
                        self.core, (k - 1, *item.at((ALLR, ALLR), part)),
                        to(h, l, x, cc),
                    )
        if number == 1:
            for k in range(1, lay.X):
                xx = (x + k) % lay.X
                send(
                    self.core, (0, *item.at((ALLR, ALLR), xx, item.rows_a())),
                    self.one_a, (k - 1, *item.at((ALLR, ALLR), 0)),
                    to(h, l, xx, c),
                )
            for k in range(1, lay.L):
                ll = (l + k) % lay.L
                send(
                    self.core, (0, *item.at((ALLR, ll), None, item.rows_b())),
                    self.one_b, (k - 1, *item.at((ALLR,), None)),
                    to(h, ll, x, c),
                )
        if number == 2:
            for k in range(1, lay.L):
                ll = (l + k) % lay.L
                send(
                    self.one_a, (0, *item.at((ALLR, ll), 0)),
                    self.two_a, (k - 1, *item.at((ALLR,), 0)),
                    to(h, ll, x, c),
                )
            for k in range(1, lay.X):
                xx = (x + k) % lay.X
                send(
                    self.one_b, (0, *item.at((ALLR,), xx)),
                    self.two_b, (k - 1, *item.at((ALLR,), 0)),
                    to(h, l, xx, c),
                )
        if number == 3:
            for k in range(1, lay.H):
                hh = (h + k) % lay.H
                for src, dst in ((self.two_a, self.top_a), (self.two_b, self.top_b)):
                    send(src, (0, *item.at((hh,), 0)), dst, (k - 1, *item.at((), 0)), to(hh, l, x, c))
        self.sent += begin(copies)
        self.flying = copies

    def fold(self, number):
        item, lay = self.item, self.item.lay
        h, l, x, c = lay.here()
        arrive(self.flying)

        def over_high(body):
            def step(high, carry):
                body(high)
                return carry

            lax.fori_loop(0, lay.H, step, 0)

        def add(target, index, source, source_index, extra):
            total = source[source_index].astype(f32) + target[(0, *index)].astype(f32)
            for other in range(1, extra):
                total = total + target[(other, *index)].astype(f32)
            target[(0, *index)] = total.astype(bf16)

        if number == 0:

            def core(high):
                for low in range(lay.L):
                    for part in range(lay.X):
                        add(
                            self.core, item.at((high, low), part),
                            self.full, item.at((high, low), part * lay.C + c), lay.C - 1,
                        )

            over_high(core)
        if number == 1:

            def one(high):
                for low in range(lay.L):
                    add(
                        self.one_a, item.at((high, low), 0),
                        self.core, (0, *item.at((high, low), x, item.rows_a())), lay.X - 1,
                    )
                add(
                    self.one_b, item.at((high,), None),
                    self.core, (0, *item.at((high, l), None, item.rows_b())), lay.L - 1,
                )

            over_high(one)
        if number == 2:

            def two(high):
                add(self.two_a, item.at((high,), 0), self.one_a, (0, *item.at((high, l), 0)), lay.L - 1)
                add(self.two_b, item.at((high,), 0), self.one_b, (0, *item.at((high,), x)), lay.X - 1)

            over_high(two)
        if number == 3:
            for rows, mine, others in (
                (item.rows_a(), self.two_a, self.top_a), (item.rows_b(), self.two_b, self.top_b),
            ):
                total = mine[(0, *item.at((h,), 0))].astype(f32)
                for other in range(lay.H - 1):
                    total = total + others[(other, *item.at((), 0))].astype(f32)
                self.out[:, rows, :] = total

    def close(self):
        for copy in self.sent:
            copy.wait_send()

    @staticmethod
    def count(lay):
        return (lay.C - 1) * lay.X + (lay.X - 1) * 2 + (lay.L - 1) * 2 + (lay.H - 1) * 2


class Total:
    def __init__(self, lay, near, far, sems):
        self.lay, self.near, self.far, self.sems = lay, near, far, sems
        self.sent = []

    def over_mp(self, value):
        dp, mp = lax.axis_index("dp"), lax.axis_index("mp")
        self.near[mp] = value
        self.flying = begin([
            self.sems.copy(self.near.at[mp], self.near.at[mp], (dp, (mp + k) % self.lay.mp))
            for k in range(1, self.lay.mp)
        ])
        self.sent += self.flying

    def over_dp(self):
        dp, mp = lax.axis_index("dp"), lax.axis_index("mp")
        arrive(self.flying)
        total = self.near[0]
        for other in range(1, self.lay.mp):
            total = total + self.near[other]
        self.far[dp] = total
        self.flying = begin([
            self.sems.copy(self.far.at[dp], self.far.at[dp], ((dp + k) % self.lay.dp, mp))
            for k in range(1, self.lay.dp)
        ])
        self.sent += self.flying

    def result(self):
        arrive(self.flying)
        total = self.far[0]
        for other in range(1, self.lay.dp):
            total = total + self.far[other]
        return total

    def close(self):
        for copy in self.sent:
            copy.wait_send()

    @staticmethod
    def count(lay):
        return lay.mp - 1 + lay.dp - 1


def meet(lay):
    barrier = pltpu.get_barrier_semaphore()
    dp, mp = lax.axis_index("dp"), lax.axis_index("mp")
    for k in range(1, lay.mp):
        pl.semaphore_signal(barrier, inc=1, device_id=(dp, (mp + k) % lay.mp), device_id_type=MESH)
    for k in range(1, lay.dp):
        pl.semaphore_signal(barrier, inc=1, device_id=((dp + k) % lay.dp, mp), device_id_type=MESH)
    pl.semaphore_wait(barrier, lay.mp + lay.dp - 2)


def spread_rows(row):
    return jnp.concatenate([row[:, at : at + 128] for at in range(0, row.shape[1], 128)], axis=0)


def joined_row(rows):
    return jnp.concatenate([rows[at : at + 1] for at in range(rows.shape[0])], axis=1)


def diagonal_column(row, count):
    same = iota((count, count), 0) == iota((count, count), 1)
    return jnp.sum(jnp.where(same, jnp.broadcast_to(row, (count, count)), 0.0), axis=1, keepdims=True)


def step_kernel(
    lay, items, total_tokens,
    x_ref, cot_ref, seg_ref, small_ref, qkv_in, sorter_in, wo_in, feed_in,
    out_ref, grad_ref, qkv_out, sorter_out, wo_out, feed_out, small_out,
    *scratch,
):
    qkv_item, sorter_item, wo_item, feed_item = items
    scratch = list(scratch)
    (
        qkv_ref, sorter_blocks, wo_ref, feed_ref, dqkv_ref, dsorter_blocks, dwo_ref, dfeed_ref,
        sorter_ref, first_ref, q_ref, k_ref, v_ref, sk_ref, sv_ref, att_ref, mixed_ref, means_ref, sink_ref, logs_ref,
        segrow_ref, spread_ref, gain_grad_ref,
        near_a, far_a, near_b, far_b, send_sems, recv_sems,
    ) = scratch[:29]
    rest = scratch[29:]
    sems = Sems(send_sems, recv_sems)
    meet(lay)
    gather_qkv = Gather(qkv_item, qkv_in, qkv_ref, sems)
    gather_sorter = Gather(sorter_item, sorter_in, sorter_blocks, sems)
    gather_wo = Gather(wo_item, wo_in, wo_ref, sems)
    gather_feed = Gather(feed_item, feed_in, feed_ref, sems)
    early, late = (gather_qkv, gather_sorter), (gather_wo, gather_feed)
    scatters = []
    for item, full, out in (
        (qkv_item, dqkv_ref, qkv_out), (sorter_item, dsorter_blocks, sorter_out),
        (wo_item, dwo_ref, wo_out), (feed_item, dfeed_ref, feed_out),
    ):
        scatters.append(Scatter(item, full, rest[:7], out, sems))
        rest = rest[7:]
    scatter_qkv, scatter_sorter, scatter_wo, scatter_feed = scatters
    total_a = Total(lay, near_a, far_a, sems)
    total_b = Total(lay, near_b, far_b, sems)

    def each(group, name, *args):
        for member in group:
            getattr(member, name)(*args)

    seg = seg_ref[...].astype(f32)
    real_col = (seg[:, 0:1] > 0).astype(f32)
    lane_block = iota((BLOCKS, LOGITS), 1) % BLOCKS
    real_row = jnp.sum(jnp.where(iota((BLOCKS, LOGITS), 0) == lane_block, real_col, 0.0), axis=0, keepdims=True)
    count = jnp.broadcast_to(jnp.sum(real_col, axis=0, keepdims=True), (8, 128))
    total_a.over_mp(jnp.concatenate([small_ref[...], count], axis=0))
    each(early, "stage", 0)
    each(early + late, "place")
    segrow_ref[...] = jnp.concatenate([seg] * PACK, axis=1)
    total_a.over_dp()
    each(early, "landed")
    each(early, "stage", 1)
    each(late, "stage", 0)
    summed = total_a.result()
    gain_first = joined_row(summed[0:4])
    gain_second = joined_row(summed[4:8])
    entropy_weight = penalty_weight * total_tokens / (summed[8:9, 0:1] * HEADS)
    each(early, "landed")
    each(early, "stage", 2)
    each(early, "landed")
    each(early, "stage", 3)

    def norm_first(tile, carry):
        rows = pl.ds(pl.multiple_of(tile * ROWS, ROWS), ROWS)
        normed, _ = normalize(x_ref[rows, :].astype(f32))
        first_ref[rows, :] = (normed * gain_first).astype(bf16)
        return carry

    lax.fori_loop(0, TILES, norm_first, 0)
    member = (iota((BLOCKS, SEQ_LEN), 0) == iota((BLOCKS, SEQ_LEN), 1) // BLOCK).astype(bf16)
    means = (mm(member, first_ref[...]) / BLOCK).astype(bf16)
    means_ref[...] = means
    each(early, "landed")
    each(late, "landed")
    each(late, "stage", 1)

    def weight(ref, j, cols=slice(None)):
        if len(ref.shape) == 6:
            parts = [ref[j, :, :, part].reshape(WIDTH, ref.shape[-1]) for part in range(lay.mp)]
            return jnp.concatenate(parts, axis=1)
        tile = ref[j, :, :, :, cols]
        return tile.reshape(WIDTH, tile.shape[-1])

    def project(tile, carry):
        rows = pl.ds(pl.multiple_of(tile * ROWS, ROWS), ROWS)
        first = first_ref[rows, :]
        q_ref[rows, :] = mm(first, weight(qkv_ref, 0)).astype(bf16)
        put(k_ref, rows, mm(first, weight(qkv_ref, 1)).astype(bf16).astype(f32))
        put(v_ref, rows, mm(first, weight(qkv_ref, 2)).astype(bf16).astype(f32))
        return carry

    lax.fori_loop(0, TILES, project, 0)
    r, c = sorter_item.r, sorter_item.c
    for high in range(lay.H):
        for low in range(lay.L):
            for part in range(lay.mp):
                rows = slice((high * lay.L + low) * r, (high * lay.L + low + 1) * r)
                sorter_ref[rows, part * c : (part + 1) * c] = sorter_blocks[0, high, low, part]
    logits = mm(means, sorter_ref[...])
    allowed = permitted(real_col, real_row)
    each(late, "landed")
    each(late, "stage", 2)

    def store(index, value):
        sink_ref[index] = value

    logs, weights = sinkhorn(logits, allowed, group_matrix(), store)
    logs_ref[...] = logs
    probs = weights.astype(bf16)

    def sort(i, carry):
        rows = pl.ds(i, BLOCKS, stride=BLOCK)
        put(sk_ref, rows, mm(probs, by_head(take(k_ref, rows).astype(bf16))))
        put(sv_ref, rows, mm(probs, by_head(take(v_ref, rows).astype(bf16))))
        return carry

    lax.fori_loop(0, BLOCK, sort, 0)
    each(late, "landed")
    each(late, "stage", 3)

    def attend(block, carry):
        rows = pl.ds(pl.multiple_of(block * BLOCK, BLOCK), BLOCK)
        row = segrow_ref[pl.ds(block, 1), :]
        near = diagonal_column(row[:, :BLOCK], BLOCK) == row
        far = jnp.broadcast_to(row > 0, (BLOCK, PAIRS))
        mask = jnp.concatenate([near, far], axis=0)
        for group in range(GROUPS):
            lanes = slice(group * LANES, (group + 1) * LANES)
            low, count = group * LANES // CHUNK, LANES // CHUNK
            keys = jnp.concatenate([take(k_ref, rows, low, count), take(sk_ref, rows, low, count)], axis=0).astype(bf16)
            values = jnp.concatenate([take(v_ref, rows, low, count), take(sv_ref, rows, low, count)], axis=0).astype(bf16)
            queries = by_pack(q_ref[rows, lanes])
            scores = jnp.where(mask, mm(keys, queries, 1, 1) * (HEAD_DIM ** -0.5), excluded_fill)
            shifted = jnp.exp(scores - jnp.max(scores, axis=0, keepdims=True))
            attention = shifted * (1.0 / jnp.sum(shifted, axis=0, keepdims=True))
            att_ref[block, group] = attention
            mixed_ref[rows, lanes] = own_heads(mm(attention.astype(bf16), values, 0, 0)).astype(bf16)
        return carry

    lax.fori_loop(0, BLOCKS, attend, 0)
    each(late, "landed")
    gain_grad_ref[...] = jnp.zeros_like(gain_grad_ref)

    def keep(ref, j, cols, value):
        if len(ref.shape) == 6:
            for part in range(lay.mp):
                piece = value[:, part * ref.shape[-1] : (part + 1) * ref.shape[-1]]
                ref[j, :, :, part] = piece.astype(bf16).reshape(lay.H, lay.L, WIDTH // lay.dp, ref.shape[-1])
            return
        ref[j, :, :, :, cols] = value.astype(bf16).reshape(lay.H, lay.L, WIDTH // lay.dp, value.shape[1])

    def feed_phase(second_ref, act_ref, pre_ref):
        def feed(tile, carry):
            rows = pl.ds(pl.multiple_of(tile * ROWS, ROWS), ROWS)
            middle = x_ref[rows, :].astype(f32) + mm(mixed_ref[rows, :], weight(wo_ref, 0), 1, 1)
            normed, inverse = normalize(middle)
            second = (normed * gain_second).astype(bf16)
            second_ref[rows, :] = second
            cot = cot_ref[rows, :]
            total = middle
            second_grad = jnp.zeros((ROWS, WIDTH), f32)
            for part in range(HIDDEN // WIDTH):
                cols = slice(part * WIDTH, (part + 1) * WIDTH)
                up, down = weight(feed_ref, 0, cols), weight(feed_ref, 1, cols)
                pre = mm(second, up)
                act = jnp.maximum(pre, 0.0).astype(bf16)
                act_ref[rows, cols] = act
                total = total + mm(act, down, 1, 1)
                pre_grad = jnp.where(pre > 0, mm(cot, down), 0.0).astype(bf16)
                pre_ref[rows, cols] = pre_grad
                second_grad = second_grad + mm(pre_grad, up, 1, 1)
            out_ref[rows, :] = total.astype(bf16)
            grad_ref[rows, :] = cot.astype(f32) + norm_back(second_grad, normed, inverse, gain_second)
            gain_grad_ref[8:16, :] += jnp.sum((second_grad * normed).reshape(ROWS // 8, 8, WIDTH), axis=0)
            return carry

        lax.fori_loop(0, TILES, feed, 0)

        def feed_weights(part, carry):
            cols = pl.ds(pl.multiple_of(part * WIDTH, WIDTH), WIDTH)
            keep(dfeed_ref, 0, cols, mm(second_ref[...], pre_ref[:, cols], 0, 0))
            keep(dfeed_ref, 1, cols, mm(cot_ref[...], act_ref[:, cols], 0, 0))
            return carry

        lax.fori_loop(0, HIDDEN // WIDTH, feed_weights, 0)

    pl.run_scoped(
        feed_phase,
        pltpu.VMEM((SEQ_LEN, WIDTH), bf16),
        pltpu.VMEM((SEQ_LEN, HIDDEN), bf16),
        pltpu.VMEM((SEQ_LEN, HIDDEN), bf16),
    )
    scatter_feed.stage(0)
    keep(dwo_ref, 0, slice(None), mm(grad_ref[...].astype(bf16), mixed_ref[...], 0, 0))
    scatter_wo.stage(0)
    first_set = (scatter_feed, scatter_wo)

    def start(tile, carry):
        rows = pl.ds(pl.multiple_of(tile * ROWS, ROWS), ROWS)
        mixed_ref[rows, :] = mm(grad_ref[rows, :].astype(bf16), weight(wo_ref, 0)).astype(bf16)
        return carry

    lax.fori_loop(0, TILES, start, 0)
    each(first_set, "fold", 0)
    each(first_set, "stage", 1)

    def backward(dk_ref, dv_ref):
        def attend_back(block, carry):
            rows = pl.ds(pl.multiple_of(block * BLOCK, BLOCK), BLOCK)
            for group in range(GROUPS):
                lanes = slice(group * LANES, (group + 1) * LANES)
                low, count = group * LANES // CHUNK, LANES // CHUNK
                keys = jnp.concatenate([take(k_ref, rows, low, count), take(sk_ref, rows, low, count)], axis=0).astype(bf16)
                values = jnp.concatenate([take(v_ref, rows, low, count), take(sv_ref, rows, low, count)], axis=0).astype(bf16)
                queries = by_pack(q_ref[rows, lanes])
                mixed_grad = by_pack(mixed_ref[rows, lanes])
                attention = att_ref[block, group]
                prob_grad = mm(values, mixed_grad, 1, 1)
                inner = jnp.sum(attention * prob_grad, axis=0, keepdims=True)
                score_grad = (attention * (prob_grad - inner) * (HEAD_DIM ** -0.5)).astype(bf16)
                q_ref[rows, lanes] = own_heads(mm(score_grad, keys, 0, 0)).astype(bf16)
                key_grad = mm(score_grad, queries)
                value_grad = mm(attention.astype(bf16), mixed_grad)
                put(dk_ref, rows, key_grad[:BLOCK], low)
                put(dv_ref, rows, value_grad[:BLOCK], low)
                put(sk_ref, rows, key_grad[BLOCK:].astype(bf16).astype(f32), low)
                put(sv_ref, rows, value_grad[BLOCK:].astype(bf16).astype(f32), low)
            return carry

        lax.fori_loop(0, BLOCKS // 2, attend_back, 0)
        each(first_set, "fold", 1)
        each(first_set, "stage", 2)
        lax.fori_loop(BLOCKS // 2, BLOCKS, attend_back, 0)
        each(first_set, "fold", 2)
        each(first_set, "stage", 3)
        weights = sink_ref[2 * SINK_ITERS - 1]
        same_head = iota((LOGITS, LOGITS), 0) // BLOCKS == iota((LOGITS, LOGITS), 1) // BLOCKS
        turned = jnp.where(same_head, jnp.concatenate([weights] * HEADS, axis=0), 0.0).T
        probs_back = turned[:BLOCKS]
        for head in range(1, HEADS):
            probs_back = probs_back + turned[head * BLOCKS : (head + 1) * BLOCKS]
        probs_back = probs_back.astype(bf16)

        def sort_back(i, total):
            rows = pl.ds(i, BLOCKS, stride=BLOCK)
            key_part = by_head(take(sk_ref, rows).astype(bf16))
            value_part = by_head(take(sv_ref, rows).astype(bf16))
            put(dk_ref, rows, take(dk_ref, rows) + mm(probs_back, key_part))
            put(dv_ref, rows, take(dv_ref, rows) + mm(probs_back, value_part))
            total = total + mm(key_part, take(k_ref, rows).astype(bf16), 1, 1)
            return total + mm(value_part, take(v_ref, rows).astype(bf16), 1, 1)

        stacked = lax.fori_loop(0, BLOCK, sort_back, jnp.zeros((LOGITS, BLOCKS), f32))
        first = first_ref[...]
        keep(dqkv_ref, 0, slice(None), mm(first, q_ref[...], 0, 0))
        keep(dqkv_ref, 1, slice(None), mm(first, take(dk_ref, slice(None)).astype(bf16), 0, 0))
        keep(dqkv_ref, 2, slice(None), mm(first, take(dv_ref, slice(None)).astype(bf16), 0, 0))
        scatter_qkv.stage(0)
        each(first_set, "fold", 3)

        copies = (iota((BLOCKS, LOGITS), 0) == iota((BLOCKS, LOGITS), 1) % BLOCKS).astype(bf16)
        wide = jnp.where(same_head, exact_dot(stacked, copies), 0.0)
        probs_grad = wide[:BLOCKS]
        for head in range(1, HEADS):
            probs_grad = probs_grad + wide[head * BLOCKS : (head + 1) * BLOCKS]
        logs = logs_ref[...]
        pull = jnp.where(real_col > 0, entropy_weight * (logs + 1.0), 0.0)
        scatter_qkv.fold(0)
        scatter_qkv.stage(1)
        grad = sinkhorn_back(weights * (probs_grad - pull), group_matrix(), lambda index: sink_ref[index])
        logit_grad = jnp.where(allowed, grad / softness_factor, 0.0).astype(bf16)
        sorter_grad = mm(means_ref[...], logit_grad, 0, 0).astype(bf16)
        for high in range(lay.H):
            for low in range(lay.L):
                for part in range(lay.mp):
                    rows = slice((high * lay.L + low) * r, (high * lay.L + low + 1) * r)
                    dsorter_blocks[0, high, low, part] = sorter_grad[rows, part * c : (part + 1) * c]
        scatter_sorter.stage(0)
        spread_ref[...] = mm(logit_grad, sorter_ref[...], 1, 1) / BLOCK
        scatter_qkv.fold(1)
        scatter_qkv.stage(2)
        scatter_sorter.fold(0)
        scatter_sorter.stage(1)
        here = ROWS // BLOCK

        def finish(tile, carry):
            rows = pl.ds(pl.multiple_of(tile * ROWS, ROWS), ROWS)
            spread = spread_ref[pl.ds(pl.multiple_of(tile * here, here), here), :]
            spread = jnp.broadcast_to(spread[:, None, :], (here, BLOCK, WIDTH)).reshape(ROWS, WIDTH)
            first_grad = (
                mm(q_ref[rows, :], weight(qkv_ref, 0), 1, 1)
                + mm(take(dk_ref, rows).astype(bf16), weight(qkv_ref, 1), 1, 1)
                + mm(take(dv_ref, rows).astype(bf16), weight(qkv_ref, 2), 1, 1)
                + spread
            )
            normed, inverse = normalize(x_ref[rows, :].astype(f32))
            grad_ref[rows, :] += norm_back(first_grad, normed, inverse, gain_first)
            gain_grad_ref[0:8, :] += jnp.sum((first_grad * normed).reshape(ROWS // 8, 8, WIDTH), axis=0)
            return carry

        lax.fori_loop(0, TILES, finish, 0)
        entropy = -jnp.sum(jnp.where(real_col > 0, weights * logs, 0.0), axis=0, keepdims=True)
        entropy = jnp.broadcast_to(entropy[:, :128] + entropy[:, 128:], (8, 128))
        total_b.over_mp(jnp.concatenate([
            spread_rows(jnp.sum(gain_grad_ref[0:8, :], axis=0, keepdims=True)),
            spread_rows(jnp.sum(gain_grad_ref[8:16, :], axis=0, keepdims=True)),
            entropy,
        ], axis=0))
        scatter_qkv.fold(2)
        scatter_qkv.stage(3)
        scatter_sorter.fold(1)
        scatter_sorter.stage(2)
        total_b.over_dp()
        scatter_sorter.fold(2)
        scatter_sorter.stage(3)
        small_out[0:16, :] = total_b.result()
        small_out[16:24, :] = summed[8:16]
        scatter_qkv.fold(3)
        scatter_sorter.fold(3)
        each(early + late + tuple(scatters) + (total_a, total_b), "close")

    pl.run_scoped(
        backward,
        pltpu.VMEM((CHUNKS, SEQ_LEN, CHUNK), f32),
        pltpu.VMEM((CHUNKS, SEQ_LEN, CHUNK), f32),
    )


def shape(dims, dtype):
    return jax.ShapeDtypeStruct(dims, dtype)


LIMIT = 63 * 1024 * 1024
TOK = (SEQ_LEN, WIDTH)
SPLIT = (CHUNKS, SEQ_LEN, CHUNK)


def run_step(lay, total_tokens, tokens, cotangent, seg, small, qkv, sorter, wo, feed):
    items = tuple(Item(lay, *w.shape) for w in (qkv, sorter, wo, feed))
    vm = pltpu.VMEM
    count = 4 * (Gather.count(lay) + Scatter.count(lay)) + 2 * Total.count(lay)
    scratch = (
        [vm(item.full(), bf16) for item in items] * 2
        + [vm((WIDTH, LOGITS), bf16), vm(TOK, bf16), vm(TOK, bf16)]
        + [vm(SPLIT, f32)] * 4
        + [
            vm((BLOCKS, GROUPS, 2 * BLOCK, PAIRS), f32), vm(TOK, bf16), vm((BLOCKS, WIDTH), bf16),
            vm((2 * SINK_ITERS, BLOCKS, LOGITS), f32), vm((BLOCKS, LOGITS), f32),
            vm((BLOCKS, PAIRS), f32), vm((BLOCKS, WIDTH), f32), vm((16, WIDTH), f32),
        ]
        + [vm((lay.mp, 16, 128), f32), vm((lay.dp, 16, 128), f32)] * 2
        + [pltpu.SemaphoreType.DMA((count,))] * 2
    )
    for item in items:
        scratch += Scatter.buffers(item)
    return pl.pallas_call(
        functools.partial(step_kernel, lay, items, total_tokens),
        out_shape=[shape(TOK, bf16), shape(TOK, f32)]
        + [shape(item.shard(), f32) for item in items]
        + [shape((24, 128), f32)],
        in_specs=[pl.BlockSpec(memory_space=pltpu.VMEM)] * 8,
        out_specs=[pl.BlockSpec(memory_space=pltpu.VMEM)] * 7,
        scratch_shapes=scratch,
        compiler_params=pltpu.CompilerParams(collective_id=0, has_side_effects=True, vmem_limit_bytes=LIMIT),
        name="step",
    )(tokens, cotangent, seg, small, qkv, sorter, wo, feed)


rate_mixer = 0.2
rate_feed = 0.1
rate_sorter = 0.6
rate_gains = 1.0
beta_first = 0.9
beta_second = 0.95
adam_eps = 1e-08
weight_decay = 0.1


def adamw(master, moment, second, grad, rate, step_value):
    moment_new = beta_first * moment + (1.0 - beta_first) * grad
    second_new = beta_second * second + (1.0 - beta_second) * grad * grad
    first_hat = moment_new / (1.0 - beta_first**step_value)
    second_hat = second_new / (1.0 - beta_second**step_value)
    master_new = master - rate * (
        first_hat / (jnp.sqrt(second_hat) + adam_eps) + weight_decay * master
    )
    return (moment_new, second_new, master_new)


def local(
    lay,
    tokens,
    segment_ids,
    cotangent,
    step_count,
    mixer_weights,
    mixer_moment,
    mixer_second,
    feed_weights,
    feed_moment,
    feed_second,
    sorter_weights,
    sorter_moment,
    sorter_second,
    norm_gains,
    gain_moment,
    gain_second,
):
    dp, mp = lax.axis_index("dp"), lax.axis_index("mp")
    total_tokens = lay.dp * segment_ids.shape[0] * SEQ_LEN
    seg = lax.dynamic_slice_in_dim(segment_ids, mp, 1, axis=0).reshape(BLOCKS, BLOCK)
    mixer = mixer_weights.astype(bf16).transpose(1, 0, 2)
    feed = feed_weights.astype(bf16).transpose(1, 0, 2)
    sorter = sorter_weights.astype(bf16)[None]
    width = norm_gains.shape[1]
    at = (dp * lay.mp + mp) * width
    small = lax.dynamic_update_slice(jnp.zeros((2, WIDTH), f32), norm_gains, (0, at)).reshape(8, 128)
    block_output, token_grad, qkv_sum, sorter_sum, wo_sum, feed_sum, sums = run_step(
        lay, float(total_tokens), tokens, cotangent, seg, small, mixer[:3], sorter, mixer[3:], feed
    )
    block_count = sums[16, 0]
    penalty = jnp.sum(sums[8]) / (block_count * HEADS)
    gain_sum = lax.dynamic_slice(sums[:8].reshape(2, WIDTH), (0, at), (2, width))
    mixer_sum = jnp.concatenate([qkv_sum, wo_sum], axis=0).transpose(1, 0, 2)
    step_value = step_count[0].astype(f32)
    mixer_new = adamw(mixer_weights, mixer_moment, mixer_second, mixer_sum, rate_mixer, step_value)
    feed_new = adamw(feed_weights, feed_moment, feed_second, feed_sum.transpose(1, 0, 2), rate_feed, step_value)
    sorter_new = adamw(sorter_weights, sorter_moment, sorter_second, sorter_sum[0], rate_sorter, step_value)
    gain_new = adamw(norm_gains, gain_moment, gain_second, gain_sum, rate_gains, step_value)
    return (block_output, token_grad, penalty.reshape(1), *mixer_new, *feed_new, *sorter_new, *gain_new)


def solution(mesh):
    return jax.shard_map(
        functools.partial(local, Layout(mesh.shape["dp"], mesh.shape["mp"])),
        mesh=mesh,
        in_specs=(
            P(("dp", "mp"), None),
            P("dp", None),
            P(("dp", "mp"), None),
            P(),
            P("dp", None, "mp"),
            P("dp", None, "mp"),
            P("dp", None, "mp"),
            P("dp", None, "mp"),
            P("dp", None, "mp"),
            P("dp", None, "mp"),
            P("dp", "mp"),
            P("dp", "mp"),
            P("dp", "mp"),
            P(None, ("dp", "mp")),
            P(None, ("dp", "mp")),
            P(None, ("dp", "mp")),
        ),
        out_specs=(
            P(("dp", "mp"), None),
            P(("dp", "mp"), None),
            P(),
            P("dp", None, "mp"),
            P("dp", None, "mp"),
            P("dp", None, "mp"),
            P("dp", None, "mp"),
            P("dp", None, "mp"),
            P("dp", None, "mp"),
            P("dp", "mp"),
            P("dp", "mp"),
            P("dp", "mp"),
            P(None, ("dp", "mp")),
            P(None, ("dp", "mp")),
            P(None, ("dp", "mp")),
        ),
        check_vma=False,
    )
```

time: 1120 us -> 199 us (0.18)
  waiting for transfers between devices: 531 us -> 0 us
  matrix products: 206 us -> 0 us
  Pallas kernels: 0 us -> 171 us
  blocking collectives: 165 us -> 0 us
  local copies, waits for them, and re-layouts: 109 us -> 17 us
  other arithmetic: 78.5 us -> 6.33 us
  between operations: 23.3 us -> 3.92 us
    reduce_scatter x6 -> x0, waiting for transfers between devices: 270 us -> none  [the longest x4 270 us: scatter_rows(): lax.psum_scatter(term_fn(jnp.int32(0), local_rows * lax.axis_size('mp')),...]
    dot_general x24 -> x0, matrix products: 206 us -> none  [the longest x1 55.8 us: local(): jnp.einsum('ghnij,ghnie->ghnje', raw_grad, query_blocks, preferred_elemen...]
    unnamed x15 -> x0, waiting for transfers between devices: 200 us -> none
    pallas_call x0 -> x1, Pallas kernels: none -> 171 us  [run_step(): pl.pallas_call(functools.partial(step_kernel, lay, items, total_tokens),...]
    all_gather x3 -> x0, blocking collectives: 106 us -> none  [the longest x1 43.5 us: local(): gain_rows = lax.all_gather(norm_gains, ('dp', 'mp'), axis=1, tiled=True)]
    all_gather x5 -> x0, waiting for transfers between devices: 61.6 us -> none  [the longest x4 61.6 us: gather_rows(): return lax.all_gather(block_rows, 'mp', axis=0, tiled=True)]
    psum x2 -> x0, blocking collectives: 59.2 us -> none  [the longest x1 36.8 us: local(): entropy_total = lax.psum(entropy_local, ('dp', 'mp'))]
    reshape x19 -> x3, local copies, waits for them, and re-layouts: 54.7 us -> 1.29 us  [the longest x1 0.68 us: local(): lax.dynamic_slice_in_dim(segment_ids, mp, 1, axis=0).reshape(BLOCKS, BLOCK)]
  transfers between devices with their start and end apart: 13 -> 0, of which waited for: 8 -> 0; matrix products, arithmetic and copies ran while one was open for 26% -> 0% of each run, Pallas kernels for 0% -> 0%
where the time goes in v1:
time: 199 us; the launch traced here: 198 us
  Pallas kernels  171 us (86%)
  local copies, waits for them, and re-layouts  17 us (9%)
  other arithmetic  6.33 us (3%)
  between operations  3.92 us (2%)
    pallas_call x1, Pallas kernels, run_step(): pl.pallas_call(functools.partial(step_kernel, lay, items, total_tokens),...  171 us
    unnamed x36, local copies, waits for them, and re-layouts  11.8 us

profile of v1, /device:TPU:0, one launch (start us, length us, event | category | flops | bytes accessed | tf_op | source)
XLA Modules:
  0.0 198.3 jit_solution(7480530580250231496)
XLA Ops:
  0.6 0.0 copy-start
  0.7 0.0 copy-start.3
  0.7 0.7 copy-done
  1.4 0.7 reshape.53.seg_ref
  2.1 0.8 dynamic_update_slice.3
  2.9 0.6 reshape.54.small_ref
  3.5 0.9 copy.72
  4.4 0.6 slice.20.qkv_in
  5.0 1.4 convert_bitcast_fusion.sorter_in
  6.4 0.6 slice.21.wo_in
  7.0 1.6 copy.71
  8.6 0.0 copy-start.2
  8.6 0.0 copy-start.4
  8.6 0.0 copy-start.5
  8.6 171.0 %step.1 = (bf16[1024,512]{1,0:T(8,128)(2,1)}, f32[1024,512]{1,0:T(8,128)}, f32[3,64,128]{2,1,0:T(8,128)}, f32[1,64,64]{2,1,0:T(8,128)}, f32[1,64,128]{2,1,0:T(8,...) custom-call(bf16[1024,512]{1,0:T(8,128)(2,1)} %x_ref.1, bf16[1024,512]{1,0:T(8,128)(2,1)} %cot_ref.1, ...), custom_call_target="tpu_custom_call" | custom-call | tf_op jit(solution)/shard_map/step/pallas_call | solution.py:847
  179.6 1.3 slice_reduce_fusion
  180.9 1.2 slice.18
  184.1 0.0 copy-done.3
  184.1 1.2 multiply_subtract_fusion.1
  185.3 0.0 copy-start.6
  185.3 0.0 copy-start.7
  185.3 0.0 copy-start.8
  185.3 0.0 copy-start.9
  185.3 0.7 copy.41
  186.1 0.0 copy-start.10
  186.1 0.0 copy-start.11
  186.1 0.7 copy.42
  186.8 0.7 copy.43
  187.6 0.0 copy-done.2
  187.6 0.0 copy-done.4
  187.6 0.0 copy-done.5
  187.6 1.2 multiply_subtract_fusion
  188.8 0.9 copy.44
  189.7 0.9 copy.45
  190.6 0.9 copy.46
  191.5 0.0 copy-done.6
  191.5 0.0 copy-done.7
  191.5 0.0 copy-done.8
  191.5 0.0 copy-done.9
  191.5 0.7 multiply_subtract_fusion.2
  192.2 0.7 slice.19
  192.9 0.0 copy-done.10
  192.9 0.0 copy-done.11
  192.9 0.0 copy-done.12
  192.9 0.7 add_subtract_fusion
  193.6 2.3 %copy.77 = bf16[1024,512]{1,0:T(8,128)(2,1)} copy(bf16[1024,512]{1,0:T(8,128)(2,1)} %get-tuple-element.71) | data formatting | bytes 2097152
  195.8 0.0 copy-done.1
  195.8 1.3 copy.78
  (5 shorter events, 0.0 us)
Async XLA Ops:
  0.6 0.7 copy-start
  0.7 183.5 %copy-start.3 = (f32[64,4,128]{2,1,0:T(4,128)S(1)}, f32[64,4,128]{2,1,0:T(4,128)}, u32[]{:S(2)}) copy-start(f32[64,4,128]{2,1,0:T(4,128)} %param.20) | copy-start | bytes 393220
  8.6 179.0 %copy-start.2 = (f32[64,2,512]{2,1,0:T(2,128)S(1)}, f32[64,2,512]{2,1,0:T(2,128)}, u32[]{:S(2)}) copy-start(f32[64,2,512]{2,1,0:T(2,128)} %param.23) | copy-start | bytes 786436
  8.6 179.0 %copy-start.4 = (f32[64,2,512]{2,1,0:T(2,128)S(1)}, f32[64,2,512]{2,1,0:T(2,128)}, u32[]{:S(2)}) copy-start(f32[64,2,512]{2,1,0:T(2,128)} %param.25) | copy-start | bytes 786436
  8.6 179.0 %copy-start.5 = (f32[64,2,512]{2,1,0:T(2,128)S(1)}, f32[64,2,512]{2,1,0:T(2,128)}, u32[]{:S(2)}) copy-start(f32[64,2,512]{2,1,0:T(2,128)} %param.24) | copy-start | bytes 786436
  185.3 6.2 %copy-start.6 = (f32[64,64]{1,0:T(8,128)S(1)}, f32[64,64]{1,0:T(8,128)}, u32[]{:S(2)}) copy-start(f32[64,64]{1,0:T(8,128)} %param.26) | copy-start | bytes 49156
  185.3 6.2 %copy-start.7 = (f32[64,64]{1,0:T(8,128)S(1)}, f32[64,64]{1,0:T(8,128)}, u32[]{:S(2)}) copy-start(f32[64,64]{1,0:T(8,128)} %param.28) | copy-start | bytes 49156
  185.3 6.2 %copy-start.8 = (f32[64,64]{1,0:T(8,128)S(1)}, f32[64,64]{1,0:T(8,128)}, u32[]{:S(2)}) copy-start(f32[64,64]{1,0:T(8,128)} %param.27) | copy-start | bytes 49156
  185.3 6.2 %copy-start.9 = (f32[1,64,64]{2,1,0:T(8,128)S(1)}, f32[1,64,64]{2,1,0:T(8,128)}, u32[]{:S(2)}) copy-start(f32[1,64,64]{2,1,0:T(8,128)} %get-tuple-element.28) | copy-start | bytes 49156
  186.1 6.8 %copy-start.10 = (f32[2,16]{1,0:T(2,128)S(1)}, f32[2,16]{1,0:T(2,128)}, u32[]{:S(2)}) copy-start(f32[2,16]{1,0:T(2,128)} %param.29) | copy-start | bytes 388
  186.1 6.8 %copy-start.11 = (f32[2,16]{1,0:T(2,128)S(1)}, f32[2,16]{1,0:T(2,128)}, u32[]{:S(2)}) copy-start(f32[2,16]{1,0:T(2,128)} %param.31) | copy-start | bytes 388
  186.1 6.8 %copy-start.12 = (f32[2,16]{1,0:T(2,128)S(1)}, f32[2,16]{1,0:T(2,128)}, u32[]{:S(2)}) copy-start(f32[2,16]{1,0:T(2,128)} %param.30) | copy-start | bytes 388
  188.8 7.0 %copy-start.1 = (f32[1024,512]{1,0:T(8,128)S(1)}, f32[1024,512]{1,0:T(8,128)}, u32[]{:S(2)}) copy-start(f32[1024,512]{1,0:T(8,128)} %get-tuple-element.72) | copy-start | bytes 6291460

commit v2 on v1

--- a/solution.py
+++ b/solution.py
@@ -1,4 +1,5 @@
 import functools
+import math
 import jax
 import jax.numpy as jnp
 from jax import lax
@@ -21,6 +22,8 @@
 GROUPS = HEADS // PACK
 LANES = PACK * HEAD_DIM
 PAIRS = PACK * BLOCK
+PAIR = 2 * HEAD_DIM
+UNROLL = 4
 
 norm_eps = 1e-05
 softness_factor = 0.75
@@ -112,12 +115,6 @@
     return grad
 
 
-def by_head(tile):
-    rows = jnp.concatenate([tile] * HEADS, axis=0)
-    keep = iota((LOGITS, WIDTH), 0) // BLOCKS == iota((LOGITS, WIDTH), 1) // HEAD_DIM
-    return jnp.where(keep, rows, jnp.zeros_like(rows))
-
-
 def by_pack(tile):
     rows = jnp.concatenate([tile] * PACK, axis=0)
     keep = iota((PAIRS, LANES), 0) // BLOCK == iota((PAIRS, LANES), 1) // HEAD_DIM
@@ -132,17 +129,20 @@
     return out
 
 
-CHUNK = 128
-CHUNKS = WIDTH // CHUNK
-
-
-def take(ref, rows, low=0, count=CHUNKS):
-    return jnp.concatenate([ref[part, rows, :] for part in range(low, low + count)], axis=1)
-
-
-def put(ref, rows, value, low=0):
-    for part in range(value.shape[1] // CHUNK):
-        ref[low + part, rows, :] = value[:, part * CHUNK : (part + 1) * CHUNK]
+STACK = 8
+SPAN = STACK * BLOCKS
+
+
+def by_place(rows):
+    lanes = rows.shape[1]
+    return jnp.swapaxes(rows.reshape(BLOCKS, BLOCK, lanes), 0, 1).reshape(SEQ_LEN, lanes)
+
+
+def repeated(matrix):
+    wide = jnp.concatenate([matrix] * STACK, axis=1)
+    wide = jnp.concatenate([wide] * STACK, axis=0)
+    keep = iota((SPAN, SPAN), 0) // BLOCKS == iota((SPAN, SPAN), 1) // BLOCKS
+    return jnp.where(keep, wide, jnp.zeros_like(wide))
 
 
 MESH = pl.DeviceIdType.MESH
@@ -492,36 +492,53 @@
     return jnp.sum(jnp.where(same, jnp.broadcast_to(row, (count, count)), 0.0), axis=1, keepdims=True)
 
 
+def spot(width):
+    at = (lax.axis_index("dp") * lax.axis_size("mp") + lax.axis_index("mp")) * width
+    return (iota((width, WIDTH), 1) == iota((width, WIDTH), 0) + at).astype(bf16)
+
+
+def packing(r, c):
+    return 128 // c if c < 128 and (r * c // 128) % 16 == 0 else 1
+
+
 def step_kernel(
-    lay, items, total_tokens,
-    x_ref, cot_ref, seg_ref, small_ref, qkv_in, sorter_in, wo_in, feed_in,
-    out_ref, grad_ref, qkv_out, sorter_out, wo_out, feed_out, small_out,
+    lay, gathers, scatter_items, total_tokens,
+    tokens_ref, cotangent_ref, segment_ref, gains_in, mixer_in, feed_in, sorter_in,
+    out_hbm, grad_hbm, feed_a_out, feed_b_out, woq_out, kv_out, sorter_out, small_out,
     *scratch,
 ):
-    qkv_item, sorter_item, wo_item, feed_item = items
     scratch = list(scratch)
+
+    def pop(count):
+        taken = scratch[:count]
+        del scratch[:count]
+        return taken
+
+    shards, weights_full, grads_full = pop(5), pop(5), pop(5)
+    qkv_ref, sorter_full, wo_ref, feed_a_ref, feed_b_ref = weights_full
+    dfeed_a_ref, dfeed_b_ref, dwoq_ref, dkv_ref, dsorter_full = grads_full
+    x_ref, cot_ref, out_ref, grad_ref = pop(4)
     (
-        qkv_ref, sorter_blocks, wo_ref, feed_ref, dqkv_ref, dsorter_blocks, dwo_ref, dfeed_ref,
-        sorter_ref, first_ref, q_ref, k_ref, v_ref, sk_ref, sv_ref, att_ref, mixed_ref, means_ref, sink_ref, logs_ref,
-        segrow_ref, spread_ref, gain_grad_ref,
-        near_a, far_a, near_b, far_b, send_sems, recv_sems,
-    ) = scratch[:29]
-    rest = scratch[29:]
+        sorter_ref, first_ref, q_ref, k_ref, v_ref, sk_ref, sv_ref, place_k_ref, place_v_ref,
+        att_ref, mixed_ref, means_ref, sink_ref, logs_ref, segrow_ref, spread_ref, gain_grad_ref,
+        second_ref, act_ref, pre_ref, total_ref, second_grad_ref, pair_k_ref, pair_v_ref,
+    ) = pop(24)
+    dk_ref, dv_ref = total_ref, second_grad_ref
+    near_a, far_a, near_b, far_b, send_sems, recv_sems, copy_sems = pop(7)
     sems = Sems(send_sems, recv_sems)
+    fetch_x = pltpu.make_async_copy(tokens_ref, x_ref, copy_sems.at[0])
+    fetch_cot = pltpu.make_async_copy(cotangent_ref, cot_ref, copy_sems.at[1])
+    fetch_x.start()
+    fetch_cot.start()
+    mp = lax.axis_index("mp")
     meet(lay)
-    gather_qkv = Gather(qkv_item, qkv_in, qkv_ref, sems)
-    gather_sorter = Gather(sorter_item, sorter_in, sorter_blocks, sems)
-    gather_wo = Gather(wo_item, wo_in, wo_ref, sems)
-    gather_feed = Gather(feed_item, feed_in, feed_ref, sems)
-    early, late = (gather_qkv, gather_sorter), (gather_wo, gather_feed)
+    gather = [Gather(item, shard, full, sems) for item, shard, full in zip(gathers, shards, weights_full)]
+    early, middle_set, late = tuple(gather[:2]), (gather[2], gather[3]), (gather[4],)
     scatters = []
-    for item, full, out in (
-        (qkv_item, dqkv_ref, qkv_out), (sorter_item, dsorter_blocks, sorter_out),
-        (wo_item, dwo_ref, wo_out), (feed_item, dfeed_ref, feed_out),
-    ):
-        scatters.append(Scatter(item, full, rest[:7], out, sems))
-        rest = rest[7:]
-    scatter_qkv, scatter_sorter, scatter_wo, scatter_feed = scatters
+    outs = (feed_a_out, feed_b_out, woq_out, kv_out, sorter_out)
+    for item, full, out in zip(scatter_items, grads_full, outs):
+        scatters.append(Scatter(item, full, pop(7), out, sems))
+    scatter_a, scatter_b, scatter_woq, scatter_kv, scatter_sorter = scatters
     total_a = Total(lay, near_a, far_a, sems)
     total_b = Total(lay, near_b, far_b, sems)
 
@@ -529,27 +546,48 @@
         for member in group:
             getattr(member, name)(*args)
 
-    seg = seg_ref[...].astype(f32)
+    width = gains_in.shape[1]
+    lane = iota((BLOCKS, SEQ_LEN), 1)
+    row = segment_ref[pl.ds(mp, 1), :].astype(f32)
+    picked = jnp.where(lane // BLOCK == iota((BLOCKS, SEQ_LEN), 0), jnp.broadcast_to(row, (BLOCKS, SEQ_LEN)), 0.0)
+    seg = picked[:, :PAIRS]
+    for at in range(PAIRS, SEQ_LEN, PAIRS):
+        seg = seg + picked[:, at : at + PAIRS]
+    tiling = (iota((PAIRS, PAIRS), 0) % BLOCK == iota((PAIRS, PAIRS), 1) % BLOCK).astype(bf16)
+    seg = exact_dot(seg, tiling)
+    segrow_ref[...] = seg
     real_col = (seg[:, 0:1] > 0).astype(f32)
+    count = jnp.broadcast_to(jnp.sum(real_col, axis=0, keepdims=True), (8, 128))
+    placed = exact_dot(gains_in[...], spot(width))
+    total_a.over_mp(jnp.concatenate([spread_rows(placed[0:1]), spread_rows(placed[1:2]), count], axis=0))
+    for j in range(3):
+        shards[0][j] = mixer_in[:, j, :].astype(bf16)
+    pack = packing(*sorter_in.shape)
+    deep = sorter_in.shape[0] // pack
+    sorter_shard = sorter_in[...].astype(bf16)
+    shards[1][0] = jnp.concatenate([sorter_shard[k * deep : (k + 1) * deep] for k in range(pack)], axis=1)
+    each(early, "stage", 0)
+    each(early, "place")
+    shards[2][0] = mixer_in[:, 3, :].astype(bf16)
+    half_width = feed_in.shape[2] // 2
+    for j in range(2):
+        shards[3][j] = feed_in[:, j, :half_width].astype(bf16)
+        shards[4][j] = feed_in[:, j, half_width:].astype(bf16)
+    each(middle_set + late, "place")
     lane_block = iota((BLOCKS, LOGITS), 1) % BLOCKS
     real_row = jnp.sum(jnp.where(iota((BLOCKS, LOGITS), 0) == lane_block, real_col, 0.0), axis=0, keepdims=True)
-    count = jnp.broadcast_to(jnp.sum(real_col, axis=0, keepdims=True), (8, 128))
-    total_a.over_mp(jnp.concatenate([small_ref[...], count], axis=0))
-    each(early, "stage", 0)
-    each(early + late, "place")
-    segrow_ref[...] = jnp.concatenate([seg] * PACK, axis=1)
+    allowed = permitted(real_col, real_row)
     total_a.over_dp()
     each(early, "landed")
     each(early, "stage", 1)
-    each(late, "stage", 0)
+    each(middle_set, "stage", 0)
     summed = total_a.result()
     gain_first = joined_row(summed[0:4])
     gain_second = joined_row(summed[4:8])
     entropy_weight = penalty_weight * total_tokens / (summed[8:9, 0:1] * HEADS)
     each(early, "landed")
     each(early, "stage", 2)
-    each(early, "landed")
-    each(early, "stage", 3)
+    fetch_x.wait()
 
     def norm_first(tile, carry):
         rows = pl.ds(pl.multiple_of(tile * ROWS, ROWS), ROWS)
@@ -562,8 +600,11 @@
     means = (mm(member, first_ref[...]) / BLOCK).astype(bf16)
     means_ref[...] = means
     each(early, "landed")
-    each(late, "landed")
-    each(late, "stage", 1)
+    each(early, "stage", 3)
+    each(middle_set, "landed")
+    each(middle_set, "stage", 1)
+    each(late, "stage", 0)
+    each(early, "landed")
 
     def weight(ref, j, cols=slice(None)):
         if len(ref.shape) == 6:
@@ -576,21 +617,32 @@
         rows = pl.ds(pl.multiple_of(tile * ROWS, ROWS), ROWS)
         first = first_ref[rows, :]
         q_ref[rows, :] = mm(first, weight(qkv_ref, 0)).astype(bf16)
-        put(k_ref, rows, mm(first, weight(qkv_ref, 1)).astype(bf16).astype(f32))
-        put(v_ref, rows, mm(first, weight(qkv_ref, 2)).astype(bf16).astype(f32))
+        k_ref[rows, :] = mm(first, weight(qkv_ref, 1)).astype(bf16)
+        v_ref[rows, :] = mm(first, weight(qkv_ref, 2)).astype(bf16)
         return carry
 
     lax.fori_loop(0, TILES, project, 0)
-    r, c = sorter_item.r, sorter_item.c
-    for high in range(lay.H):
-        for low in range(lay.L):
-            for part in range(lay.mp):
-                rows = slice((high * lay.L + low) * r, (high * lay.L + low + 1) * r)
-                sorter_ref[rows, part * c : (part + 1) * c] = sorter_blocks[0, high, low, part]
+    r, c = sorter_in.shape
+
+    def sorter_places():
+        for high in range(lay.H):
+            for low in range(lay.L):
+                for part in range(lay.mp):
+                    base = (high * lay.L + low) * r
+                    if pack == 1:
+                        index = (0, high, low, part)
+                    else:
+                        index = (0, high, low, slice(None), slice(part * 128, (part + 1) * 128))
+                    rows = [slice(base + k * deep, base + (k + 1) * deep) for k in range(pack)]
+                    yield index, rows, slice(part * c, (part + 1) * c)
+
+    for index, rows, cols in sorter_places():
+        tile = sorter_full[index]
+        for k in range(pack):
+            sorter_ref[rows[k], cols] = tile[:, k * c : (k + 1) * c]
     logits = mm(means, sorter_ref[...])
-    allowed = permitted(real_col, real_row)
-    each(late, "landed")
-    each(late, "stage", 2)
+    each(middle_set, "landed")
+    each(middle_set, "stage", 2)
 
     def store(index, value):
         sink_ref[index] = value
@@ -598,39 +650,69 @@
     logs, weights = sinkhorn(logits, allowed, group_matrix(), store)
     logs_ref[...] = logs
     probs = weights.astype(bf16)
-
-    def sort(i, carry):
-        rows = pl.ds(i, BLOCKS, stride=BLOCK)
-        put(sk_ref, rows, mm(probs, by_head(take(k_ref, rows).astype(bf16))))
-        put(sv_ref, rows, mm(probs, by_head(take(v_ref, rows).astype(bf16))))
-        return carry
-
-    lax.fori_loop(0, BLOCK, sort, 0)
+    place_k_ref[...] = by_place(k_ref[...])
+    place_v_ref[...] = by_place(v_ref[...])
+    first_head = iota((SPAN, 2 * PAIR), 1) % PAIR < HEAD_DIM
+
+    def rearrange(matrices, keys, values, keys_out, values_out):
+        for pair in range(HEADS // 2):
+            lanes = slice(pair * PAIR, (pair + 1) * PAIR)
+            one, two = matrices(2 * pair), matrices(2 * pair + 1)
+            for part in range(SEQ_LEN // SPAN):
+                rows = slice(part * SPAN, (part + 1) * SPAN)
+                both = jnp.concatenate([keys[rows, lanes], values[rows, lanes]], axis=1)
+                out = jnp.where(first_head, mm(one, both), mm(two, both))
+                keys_out[rows, lanes] = out[:, :PAIR].astype(keys_out.dtype)
+                values_out[rows, lanes] = out[:, PAIR:].astype(values_out.dtype)
+
+    def forth(head):
+        return repeated(probs[:, head * BLOCKS : (head + 1) * BLOCKS])
+
+    rearrange(forth, place_k_ref, place_v_ref, sk_ref, sv_ref)
+    sk_ref[...] = by_place(sk_ref[...])
+    sv_ref[...] = by_place(sv_ref[...])
     each(late, "landed")
-    each(late, "stage", 3)
-
-    def attend(block, carry):
-        rows = pl.ds(pl.multiple_of(block * BLOCK, BLOCK), BLOCK)
-        row = segrow_ref[pl.ds(block, 1), :]
-        near = diagonal_column(row[:, :BLOCK], BLOCK) == row
-        far = jnp.broadcast_to(row > 0, (BLOCK, PAIRS))
-        mask = jnp.concatenate([near, far], axis=0)
-        for group in range(GROUPS):
-            lanes = slice(group * LANES, (group + 1) * LANES)
-            low, count = group * LANES // CHUNK, LANES // CHUNK
-            keys = jnp.concatenate([take(k_ref, rows, low, count), take(sk_ref, rows, low, count)], axis=0).astype(bf16)
-            values = jnp.concatenate([take(v_ref, rows, low, count), take(sv_ref, rows, low, count)], axis=0).astype(bf16)
-            queries = by_pack(q_ref[rows, lanes])
+    each(late, "stage", 1)
+
+    def block_rows(block):
+        return pl.ds(pl.multiple_of(block * BLOCK, BLOCK), BLOCK)
+
+    def operands(block, group):
+        rows = block_rows(block)
+        lanes = slice(group * LANES, (group + 1) * LANES)
+        keys = jnp.concatenate([k_ref[rows, lanes], sk_ref[rows, lanes]], axis=0)
+        values = jnp.concatenate([v_ref[rows, lanes], sv_ref[rows, lanes]], axis=0)
+        return keys, values, by_pack(q_ref[rows, lanes])
+
+    def attend(step, carry):
+        units = []
+        for block in [step * UNROLL + k for k in range(UNROLL)]:
+            row = segrow_ref[pl.ds(block, 1), :]
+            near = diagonal_column(row[:, :BLOCK], BLOCK) == row
+            far = jnp.broadcast_to(row > 0, (BLOCK, PAIRS))
+            mask = jnp.concatenate([near, far], axis=0)
+            units += [(block, group, mask, *operands(block, group)) for group in range(GROUPS)]
+        results = []
+        for block, group, mask, keys, values, queries in units:
             scores = jnp.where(mask, mm(keys, queries, 1, 1) * (HEAD_DIM ** -0.5), excluded_fill)
             shifted = jnp.exp(scores - jnp.max(scores, axis=0, keepdims=True))
             attention = shifted * (1.0 / jnp.sum(shifted, axis=0, keepdims=True))
+            results.append((attention, own_heads(mm(attention.astype(bf16), values, 0, 0)).astype(bf16)))
+        for (block, group, *_), (attention, mixed) in zip(units, results):
             att_ref[block, group] = attention
-            mixed_ref[rows, lanes] = own_heads(mm(attention.astype(bf16), values, 0, 0)).astype(bf16)
+            mixed_ref[block_rows(block), group * LANES : (group + 1) * LANES] = mixed
         return carry
 
-    lax.fori_loop(0, BLOCKS, attend, 0)
+    half = BLOCKS // UNROLL // 2
+    lax.fori_loop(0, half, attend, 0)
+    each(middle_set, "landed")
+    each(middle_set, "stage", 3)
     each(late, "landed")
+    each(late, "stage", 2)
+    lax.fori_loop(half, 2 * half, attend, 0)
+    fetch_cot.wait()
     gain_grad_ref[...] = jnp.zeros_like(gain_grad_ref)
+    each(middle_set, "landed")
 
     def keep(ref, j, cols, value):
         if len(ref.shape) == 6:
@@ -640,51 +722,75 @@
             return
         ref[j, :, :, :, cols] = value.astype(bf16).reshape(lay.H, lay.L, WIDTH // lay.dp, value.shape[1])
 
-    def feed_phase(second_ref, act_ref, pre_ref):
-        def feed(tile, carry):
-            rows = pl.ds(pl.multiple_of(tile * ROWS, ROWS), ROWS)
-            middle = x_ref[rows, :].astype(f32) + mm(mixed_ref[rows, :], weight(wo_ref, 0), 1, 1)
-            normed, inverse = normalize(middle)
-            second = (normed * gain_second).astype(bf16)
-            second_ref[rows, :] = second
-            cot = cot_ref[rows, :]
-            total = middle
-            second_grad = jnp.zeros((ROWS, WIDTH), f32)
-            for part in range(HIDDEN // WIDTH):
-                cols = slice(part * WIDTH, (part + 1) * WIDTH)
-                up, down = weight(feed_ref, 0, cols), weight(feed_ref, 1, cols)
-                pre = mm(second, up)
-                act = jnp.maximum(pre, 0.0).astype(bf16)
-                act_ref[rows, cols] = act
-                total = total + mm(act, down, 1, 1)
-                pre_grad = jnp.where(pre > 0, mm(cot, down), 0.0).astype(bf16)
-                pre_ref[rows, cols] = pre_grad
-                second_grad = second_grad + mm(pre_grad, up, 1, 1)
-            out_ref[rows, :] = total.astype(bf16)
-            grad_ref[rows, :] = cot.astype(f32) + norm_back(second_grad, normed, inverse, gain_second)
-            gain_grad_ref[8:16, :] += jnp.sum((second_grad * normed).reshape(ROWS // 8, 8, WIDTH), axis=0)
-            return carry
-
-        lax.fori_loop(0, TILES, feed, 0)
-
-        def feed_weights(part, carry):
+    def open_rows(tile, carry):
+        rows = pl.ds(pl.multiple_of(tile * ROWS, ROWS), ROWS)
+        middle = x_ref[rows, :].astype(f32) + mm(mixed_ref[rows, :], weight(wo_ref, 0), 1, 1)
+        grad_ref[rows, :] = middle
+        normed, _ = normalize(middle)
+        second_ref[rows, :] = (normed * gain_second).astype(bf16)
+        return carry
+
+    def feed_rows(feed_ref, rows, total, second_grad):
+        second, cot = second_ref[rows, :], cot_ref[rows, :]
+        for part in range(feed_ref.shape[-1] // WIDTH):
+            cols = slice(part * WIDTH, (part + 1) * WIDTH)
+            up, down = weight(feed_ref, 0, cols), weight(feed_ref, 1, cols)
+            pre = mm(second, up)
+            act = jnp.maximum(pre, 0.0).astype(bf16)
+            act_ref[rows, cols] = act
+            total = total + mm(act, down, 1, 1)
+            pre_grad = jnp.where(pre > 0, mm(cot, down), 0.0).astype(bf16)
+            pre_ref[rows, cols] = pre_grad
+            partial = mm(pre_grad, up, 1, 1)
+            second_grad = partial if second_grad is None else second_grad + partial
+        return total, second_grad
+
+    def feed_a(tile, carry):
+        rows = pl.ds(pl.multiple_of(tile * ROWS, ROWS), ROWS)
+        total, second_grad = feed_rows(feed_a_ref, rows, grad_ref[rows, :], None)
+        total_ref[rows, :] = total
+        second_grad_ref[rows, :] = second_grad
+        return carry
+
+    def feed_b(tile, carry):
+        rows = pl.ds(pl.multiple_of(tile * ROWS, ROWS), ROWS)
+        total, second_grad = feed_rows(feed_b_ref, rows, total_ref[rows, :], second_grad_ref[rows, :])
+        out_ref[rows, :] = total.astype(bf16)
+        normed, inverse = normalize(grad_ref[rows, :])
+        grad_ref[rows, :] = cot_ref[rows, :].astype(f32) + norm_back(second_grad, normed, inverse, gain_second)
+        gain_grad_ref[8:16, :] += jnp.sum((second_grad * normed).reshape(ROWS // 8, 8, WIDTH), axis=0)
+        return carry
+
+    def feed_weights(dfeed_ref):
+        def run(part, carry):
             cols = pl.ds(pl.multiple_of(part * WIDTH, WIDTH), WIDTH)
             keep(dfeed_ref, 0, cols, mm(second_ref[...], pre_ref[:, cols], 0, 0))
             keep(dfeed_ref, 1, cols, mm(cot_ref[...], act_ref[:, cols], 0, 0))
             return carry
 
-        lax.fori_loop(0, HIDDEN // WIDTH, feed_weights, 0)
-
-    pl.run_scoped(
-        feed_phase,
-        pltpu.VMEM((SEQ_LEN, WIDTH), bf16),
-        pltpu.VMEM((SEQ_LEN, HIDDEN), bf16),
-        pltpu.VMEM((SEQ_LEN, HIDDEN), bf16),
-    )
-    scatter_feed.stage(0)
-    keep(dwo_ref, 0, slice(None), mm(grad_ref[...].astype(bf16), mixed_ref[...], 0, 0))
-    scatter_wo.stage(0)
-    first_set = (scatter_feed, scatter_wo)
+        lax.fori_loop(0, dfeed_ref.shape[-1] // WIDTH, run, 0)
+
+    lax.fori_loop(0, TILES, open_rows, 0)
+    lax.fori_loop(0, TILES // 2, feed_a, 0)
+    each(late, "landed")
+    each(late, "stage", 3)
+    lax.fori_loop(TILES // 2, TILES, feed_a, 0)
+    feed_weights(dfeed_a_ref)
+    scatter_a.stage(0)
+    each(late, "landed")
+    lax.fori_loop(0, TILES // 2, feed_b, 0)
+    scatter_a.fold(0)
+    scatter_a.stage(1)
+    lax.fori_loop(TILES // 2, TILES, feed_b, 0)
+    write_out = pltpu.make_async_copy(out_ref, out_hbm, copy_sems.at[2])
+    write_out.start()
+    scatter_a.fold(1)
+    scatter_a.stage(2)
+    feed_weights(dfeed_b_ref)
+    scatter_b.stage(0)
+    scatter_a.fold(2)
+    scatter_a.stage(3)
+    keep(dwoq_ref, 0, slice(None), mm(grad_ref[...].astype(bf16), mixed_ref[...], 0, 0))
 
     def start(tile, carry):
         rows = pl.ds(pl.multiple_of(tile * ROWS, ROWS), ROWS)
@@ -692,129 +798,216 @@
         return carry
 
     lax.fori_loop(0, TILES, start, 0)
-    each(first_set, "fold", 0)
-    each(first_set, "stage", 1)
-
-    def backward(dk_ref, dv_ref):
-        def attend_back(block, carry):
-            rows = pl.ds(pl.multiple_of(block * BLOCK, BLOCK), BLOCK)
+    scatter_b.fold(0)
+    scatter_b.stage(1)
+
+    def attend_back(step, carry):
+        units = []
+        for block in [step * UNROLL + k for k in range(UNROLL)]:
             for group in range(GROUPS):
-                lanes = slice(group * LANES, (group + 1) * LANES)
-                low, count = group * LANES // CHUNK, LANES // CHUNK
-                keys = jnp.concatenate([take(k_ref, rows, low, count), take(sk_ref, rows, low, count)], axis=0).astype(bf16)
-                values = jnp.concatenate([take(v_ref, rows, low, count), take(sv_ref, rows, low, count)], axis=0).astype(bf16)
-                queries = by_pack(q_ref[rows, lanes])
-                mixed_grad = by_pack(mixed_ref[rows, lanes])
-                attention = att_ref[block, group]
-                prob_grad = mm(values, mixed_grad, 1, 1)
-                inner = jnp.sum(attention * prob_grad, axis=0, keepdims=True)
-                score_grad = (attention * (prob_grad - inner) * (HEAD_DIM ** -0.5)).astype(bf16)
-                q_ref[rows, lanes] = own_heads(mm(score_grad, keys, 0, 0)).astype(bf16)
-                key_grad = mm(score_grad, queries)
-                value_grad = mm(attention.astype(bf16), mixed_grad)
-                put(dk_ref, rows, key_grad[:BLOCK], low)
-                put(dv_ref, rows, value_grad[:BLOCK], low)
-                put(sk_ref, rows, key_grad[BLOCK:].astype(bf16).astype(f32), low)
-                put(sv_ref, rows, value_grad[BLOCK:].astype(bf16).astype(f32), low)
-            return carry
-
-        lax.fori_loop(0, BLOCKS // 2, attend_back, 0)
-        each(first_set, "fold", 1)
-        each(first_set, "stage", 2)
-        lax.fori_loop(BLOCKS // 2, BLOCKS, attend_back, 0)
-        each(first_set, "fold", 2)
-        each(first_set, "stage", 3)
-        weights = sink_ref[2 * SINK_ITERS - 1]
-        same_head = iota((LOGITS, LOGITS), 0) // BLOCKS == iota((LOGITS, LOGITS), 1) // BLOCKS
-        turned = jnp.where(same_head, jnp.concatenate([weights] * HEADS, axis=0), 0.0).T
-        probs_back = turned[:BLOCKS]
-        for head in range(1, HEADS):
-            probs_back = probs_back + turned[head * BLOCKS : (head + 1) * BLOCKS]
-        probs_back = probs_back.astype(bf16)
-
-        def sort_back(i, total):
-            rows = pl.ds(i, BLOCKS, stride=BLOCK)
-            key_part = by_head(take(sk_ref, rows).astype(bf16))
-            value_part = by_head(take(sv_ref, rows).astype(bf16))
-            put(dk_ref, rows, take(dk_ref, rows) + mm(probs_back, key_part))
-            put(dv_ref, rows, take(dv_ref, rows) + mm(probs_back, value_part))
-            total = total + mm(key_part, take(k_ref, rows).astype(bf16), 1, 1)
-            return total + mm(value_part, take(v_ref, rows).astype(bf16), 1, 1)
-
-        stacked = lax.fori_loop(0, BLOCK, sort_back, jnp.zeros((LOGITS, BLOCKS), f32))
-        first = first_ref[...]
-        keep(dqkv_ref, 0, slice(None), mm(first, q_ref[...], 0, 0))
-        keep(dqkv_ref, 1, slice(None), mm(first, take(dk_ref, slice(None)).astype(bf16), 0, 0))
-        keep(dqkv_ref, 2, slice(None), mm(first, take(dv_ref, slice(None)).astype(bf16), 0, 0))
-        scatter_qkv.stage(0)
-        each(first_set, "fold", 3)
-
-        copies = (iota((BLOCKS, LOGITS), 0) == iota((BLOCKS, LOGITS), 1) % BLOCKS).astype(bf16)
-        wide = jnp.where(same_head, exact_dot(stacked, copies), 0.0)
-        probs_grad = wide[:BLOCKS]
-        for head in range(1, HEADS):
-            probs_grad = probs_grad + wide[head * BLOCKS : (head + 1) * BLOCKS]
-        logs = logs_ref[...]
-        pull = jnp.where(real_col > 0, entropy_weight * (logs + 1.0), 0.0)
-        scatter_qkv.fold(0)
-        scatter_qkv.stage(1)
-        grad = sinkhorn_back(weights * (probs_grad - pull), group_matrix(), lambda index: sink_ref[index])
-        logit_grad = jnp.where(allowed, grad / softness_factor, 0.0).astype(bf16)
-        sorter_grad = mm(means_ref[...], logit_grad, 0, 0).astype(bf16)
-        for high in range(lay.H):
-            for low in range(lay.L):
-                for part in range(lay.mp):
-                    rows = slice((high * lay.L + low) * r, (high * lay.L + low + 1) * r)
-                    dsorter_blocks[0, high, low, part] = sorter_grad[rows, part * c : (part + 1) * c]
-        scatter_sorter.stage(0)
-        spread_ref[...] = mm(logit_grad, sorter_ref[...], 1, 1) / BLOCK
-        scatter_qkv.fold(1)
-        scatter_qkv.stage(2)
-        scatter_sorter.fold(0)
-        scatter_sorter.stage(1)
-        here = ROWS // BLOCK
-
-        def finish(tile, carry):
-            rows = pl.ds(pl.multiple_of(tile * ROWS, ROWS), ROWS)
-            spread = spread_ref[pl.ds(pl.multiple_of(tile * here, here), here), :]
-            spread = jnp.broadcast_to(spread[:, None, :], (here, BLOCK, WIDTH)).reshape(ROWS, WIDTH)
-            first_grad = (
-                mm(q_ref[rows, :], weight(qkv_ref, 0), 1, 1)
-                + mm(take(dk_ref, rows).astype(bf16), weight(qkv_ref, 1), 1, 1)
-                + mm(take(dv_ref, rows).astype(bf16), weight(qkv_ref, 2), 1, 1)
-                + spread
-            )
-            normed, inverse = normalize(x_ref[rows, :].astype(f32))
-            grad_ref[rows, :] += norm_back(first_grad, normed, inverse, gain_first)
-            gain_grad_ref[0:8, :] += jnp.sum((first_grad * normed).reshape(ROWS // 8, 8, WIDTH), axis=0)
-            return carry
-
-        lax.fori_loop(0, TILES, finish, 0)
-        entropy = -jnp.sum(jnp.where(real_col > 0, weights * logs, 0.0), axis=0, keepdims=True)
-        entropy = jnp.broadcast_to(entropy[:, :128] + entropy[:, 128:], (8, 128))
-        total_b.over_mp(jnp.concatenate([
-            spread_rows(jnp.sum(gain_grad_ref[0:8, :], axis=0, keepdims=True)),
-            spread_rows(jnp.sum(gain_grad_ref[8:16, :], axis=0, keepdims=True)),
-            entropy,
-        ], axis=0))
-        scatter_qkv.fold(2)
-        scatter_qkv.stage(3)
-        scatter_sorter.fold(1)
-        scatter_sorter.stage(2)
-        total_b.over_dp()
-        scatter_sorter.fold(2)
-        scatter_sorter.stage(3)
-        small_out[0:16, :] = total_b.result()
-        small_out[16:24, :] = summed[8:16]
-        scatter_qkv.fold(3)
-        scatter_sorter.fold(3)
-        each(early + late + tuple(scatters) + (total_a, total_b), "close")
-
-    pl.run_scoped(
-        backward,
-        pltpu.VMEM((CHUNKS, SEQ_LEN, CHUNK), f32),
-        pltpu.VMEM((CHUNKS, SEQ_LEN, CHUNK), f32),
-    )
+                mixed_grad = by_pack(mixed_ref[block_rows(block), group * LANES : (group + 1) * LANES])
+                units.append((block, group, mixed_grad, att_ref[block, group], *operands(block, group)))
+        results = []
+        for block, group, mixed_grad, attention, keys, values, queries in units:
+            prob_grad = mm(values, mixed_grad, 1, 1)
+            inner = jnp.sum(attention * prob_grad, axis=0, keepdims=True)
+            score_grad = (attention * (prob_grad - inner) * (HEAD_DIM ** -0.5)).astype(bf16)
+            results.append((
+                own_heads(mm(score_grad, keys, 0, 0)).astype(bf16),
+                mm(score_grad, queries),
+                mm(attention.astype(bf16), mixed_grad),
+            ))
+        for (block, group, *_), (query_grad, key_grad, value_grad) in zip(units, results):
+            rows = block_rows(block)
+            lanes = slice(group * LANES, (group + 1) * LANES)
+            q_ref[rows, lanes] = query_grad
+            dk_ref[rows, lanes] = key_grad[:BLOCK]
+            dv_ref[rows, lanes] = value_grad[:BLOCK]
+            sk_ref[rows, lanes] = key_grad[BLOCK:].astype(bf16)
+            sv_ref[rows, lanes] = value_grad[BLOCK:].astype(bf16)
+        return carry
+
+    lax.fori_loop(0, half, attend_back, 0)
+    scatter_a.fold(3)
+    scatter_b.fold(1)
+    scatter_b.stage(2)
+    lax.fori_loop(half, 2 * half, attend_back, 0)
+    first = first_ref[...]
+    keep(dwoq_ref, 1, slice(None), mm(first, q_ref[...], 0, 0))
+    scatter_woq.stage(0)
+    scatter_b.fold(2)
+    scatter_b.stage(3)
+    weights = sink_ref[2 * SINK_ITERS - 1]
+    same_head = iota((LOGITS, LOGITS), 0) // BLOCKS == iota((LOGITS, LOGITS), 1) // BLOCKS
+    turned = jnp.where(same_head, jnp.concatenate([weights] * HEADS, axis=0), 0.0).T
+
+    def back(head):
+        rows = slice(head * BLOCKS, (head + 1) * BLOCKS)
+        return repeated(turned[rows, rows].astype(bf16))
+
+    sk_ref[...] = by_place(sk_ref[...])
+    sv_ref[...] = by_place(sv_ref[...])
+    rearrange(back, sk_ref, sv_ref, pair_k_ref, pair_v_ref)
+    key_grad = (dk_ref[...] + by_place(pair_k_ref[...])).astype(bf16)
+    value_grad = (dv_ref[...] + by_place(pair_v_ref[...])).astype(bf16)
+    k_ref[...] = key_grad
+    v_ref[...] = value_grad
+    keep(dkv_ref, 0, slice(None), mm(first, key_grad, 0, 0))
+    keep(dkv_ref, 1, slice(None), mm(first, value_grad, 0, 0))
+    scatter_kv.stage(0)
+    scatter_woq.fold(0)
+    scatter_woq.stage(1)
+    scatter_b.fold(3)
+    lane_head = iota((SPAN, PAIR), 1) // HEAD_DIM
+    diagonal = iota((SPAN, SPAN), 0) // BLOCKS == iota((SPAN, SPAN), 1) // BLOCKS
+    folded = []
+    for pair in range(HEADS // 2):
+        lanes = slice(pair * PAIR, (pair + 1) * PAIR)
+        parts = [slice(part * SPAN, (part + 1) * SPAN) for part in range(SEQ_LEN // SPAN)]
+        right = [ref[rows, lanes] for rows in parts for ref in (place_k_ref, place_v_ref)]
+        left = [ref[rows, lanes] for rows in parts for ref in (sk_ref, sv_ref)]
+        for head in range(2):
+            mine = [jnp.where(lane_head == head, tile, jnp.zeros_like(tile)) for tile in left]
+            square = mm(jnp.concatenate(mine, axis=1), jnp.concatenate(right, axis=1), 1, 1)
+            square = jnp.where(diagonal, square, 0.0)
+            total = square[:BLOCKS]
+            for place in range(1, STACK):
+                total = total + square[place * BLOCKS : (place + 1) * BLOCKS]
+            folded.append(total)
+    copies = (iota((BLOCKS, LOGITS), 0) == iota((BLOCKS, LOGITS), 1) % BLOCKS).astype(bf16)
+    stacked = exact_dot(jnp.concatenate(folded, axis=0), copies.T)
+    wide = jnp.where(same_head, exact_dot(stacked, copies), 0.0)
+    probs_grad = wide[:BLOCKS]
+    for head in range(1, HEADS):
+        probs_grad = probs_grad + wide[head * BLOCKS : (head + 1) * BLOCKS]
+    logs = logs_ref[...]
+    pull = jnp.where(real_col > 0, entropy_weight * (logs + 1.0), 0.0)
+    scatter_kv.fold(0)
+    scatter_kv.stage(1)
+    grad = sinkhorn_back(weights * (probs_grad - pull), group_matrix(), lambda index: sink_ref[index])
+    logit_grad = jnp.where(allowed, grad / softness_factor, 0.0).astype(bf16)
+    sorter_grad = mm(means_ref[...], logit_grad, 0, 0).astype(bf16)
+    for index, rows, cols in sorter_places():
+        pieces = [sorter_grad[rows[k], cols] for k in range(pack)]
+        dsorter_full[index] = jnp.concatenate(pieces, axis=1) if pack > 1 else pieces[0]
+    scatter_sorter.stage(0)
+    spread_ref[...] = mm(logit_grad, sorter_ref[...], 1, 1) / BLOCK
+    scatter_woq.fold(1)
+    scatter_woq.stage(2)
+    scatter_kv.fold(1)
+    scatter_kv.stage(2)
+    scatter_sorter.fold(0)
+    scatter_sorter.stage(1)
+    here = ROWS // BLOCK
+
+    def finish(tile, carry):
+        rows = pl.ds(pl.multiple_of(tile * ROWS, ROWS), ROWS)
+        spread = spread_ref[pl.ds(pl.multiple_of(tile * here, here), here), :]
+        spread = jnp.broadcast_to(spread[:, None, :], (here, BLOCK, WIDTH)).reshape(ROWS, WIDTH)
+        first_grad = (
+            mm(q_ref[rows, :], weight(qkv_ref, 0), 1, 1)
+            + mm(k_ref[rows, :], weight(qkv_ref, 1), 1, 1)
+            + mm(v_ref[rows, :], weight(qkv_ref, 2), 1, 1)
+            + spread
+        )
+        normed, inverse = normalize(x_ref[rows, :].astype(f32))
+        grad_ref[rows, :] += norm_back(first_grad, normed, inverse, gain_first)
+        gain_grad_ref[0:8, :] += jnp.sum((first_grad * normed).reshape(ROWS // 8, 8, WIDTH), axis=0)
+        return carry
+
+    writes = []
+
+    def write_rows(part):
+        rows = slice(part * SEQ_LEN // 2, (part + 1) * SEQ_LEN // 2)
+        copy = pltpu.make_async_copy(grad_ref.at[rows], grad_hbm.at[rows], copy_sems.at[3 + part])
+        copy.start()
+        writes.append(copy)
+
+    lax.fori_loop(0, TILES // 2, finish, 0)
+    write_rows(0)
+    scatter_woq.fold(2)
+    scatter_woq.stage(3)
+    scatter_kv.fold(2)
+    scatter_kv.stage(3)
+    scatter_sorter.fold(1)
+    scatter_sorter.stage(2)
+    lax.fori_loop(TILES // 2, TILES, finish, 0)
+    write_rows(1)
+    entropy = -jnp.sum(jnp.where(real_col > 0, weights * logs, 0.0), axis=0, keepdims=True)
+    entropy = jnp.broadcast_to(entropy[:, :128] + entropy[:, 128:], (8, 128))
+    total_b.over_mp(jnp.concatenate([
+        spread_rows(jnp.sum(gain_grad_ref[0:8, :], axis=0, keepdims=True)),
+        spread_rows(jnp.sum(gain_grad_ref[8:16, :], axis=0, keepdims=True)),
+        entropy,
+    ], axis=0))
+    scatter_sorter.fold(2)
+    scatter_sorter.stage(3)
+    total_b.over_dp()
+    scatter_woq.fold(3)
+    scatter_kv.fold(3)
+    scatter_sorter.fold(3)
+    small_out[0:16, :] = total_b.result()
+    small_out[16:24, :] = summed[8:16]
+    write_out.wait()
+    for copy in writes:
+        copy.wait()
+    each(tuple(gather) + tuple(scatters) + (total_a, total_b), "close")
+
+
+def update_kernel(
+    lay, step_ref, out_in, grad_in, feed_a, feed_b, woq, kv, sorter, sums, *refs
+):
+    masters, results = refs[:12], refs[12:27]
+    out_rows, grad_rows, sem = refs[27:]
+    block_out, token_out, penalty_out = results[:3]
+    moves = []
+    for part in range(2):
+        rows = slice(part * SEQ_LEN // 2, (part + 1) * SEQ_LEN // 2)
+        for which, (source, middle, target) in enumerate(
+            ((out_in, out_rows, block_out), (grad_in, grad_rows, token_out))
+        ):
+            moves.append((
+                pltpu.make_async_copy(source.at[rows], middle.at[rows], sem.at[part, which, 0]),
+                pltpu.make_async_copy(middle.at[rows], target.at[rows], sem.at[part, which, 1]),
+            ))
+    for bring, _ in moves:
+        bring.start()
+    step_value = jnp.full((1, 128), step_ref[0], jnp.int32).astype(f32)
+    scale_first = 1.0 / (1.0 - jnp.exp(step_value * math.log(beta_first)))[:, 0:1]
+    scale_second = 1.0 / (1.0 - jnp.exp(step_value * math.log(beta_second)))[:, 0:1]
+
+    def adamw(which, index, grad, rate):
+        master, moment, second = [ref[index] for ref in masters[3 * which : 3 * which + 3]]
+        moment_new = beta_first * moment + (1.0 - beta_first) * grad
+        second_new = beta_second * second + (1.0 - beta_second) * grad * grad
+        change = (moment_new * scale_first) / (jnp.sqrt(second_new * scale_second) + adam_eps)
+        outs = results[3 + 3 * which : 6 + 3 * which]
+        outs[0][index] = moment_new
+        outs[1][index] = second_new
+        outs[2][index] = master - rate * (change + weight_decay * master)
+
+    for j, grad in enumerate((woq[1], kv[0], kv[1], woq[0])):
+        adamw(0, (ALLR, j, ALLR), grad, rate_mixer)
+    for bring, send in moves:
+        bring.wait()
+        send.start()
+    half = feed_a.shape[2]
+    for j in range(2):
+        adamw(1, (ALLR, j, slice(0, half)), feed_a[j], rate_feed)
+        adamw(1, (ALLR, j, slice(half, 2 * half)), feed_b[j], rate_feed)
+    r, c = masters[6].shape
+    pack = packing(r, c)
+    deep = r // pack
+    grad = jnp.concatenate([sorter[0][:, k * c : (k + 1) * c] for k in range(pack)], axis=0) if pack > 1 else sorter[0]
+    adamw(2, (ALLR, ALLR), grad, rate_sorter)
+    rows = jnp.concatenate([joined_row(sums[0:4, :]), joined_row(sums[4:8, :])], axis=0)
+    own = spot(masters[9].shape[1])
+    grad = sum(mm(part, own, 1, 1) for part in three_parts(rows))
+    adamw(3, (ALLR, ALLR), grad, rate_gains)
+    entropy = jnp.sum(sums[8:9, :], axis=1, keepdims=True)
+    penalty_out[...] = jnp.broadcast_to(entropy / (sums[16:17, 0:1] * HEADS), (1, 128))
+    for _, send in moves:
+        send.wait()
 
 
 def shape(dims, dtype):
@@ -823,38 +1016,64 @@
 
 LIMIT = 63 * 1024 * 1024
 TOK = (SEQ_LEN, WIDTH)
-SPLIT = (CHUNKS, SEQ_LEN, CHUNK)
-
-
-def run_step(lay, total_tokens, tokens, cotangent, seg, small, qkv, sorter, wo, feed):
-    items = tuple(Item(lay, *w.shape) for w in (qkv, sorter, wo, feed))
+
+
+def run_step(lay, total_tokens, tokens, cotangent, segment_ids, gains, mixer, feed, sorter):
+    r, c, half = mixer.shape[0], mixer.shape[2], feed.shape[2] // 2
+    pack = packing(*sorter.shape)
+    sorter_item = Item(lay, 1, sorter.shape[0] // pack, sorter.shape[1] * pack)
+    feed_item, pair_item = Item(lay, 2, r, half), Item(lay, 2, r, c)
+    gathers = (Item(lay, 3, r, c), sorter_item, Item(lay, 1, r, c), feed_item, feed_item)
+    scatters = (feed_item, feed_item, pair_item, pair_item, sorter_item)
     vm = pltpu.VMEM
-    count = 4 * (Gather.count(lay) + Scatter.count(lay)) + 2 * Total.count(lay)
+    count = 5 * (Gather.count(lay) + Scatter.count(lay)) + 2 * Total.count(lay)
     scratch = (
-        [vm(item.full(), bf16) for item in items] * 2
-        + [vm((WIDTH, LOGITS), bf16), vm(TOK, bf16), vm(TOK, bf16)]
-        + [vm(SPLIT, f32)] * 4
+        [vm(item.shard(), bf16) for item in gathers]
+        + [vm(item.full(), bf16) for item in gathers + scatters]
+        + [vm(TOK, bf16), vm(TOK, bf16), vm(TOK, bf16), vm(TOK, f32)]
+        + [vm((WIDTH, LOGITS), bf16)]
+        + [vm(TOK, bf16)] * 8
         + [
             vm((BLOCKS, GROUPS, 2 * BLOCK, PAIRS), f32), vm(TOK, bf16), vm((BLOCKS, WIDTH), bf16),
             vm((2 * SINK_ITERS, BLOCKS, LOGITS), f32), vm((BLOCKS, LOGITS), f32),
             vm((BLOCKS, PAIRS), f32), vm((BLOCKS, WIDTH), f32), vm((16, WIDTH), f32),
+            vm(TOK, bf16), vm((SEQ_LEN, HIDDEN // 2), bf16), vm((SEQ_LEN, HIDDEN // 2), bf16),
         ]
+        + [vm(TOK, f32)] * 4
         + [vm((lay.mp, 16, 128), f32), vm((lay.dp, 16, 128), f32)] * 2
         + [pltpu.SemaphoreType.DMA((count,))] * 2
+        + [pltpu.SemaphoreType.DMA((5,))]
     )
-    for item in items:
+    for item in scatters:
         scratch += Scatter.buffers(item)
+    inside = pl.BlockSpec(memory_space=pltpu.VMEM)
+    outside = pl.BlockSpec(memory_space=pl.ANY)
     return pl.pallas_call(
-        functools.partial(step_kernel, lay, items, total_tokens),
+        functools.partial(step_kernel, lay, gathers, scatters, total_tokens),
         out_shape=[shape(TOK, bf16), shape(TOK, f32)]
-        + [shape(item.shard(), f32) for item in items]
+        + [shape(item.shard(), f32) for item in scatters]
         + [shape((24, 128), f32)],
-        in_specs=[pl.BlockSpec(memory_space=pltpu.VMEM)] * 8,
-        out_specs=[pl.BlockSpec(memory_space=pltpu.VMEM)] * 7,
+        in_specs=[outside] * 2 + [inside] * 5,
+        out_specs=[outside] * 2 + [inside] * 6,
         scratch_shapes=scratch,
         compiler_params=pltpu.CompilerParams(collective_id=0, has_side_effects=True, vmem_limit_bytes=LIMIT),
         name="step",
-    )(tokens, cotangent, seg, small, qkv, sorter, wo, feed)
+    )(tokens, cotangent, segment_ids, gains, mixer, feed, sorter)
+
+
+def run_update(lay, step_count, block_output, token_grad, sums, states):
+    inside = pl.BlockSpec(memory_space=pltpu.VMEM)
+    outside = pl.BlockSpec(memory_space=pl.ANY)
+    outs = [shape(TOK, bf16), shape(TOK, f32), shape((1, 128), f32)] + [shape(state.shape, f32) for state in states]
+    return pl.pallas_call(
+        functools.partial(update_kernel, lay),
+        out_shape=outs,
+        in_specs=[pl.BlockSpec(memory_space=pltpu.SMEM)] + [outside] * 2 + [inside] * 18,
+        out_specs=[outside] * 2 + [inside] * 13,
+        scratch_shapes=[pltpu.VMEM(TOK, bf16), pltpu.VMEM(TOK, f32), pltpu.SemaphoreType.DMA((2, 2, 2))],
+        compiler_params=pltpu.CompilerParams(vmem_limit_bytes=LIMIT),
+        name="update",
+    )(step_count, block_output, token_grad, *sums, *states)
 
 
 rate_mixer = 0.2
@@ -865,17 +1084,6 @@
 beta_second = 0.95
 adam_eps = 1e-08
 weight_decay = 0.1
-
-
-def adamw(master, moment, second, grad, rate, step_value):
-    moment_new = beta_first * moment + (1.0 - beta_first) * grad
-    second_new = beta_second * second + (1.0 - beta_second) * grad * grad
-    first_hat = moment_new / (1.0 - beta_first**step_value)
-    second_hat = second_new / (1.0 - beta_second**step_value)
-    master_new = master - rate * (
-        first_hat / (jnp.sqrt(second_hat) + adam_eps) + weight_decay * master
-    )
-    return (moment_new, second_new, master_new)
 
 
 def local(
@@ -897,28 +1105,16 @@
     gain_moment,
     gain_second,
 ):
-    dp, mp = lax.axis_index("dp"), lax.axis_index("mp")
-    total_tokens = lay.dp * segment_ids.shape[0] * SEQ_LEN
-    seg = lax.dynamic_slice_in_dim(segment_ids, mp, 1, axis=0).reshape(BLOCKS, BLOCK)
-    mixer = mixer_weights.astype(bf16).transpose(1, 0, 2)
-    feed = feed_weights.astype(bf16).transpose(1, 0, 2)
-    sorter = sorter_weights.astype(bf16)[None]
-    width = norm_gains.shape[1]
-    at = (dp * lay.mp + mp) * width
-    small = lax.dynamic_update_slice(jnp.zeros((2, WIDTH), f32), norm_gains, (0, at)).reshape(8, 128)
-    block_output, token_grad, qkv_sum, sorter_sum, wo_sum, feed_sum, sums = run_step(
-        lay, float(total_tokens), tokens, cotangent, seg, small, mixer[:3], sorter, mixer[3:], feed
+    total_tokens = float(lay.dp * segment_ids.shape[0] * SEQ_LEN)
+    block_output, token_grad, *sums = run_step(
+        lay, total_tokens, tokens, cotangent, segment_ids, norm_gains, mixer_weights, feed_weights, sorter_weights
     )
-    block_count = sums[16, 0]
-    penalty = jnp.sum(sums[8]) / (block_count * HEADS)
-    gain_sum = lax.dynamic_slice(sums[:8].reshape(2, WIDTH), (0, at), (2, width))
-    mixer_sum = jnp.concatenate([qkv_sum, wo_sum], axis=0).transpose(1, 0, 2)
-    step_value = step_count[0].astype(f32)
-    mixer_new = adamw(mixer_weights, mixer_moment, mixer_second, mixer_sum, rate_mixer, step_value)
-    feed_new = adamw(feed_weights, feed_moment, feed_second, feed_sum.transpose(1, 0, 2), rate_feed, step_value)
-    sorter_new = adamw(sorter_weights, sorter_moment, sorter_second, sorter_sum[0], rate_sorter, step_value)
-    gain_new = adamw(norm_gains, gain_moment, gain_second, gain_sum, rate_gains, step_value)
-    return (block_output, token_grad, penalty.reshape(1), *mixer_new, *feed_new, *sorter_new, *gain_new)
+    states = (
+        mixer_weights, mixer_moment, mixer_second, feed_weights, feed_moment, feed_second,
+        sorter_weights, sorter_moment, sorter_second, norm_gains, gain_moment, gain_second,
+    )
+    block_output, token_grad, penalty, *states = run_update(lay, step_count, block_output, token_grad, sums, states)
+    return (block_output, token_grad, penalty[0, :1], *states)
 
 
 def solution(mesh):

time: 199 us -> 126 us (0.63)
  Pallas kernels: 171 us -> 124 us
  local copies, waits for them, and re-layouts: 17 us -> 0 us
  other arithmetic: 6.33 us -> 0 us
  between operations: 3.92 us -> 1.48 us
    pallas_call x1 -> x2, Pallas kernels: 171 us -> 124 us  [the longest x1 118 us: run_step(): pl.pallas_call(functools.partial(step_kernel, lay, gathers, scatters, tot...]
    unnamed x36 -> x0, local copies, waits for them, and re-layouts: 11.8 us -> none
    sub x4 -> x0, other arithmetic: 3.69 us -> none  [adamw(): master - rate * (first_hat / (jnp.sqrt(second_hat) + adam_eps) + weight_d...]
    slice x4 -> x0, local copies, waits for them, and re-layouts: 3.1 us -> none  [the longest x1 1.19 us: local(): block_count = sums[16, 0]]
where the time goes in v2:
time: 126 us
  Pallas kernels  124 us (98%)
  between operations  1.48 us (1%)
    pallas_call x1, Pallas kernels, run_step(): pl.pallas_call(functools.partial(step_kernel, lay, gathers, scatters, tot...  118 us
    pallas_call x1, Pallas kernels, run_update(): pl.pallas_call(functools.partial(update_kernel, lay), out_shape=outs, in_...  5.77 us

profile of v2, /device:TPU:0, one launch (start us, length us, event | category | flops | bytes accessed | tf_op | source)
XLA Modules:
  0.0 125.6 jit_solution(2723830608548671504)
XLA Ops:
  1.3 118.3 %step.1 = (bf16[1024,512]{1,0:T(8,128)(2,1)}, f32[1024,512]{1,0:T(8,128)}, f32[2,64,256]{2,1,0:T(8,128)}, f32[2,64,256]{2,1,0:T(8,128)}, f32[2,64,128]{2,1,0:T(8...) custom-call(bf16[1024,512]{1,0:T(8,128)(2,1)} %tokens_ref.1, ...), custom_call_target="tpu_custom_call" | custom-call | tf_op jit(solution)/shard_map/step/pallas_call | solution.py:1051
  119.6 5.8 %update.1 = (bf16[1024,512]{1,0:T(8,128)(2,1)}, f32[1024,512]{1,0:T(8,128)}, f32[1,128]{1,0:T(1,128)}, f32[64,4,128]{2,1,0:T(4,128)}, f32[64,4,128]{2,1,0:T(4,12...) custom-call(s32[1]{0:T(128)S(6)} %copy.31.step_ref, ...), custom_call_target="tpu_custom_call" | custom-call | tf_op jit(solution)/shard_map/update/pallas_call | solution.py:1068

commit v3 on v2

--- a/solution.py
+++ b/solution.py
@@ -16,14 +16,14 @@
 SEQ_LEN = 1024
 BLOCKS = 32
 LOGITS = HEADS * BLOCKS
-ROWS = 256
+ROWS = 512
 TILES = SEQ_LEN // ROWS
 PACK = 4
 GROUPS = HEADS // PACK
 LANES = PACK * HEAD_DIM
 PAIRS = PACK * BLOCK
 PAIR = 2 * HEAD_DIM
-UNROLL = 4
+UNROLL = 8
 
 norm_eps = 1e-05
 softness_factor = 0.75
@@ -469,14 +469,17 @@
         return lay.mp - 1 + lay.dp - 1
 
 
-def meet(lay):
+def greet(lay):
     barrier = pltpu.get_barrier_semaphore()
     dp, mp = lax.axis_index("dp"), lax.axis_index("mp")
     for k in range(1, lay.mp):
         pl.semaphore_signal(barrier, inc=1, device_id=(dp, (mp + k) % lay.mp), device_id_type=MESH)
     for k in range(1, lay.dp):
         pl.semaphore_signal(barrier, inc=1, device_id=((dp + k) % lay.dp, mp), device_id_type=MESH)
-    pl.semaphore_wait(barrier, lay.mp + lay.dp - 2)
+
+
+def await_all(lay):
+    pl.semaphore_wait(pltpu.get_barrier_semaphore(), lay.mp + lay.dp - 2)
 
 
 def spread_rows(row):
@@ -503,11 +506,10 @@
 
 def step_kernel(
     lay, gathers, scatter_items, total_tokens,
-    tokens_ref, cotangent_ref, segment_ref, gains_in, mixer_in, feed_in, sorter_in,
-    out_hbm, grad_hbm, feed_a_out, feed_b_out, woq_out, kv_out, sorter_out, small_out,
-    *scratch,
+    tokens_ref, cotangent_ref, segment_ref, gains_in, mixer_hbm, feed_hbm, sorter_hbm,
+    out_hbm, grad_hbm, *refs,
 ):
-    scratch = list(scratch)
+    sums_hbm, scratch = refs[:6], list(refs[6:])
 
     def pop(count):
         taken = scratch[:count]
@@ -515,29 +517,42 @@
         return taken
 
     shards, weights_full, grads_full = pop(5), pop(5), pop(5)
-    qkv_ref, sorter_full, wo_ref, feed_a_ref, feed_b_ref = weights_full
+    kv_ref, sorter_full, woq_ref, feed_a_ref, feed_b_ref = weights_full
     dfeed_a_ref, dfeed_b_ref, dwoq_ref, dkv_ref, dsorter_full = grads_full
     x_ref, cot_ref, out_ref, grad_ref = pop(4)
     (
         sorter_ref, first_ref, q_ref, k_ref, v_ref, sk_ref, sv_ref, place_k_ref, place_v_ref,
         att_ref, mixed_ref, means_ref, sink_ref, logs_ref, segrow_ref, spread_ref, gain_grad_ref,
-        second_ref, act_ref, pre_ref, total_ref, second_grad_ref, pair_k_ref, pair_v_ref,
-    ) = pop(24)
+        second_ref, act_ref, pre_ref, total_ref, second_grad_ref,
+    ) = pop(22)
     dk_ref, dv_ref = total_ref, second_grad_ref
     near_a, far_a, near_b, far_b, send_sems, recv_sems, copy_sems = pop(7)
     sems = Sems(send_sems, recv_sems)
     fetch_x = pltpu.make_async_copy(tokens_ref, x_ref, copy_sems.at[0])
     fetch_cot = pltpu.make_async_copy(cotangent_ref, cot_ref, copy_sems.at[1])
+    mixer_in, feed_in, sorter_in = pop(3)
+    fetches = [
+        pltpu.make_async_copy(source, target, copy_sems.at[5 + k])
+        for k, (source, target) in enumerate(
+            ((mixer_hbm, mixer_in), (sorter_hbm, sorter_in), (feed_hbm, feed_in))
+        )
+    ]
+    begin(fetches)
     fetch_x.start()
     fetch_cot.start()
     mp = lax.axis_index("mp")
-    meet(lay)
+    greet(lay)
     gather = [Gather(item, shard, full, sems) for item, shard, full in zip(gathers, shards, weights_full)]
-    early, middle_set, late = tuple(gather[:2]), (gather[2], gather[3]), (gather[4],)
+    early = tuple(gather[:2])
+    gather_woq, gather_a, gather_b = gather[2:]
     scatters = []
-    outs = (feed_a_out, feed_b_out, woq_out, kv_out, sorter_out)
+    *outs, small_out = sums = pop(6)
     for item, full, out in zip(scatter_items, grads_full, outs):
         scatters.append(Scatter(item, full, pop(7), out, sems))
+    write_sums = [
+        pltpu.make_async_copy(buffer, target, copy_sems.at[8 + k])
+        for k, (buffer, target) in enumerate(zip(sums, sums_hbm))
+    ]
     scatter_a, scatter_b, scatter_woq, scatter_kv, scatter_sorter = scatters
     total_a = Total(lay, near_a, far_a, sems)
     total_b = Total(lay, near_b, far_b, sems)
@@ -559,51 +574,66 @@
     real_col = (seg[:, 0:1] > 0).astype(f32)
     count = jnp.broadcast_to(jnp.sum(real_col, axis=0, keepdims=True), (8, 128))
     placed = exact_dot(gains_in[...], spot(width))
-    total_a.over_mp(jnp.concatenate([spread_rows(placed[0:1]), spread_rows(placed[1:2]), count], axis=0))
-    for j in range(3):
-        shards[0][j] = mixer_in[:, j, :].astype(bf16)
+    small = jnp.concatenate([spread_rows(placed[0:1]), spread_rows(placed[1:2]), count], axis=0)
+    for fetch in fetches:
+        fetch.wait()
+    for j, source in enumerate((1, 2)):
+        shards[0][j] = mixer_in[:, source, :].astype(bf16)
     pack = packing(*sorter_in.shape)
     deep = sorter_in.shape[0] // pack
     sorter_shard = sorter_in[...].astype(bf16)
     shards[1][0] = jnp.concatenate([sorter_shard[k * deep : (k + 1) * deep] for k in range(pack)], axis=1)
-    each(early, "stage", 0)
-    each(early, "place")
-    shards[2][0] = mixer_in[:, 3, :].astype(bf16)
+    for j, source in enumerate((3, 0)):
+        shards[2][j] = mixer_in[:, source, :].astype(bf16)
     half_width = feed_in.shape[2] // 2
     for j in range(2):
         shards[3][j] = feed_in[:, j, :half_width].astype(bf16)
         shards[4][j] = feed_in[:, j, half_width:].astype(bf16)
-    each(middle_set + late, "place")
+    each(gather, "place")
     lane_block = iota((BLOCKS, LOGITS), 1) % BLOCKS
     real_row = jnp.sum(jnp.where(iota((BLOCKS, LOGITS), 0) == lane_block, real_col, 0.0), axis=0, keepdims=True)
     allowed = permitted(real_col, real_row)
+    await_all(lay)
+    each(early, "stage", 0)
+    total_a.over_mp(small)
+    gather_woq.stage(0)
+    fetch_x.wait()
+
+    def norm_rows(tile, carry):
+        rows = pl.ds(pl.multiple_of(tile * ROWS, ROWS), ROWS)
+        total_ref[rows, :] = normalize(x_ref[rows, :].astype(f32))[0]
+        return carry
+
+    lax.fori_loop(0, TILES, norm_rows, 0)
     total_a.over_dp()
     each(early, "landed")
     each(early, "stage", 1)
-    each(middle_set, "stage", 0)
+    gather_a.stage(0)
+    each(early, "landed")
+    each(early, "stage", 2)
+    gather_woq.landed()
+    gather_woq.stage(1)
     summed = total_a.result()
     gain_first = joined_row(summed[0:4])
     gain_second = joined_row(summed[4:8])
     entropy_weight = penalty_weight * total_tokens / (summed[8:9, 0:1] * HEADS)
-    each(early, "landed")
-    each(early, "stage", 2)
-    fetch_x.wait()
 
     def norm_first(tile, carry):
         rows = pl.ds(pl.multiple_of(tile * ROWS, ROWS), ROWS)
-        normed, _ = normalize(x_ref[rows, :].astype(f32))
-        first_ref[rows, :] = (normed * gain_first).astype(bf16)
+        first_ref[rows, :] = (total_ref[rows, :] * gain_first).astype(bf16)
         return carry
 
     lax.fori_loop(0, TILES, norm_first, 0)
     member = (iota((BLOCKS, SEQ_LEN), 0) == iota((BLOCKS, SEQ_LEN), 1) // BLOCK).astype(bf16)
     means = (mm(member, first_ref[...]) / BLOCK).astype(bf16)
     means_ref[...] = means
+    gather_b.stage(0)
     each(early, "landed")
     each(early, "stage", 3)
-    each(middle_set, "landed")
-    each(middle_set, "stage", 1)
-    each(late, "stage", 0)
+    gather_a.landed()
+    gather_a.stage(1)
+    gather_woq.landed()
+    gather_woq.stage(2)
     each(early, "landed")
 
     def weight(ref, j, cols=slice(None)):
@@ -613,15 +643,6 @@
         tile = ref[j, :, :, :, cols]
         return tile.reshape(WIDTH, tile.shape[-1])
 
-    def project(tile, carry):
-        rows = pl.ds(pl.multiple_of(tile * ROWS, ROWS), ROWS)
-        first = first_ref[rows, :]
-        q_ref[rows, :] = mm(first, weight(qkv_ref, 0)).astype(bf16)
-        k_ref[rows, :] = mm(first, weight(qkv_ref, 1)).astype(bf16)
-        v_ref[rows, :] = mm(first, weight(qkv_ref, 2)).astype(bf16)
-        return carry
-
-    lax.fori_loop(0, TILES, project, 0)
     r, c = sorter_in.shape
 
     def sorter_places():
@@ -641,8 +662,10 @@
         for k in range(pack):
             sorter_ref[rows[k], cols] = tile[:, k * c : (k + 1) * c]
     logits = mm(means, sorter_ref[...])
-    each(middle_set, "landed")
-    each(middle_set, "stage", 2)
+    for tile in range(TILES):
+        rows = slice(tile * ROWS, (tile + 1) * ROWS)
+        k_ref[rows, :] = mm(first_ref[rows, :], weight(kv_ref, 0)).astype(bf16)
+        v_ref[rows, :] = mm(first_ref[rows, :], weight(kv_ref, 1)).astype(bf16)
 
     def store(index, value):
         sink_ref[index] = value
@@ -650,29 +673,44 @@
     logs, weights = sinkhorn(logits, allowed, group_matrix(), store)
     logs_ref[...] = logs
     probs = weights.astype(bf16)
+    gather_a.landed()
+    gather_a.stage(2)
+    gather_woq.landed()
+    gather_woq.stage(3)
+    gather_b.landed()
+    gather_b.stage(1)
     place_k_ref[...] = by_place(k_ref[...])
     place_v_ref[...] = by_place(v_ref[...])
     first_head = iota((SPAN, 2 * PAIR), 1) % PAIR < HEAD_DIM
 
-    def rearrange(matrices, keys, values, keys_out, values_out):
+    def rearrange(matrices, keys, values, finish_pair):
         for pair in range(HEADS // 2):
             lanes = slice(pair * PAIR, (pair + 1) * PAIR)
             one, two = matrices(2 * pair), matrices(2 * pair + 1)
+            outs = []
             for part in range(SEQ_LEN // SPAN):
                 rows = slice(part * SPAN, (part + 1) * SPAN)
                 both = jnp.concatenate([keys[rows, lanes], values[rows, lanes]], axis=1)
-                out = jnp.where(first_head, mm(one, both), mm(two, both))
-                keys_out[rows, lanes] = out[:, :PAIR].astype(keys_out.dtype)
-                values_out[rows, lanes] = out[:, PAIR:].astype(values_out.dtype)
+                outs.append(jnp.where(first_head, mm(one, both), mm(two, both)))
+            out = jnp.concatenate(outs, axis=0)
+            finish_pair(lanes, out[:, :PAIR], out[:, PAIR:])
 
     def forth(head):
         return repeated(probs[:, head * BLOCKS : (head + 1) * BLOCKS])
 
-    rearrange(forth, place_k_ref, place_v_ref, sk_ref, sv_ref)
-    sk_ref[...] = by_place(sk_ref[...])
-    sv_ref[...] = by_place(sv_ref[...])
-    each(late, "landed")
-    each(late, "stage", 1)
+    def keep_sorted(lanes, keys, values):
+        sk_ref[:, lanes] = by_place(keys.astype(bf16))
+        sv_ref[:, lanes] = by_place(values.astype(bf16))
+
+    rearrange(forth, place_k_ref, place_v_ref, keep_sorted)
+    gather_woq.landed()
+
+    def project_queries(tile, carry):
+        rows = pl.ds(pl.multiple_of(tile * ROWS, ROWS), ROWS)
+        q_ref[rows, :] = mm(first_ref[rows, :], weight(woq_ref, 1)).astype(bf16)
+        return carry
+
+    lax.fori_loop(0, TILES, project_queries, 0)
 
     def block_rows(block):
         return pl.ds(pl.multiple_of(block * BLOCK, BLOCK), BLOCK)
@@ -682,37 +720,34 @@
         lanes = slice(group * LANES, (group + 1) * LANES)
         keys = jnp.concatenate([k_ref[rows, lanes], sk_ref[rows, lanes]], axis=0)
         values = jnp.concatenate([v_ref[rows, lanes], sv_ref[rows, lanes]], axis=0)
-        return keys, values, by_pack(q_ref[rows, lanes])
+        return keys, values
 
     def attend(step, carry):
-        units = []
         for block in [step * UNROLL + k for k in range(UNROLL)]:
+            rows = block_rows(block)
             row = segrow_ref[pl.ds(block, 1), :]
             near = diagonal_column(row[:, :BLOCK], BLOCK) == row
             far = jnp.broadcast_to(row > 0, (BLOCK, PAIRS))
             mask = jnp.concatenate([near, far], axis=0)
-            units += [(block, group, mask, *operands(block, group)) for group in range(GROUPS)]
-        results = []
-        for block, group, mask, keys, values, queries in units:
-            scores = jnp.where(mask, mm(keys, queries, 1, 1) * (HEAD_DIM ** -0.5), excluded_fill)
-            shifted = jnp.exp(scores - jnp.max(scores, axis=0, keepdims=True))
-            attention = shifted * (1.0 / jnp.sum(shifted, axis=0, keepdims=True))
-            results.append((attention, own_heads(mm(attention.astype(bf16), values, 0, 0)).astype(bf16)))
-        for (block, group, *_), (attention, mixed) in zip(units, results):
-            att_ref[block, group] = attention
-            mixed_ref[block_rows(block), group * LANES : (group + 1) * LANES] = mixed
+            for group in range(GROUPS):
+                lanes = slice(group * LANES, (group + 1) * LANES)
+                keys, values = operands(block, group)
+                scores = mm(keys, by_pack(q_ref[rows, lanes]), 1, 1) * (HEAD_DIM ** -0.5)
+                scores = jnp.where(mask, scores, excluded_fill)
+                shifted = jnp.exp(scores - jnp.max(scores, axis=0, keepdims=True))
+                attention = shifted * (1.0 / jnp.sum(shifted, axis=0, keepdims=True))
+                att_ref[block, group] = attention
+                mixed_ref[rows, lanes] = own_heads(mm(attention.astype(bf16), values, 0, 0)).astype(bf16)
         return carry
 
     half = BLOCKS // UNROLL // 2
-    lax.fori_loop(0, half, attend, 0)
-    each(middle_set, "landed")
-    each(middle_set, "stage", 3)
-    each(late, "landed")
-    each(late, "stage", 2)
-    lax.fori_loop(half, 2 * half, attend, 0)
+    lax.fori_loop(0, 2 * half, attend, 0)
+    gather_a.landed()
+    gather_a.stage(3)
+    gather_b.landed()
+    gather_b.stage(2)
     fetch_cot.wait()
     gain_grad_ref[...] = jnp.zeros_like(gain_grad_ref)
-    each(middle_set, "landed")
 
     def keep(ref, j, cols, value):
         if len(ref.shape) == 6:
@@ -724,7 +759,7 @@
 
     def open_rows(tile, carry):
         rows = pl.ds(pl.multiple_of(tile * ROWS, ROWS), ROWS)
-        middle = x_ref[rows, :].astype(f32) + mm(mixed_ref[rows, :], weight(wo_ref, 0), 1, 1)
+        middle = x_ref[rows, :].astype(f32) + mm(mixed_ref[rows, :], weight(woq_ref, 0), 1, 1)
         grad_ref[rows, :] = middle
         normed, _ = normalize(middle)
         second_ref[rows, :] = (normed * gain_second).astype(bf16)
@@ -771,72 +806,72 @@
         lax.fori_loop(0, dfeed_ref.shape[-1] // WIDTH, run, 0)
 
     lax.fori_loop(0, TILES, open_rows, 0)
-    lax.fori_loop(0, TILES // 2, feed_a, 0)
-    each(late, "landed")
-    each(late, "stage", 3)
-    lax.fori_loop(TILES // 2, TILES, feed_a, 0)
+    gather_a.landed()
+    lax.fori_loop(0, TILES, feed_a, 0)
+    gather_b.landed()
+    gather_b.stage(3)
     feed_weights(dfeed_a_ref)
     scatter_a.stage(0)
-    each(late, "landed")
+    gather_b.landed()
     lax.fori_loop(0, TILES // 2, feed_b, 0)
     scatter_a.fold(0)
     scatter_a.stage(1)
     lax.fori_loop(TILES // 2, TILES, feed_b, 0)
     write_out = pltpu.make_async_copy(out_ref, out_hbm, copy_sems.at[2])
     write_out.start()
+    feed_weights(dfeed_b_ref)
+    scatter_b.stage(0)
+    keep(dwoq_ref, 0, slice(None), mm(grad_ref[...].astype(bf16), mixed_ref[...], 0, 0))
+
+    def start(tile, carry):
+        rows = pl.ds(pl.multiple_of(tile * ROWS, ROWS), ROWS)
+        mixed_ref[rows, :] = mm(grad_ref[rows, :].astype(bf16), weight(woq_ref, 0)).astype(bf16)
+        return carry
+
+    lax.fori_loop(0, TILES, start, 0)
     scatter_a.fold(1)
     scatter_a.stage(2)
-    feed_weights(dfeed_b_ref)
-    scatter_b.stage(0)
+    scatter_b.fold(0)
+    scatter_b.stage(1)
+
+    def attend_back(step, carry):
+        units = [(step * UNROLL + k, group) for k in range(UNROLL) for group in range(GROUPS)]
+
+        def mixed_pack(block, group):
+            return by_pack(mixed_ref[block_rows(block), group * LANES : (group + 1) * LANES])
+
+        for block, group in units:
+            rows, at = block_rows(block), group * LANES
+            keys, values = operands(block, group)
+            attention = att_ref[block, group]
+            prob_grad = mm(values, mixed_pack(block, group), 1, 1)
+            inner = jnp.sum(attention * prob_grad, axis=0, keepdims=True)
+            score_grad = (attention * (prob_grad - inner) * (HEAD_DIM ** -0.5)).astype(bf16)
+            pre_ref[rows, WIDTH + at : WIDTH + at + PAIRS] = score_grad[:BLOCK]
+            pre_ref[rows, WIDTH + at + PAIRS : WIDTH + at + 2 * PAIRS] = score_grad[BLOCK:]
+            pre_ref[rows, at : at + LANES] = own_heads(mm(score_grad, keys, 0, 0)).astype(bf16)
+        for block, group in units:
+            rows, at = block_rows(block), group * LANES
+            lanes = slice(at, at + LANES)
+            score_grad = jnp.concatenate(
+                [pre_ref[rows, WIDTH + at : WIDTH + at + PAIRS], pre_ref[rows, WIDTH + at + PAIRS : WIDTH + at + 2 * PAIRS]],
+                axis=0,
+            )
+            key_grad = mm(score_grad, by_pack(q_ref[rows, lanes]))
+            value_grad = mm(att_ref[block, group].astype(bf16), mixed_pack(block, group))
+            dk_ref[rows, lanes] = key_grad[:BLOCK]
+            dv_ref[rows, lanes] = value_grad[:BLOCK]
+            act_ref[rows, lanes] = key_grad[BLOCK:].astype(bf16)
+            act_ref[rows, WIDTH + at : WIDTH + at + LANES] = value_grad[BLOCK:].astype(bf16)
+        return carry
+
+    lax.fori_loop(0, 2 * half, attend_back, 0)
     scatter_a.fold(2)
     scatter_a.stage(3)
-    keep(dwoq_ref, 0, slice(None), mm(grad_ref[...].astype(bf16), mixed_ref[...], 0, 0))
-
-    def start(tile, carry):
-        rows = pl.ds(pl.multiple_of(tile * ROWS, ROWS), ROWS)
-        mixed_ref[rows, :] = mm(grad_ref[rows, :].astype(bf16), weight(wo_ref, 0)).astype(bf16)
-        return carry
-
-    lax.fori_loop(0, TILES, start, 0)
-    scatter_b.fold(0)
-    scatter_b.stage(1)
-
-    def attend_back(step, carry):
-        units = []
-        for block in [step * UNROLL + k for k in range(UNROLL)]:
-            for group in range(GROUPS):
-                mixed_grad = by_pack(mixed_ref[block_rows(block), group * LANES : (group + 1) * LANES])
-                units.append((block, group, mixed_grad, att_ref[block, group], *operands(block, group)))
-        results = []
-        for block, group, mixed_grad, attention, keys, values, queries in units:
-            prob_grad = mm(values, mixed_grad, 1, 1)
-            inner = jnp.sum(attention * prob_grad, axis=0, keepdims=True)
-            score_grad = (attention * (prob_grad - inner) * (HEAD_DIM ** -0.5)).astype(bf16)
-            results.append((
-                own_heads(mm(score_grad, keys, 0, 0)).astype(bf16),
-                mm(score_grad, queries),
-                mm(attention.astype(bf16), mixed_grad),
-            ))
-        for (block, group, *_), (query_grad, key_grad, value_grad) in zip(units, results):
-            rows = block_rows(block)
-            lanes = slice(group * LANES, (group + 1) * LANES)
-            q_ref[rows, lanes] = query_grad
-            dk_ref[rows, lanes] = key_grad[:BLOCK]
-            dv_ref[rows, lanes] = value_grad[:BLOCK]
-            sk_ref[rows, lanes] = key_grad[BLOCK:].astype(bf16)
-            sv_ref[rows, lanes] = value_grad[BLOCK:].astype(bf16)
-        return carry
-
-    lax.fori_loop(0, half, attend_back, 0)
-    scatter_a.fold(3)
-    scatter_b.fold(1)
-    scatter_b.stage(2)
-    lax.fori_loop(half, 2 * half, attend_back, 0)
     first = first_ref[...]
+    q_ref[...] = pre_ref[:, :WIDTH]
     keep(dwoq_ref, 1, slice(None), mm(first, q_ref[...], 0, 0))
     scatter_woq.stage(0)
-    scatter_b.fold(2)
-    scatter_b.stage(3)
     weights = sink_ref[2 * SINK_ITERS - 1]
     same_head = iota((LOGITS, LOGITS), 0) // BLOCKS == iota((LOGITS, LOGITS), 1) // BLOCKS
     turned = jnp.where(same_head, jnp.concatenate([weights] * HEADS, axis=0), 0.0).T
@@ -845,19 +880,21 @@
         rows = slice(head * BLOCKS, (head + 1) * BLOCKS)
         return repeated(turned[rows, rows].astype(bf16))
 
-    sk_ref[...] = by_place(sk_ref[...])
-    sv_ref[...] = by_place(sv_ref[...])
-    rearrange(back, sk_ref, sv_ref, pair_k_ref, pair_v_ref)
-    key_grad = (dk_ref[...] + by_place(pair_k_ref[...])).astype(bf16)
-    value_grad = (dv_ref[...] + by_place(pair_v_ref[...])).astype(bf16)
-    k_ref[...] = key_grad
-    v_ref[...] = value_grad
-    keep(dkv_ref, 0, slice(None), mm(first, key_grad, 0, 0))
-    keep(dkv_ref, 1, slice(None), mm(first, value_grad, 0, 0))
-    scatter_kv.stage(0)
+    sk_ref[...] = by_place(act_ref[:, :WIDTH])
+    sv_ref[...] = by_place(act_ref[:, WIDTH:])
+
+    def add_pair(lanes, keys, values):
+        k_ref[:, lanes] = (dk_ref[:, lanes] + by_place(keys)).astype(bf16)
+        v_ref[:, lanes] = (dv_ref[:, lanes] + by_place(values)).astype(bf16)
+
+    rearrange(back, sk_ref, sv_ref, add_pair)
+    scatter_b.fold(1)
+    scatter_b.stage(2)
     scatter_woq.fold(0)
     scatter_woq.stage(1)
-    scatter_b.fold(3)
+    keep(dkv_ref, 0, slice(None), mm(first, k_ref[...], 0, 0))
+    keep(dkv_ref, 1, slice(None), mm(first, v_ref[...], 0, 0))
+    scatter_kv.stage(0)
     lane_head = iota((SPAN, PAIR), 1) // HEAD_DIM
     diagonal = iota((SPAN, SPAN), 0) // BLOCKS == iota((SPAN, SPAN), 1) // BLOCKS
     folded = []
@@ -891,13 +928,9 @@
         pieces = [sorter_grad[rows[k], cols] for k in range(pack)]
         dsorter_full[index] = jnp.concatenate(pieces, axis=1) if pack > 1 else pieces[0]
     scatter_sorter.stage(0)
+    scatter_b.fold(2)
+    scatter_b.stage(3)
     spread_ref[...] = mm(logit_grad, sorter_ref[...], 1, 1) / BLOCK
-    scatter_woq.fold(1)
-    scatter_woq.stage(2)
-    scatter_kv.fold(1)
-    scatter_kv.stage(2)
-    scatter_sorter.fold(0)
-    scatter_sorter.stage(1)
     here = ROWS // BLOCK
 
     def finish(tile, carry):
@@ -905,9 +938,9 @@
         spread = spread_ref[pl.ds(pl.multiple_of(tile * here, here), here), :]
         spread = jnp.broadcast_to(spread[:, None, :], (here, BLOCK, WIDTH)).reshape(ROWS, WIDTH)
         first_grad = (
-            mm(q_ref[rows, :], weight(qkv_ref, 0), 1, 1)
-            + mm(k_ref[rows, :], weight(qkv_ref, 1), 1, 1)
-            + mm(v_ref[rows, :], weight(qkv_ref, 2), 1, 1)
+            mm(q_ref[rows, :], weight(woq_ref, 1), 1, 1)
+            + mm(k_ref[rows, :], weight(kv_ref, 0), 1, 1)
+            + mm(v_ref[rows, :], weight(kv_ref, 1), 1, 1)
             + spread
         )
         normed, inverse = normalize(x_ref[rows, :].astype(f32))
@@ -925,12 +958,10 @@
 
     lax.fori_loop(0, TILES // 2, finish, 0)
     write_rows(0)
-    scatter_woq.fold(2)
-    scatter_woq.stage(3)
-    scatter_kv.fold(2)
-    scatter_kv.stage(3)
-    scatter_sorter.fold(1)
-    scatter_sorter.stage(2)
+    scatter_woq.fold(1)
+    scatter_woq.stage(2)
+    scatter_sorter.fold(0)
+    scatter_sorter.stage(1)
     lax.fori_loop(TILES // 2, TILES, finish, 0)
     write_rows(1)
     entropy = -jnp.sum(jnp.where(real_col > 0, weights * logs, 0.0), axis=0, keepdims=True)
@@ -940,38 +971,50 @@
         spread_rows(jnp.sum(gain_grad_ref[8:16, :], axis=0, keepdims=True)),
         entropy,
     ], axis=0))
+    scatter_kv.fold(1)
+    scatter_kv.stage(2)
+    scatter_woq.fold(2)
+    scatter_woq.stage(3)
+    scatter_sorter.fold(1)
+    scatter_sorter.stage(2)
+    total_b.over_dp()
+    scatter_kv.fold(2)
+    scatter_kv.stage(3)
     scatter_sorter.fold(2)
     scatter_sorter.stage(3)
-    total_b.over_dp()
-    scatter_woq.fold(3)
-    scatter_kv.fold(3)
-    scatter_sorter.fold(3)
+    scatter_a.fold(3)
+    write_sums[0].start()
+    scatter_b.fold(3)
+    write_sums[1].start()
     small_out[0:16, :] = total_b.result()
     small_out[16:24, :] = summed[8:16]
+    write_sums[5].start()
+    scatter_woq.fold(3)
+    write_sums[2].start()
     write_out.wait()
     for copy in writes:
         copy.wait()
-    each(tuple(gather) + tuple(scatters) + (total_a, total_b), "close")
-
-
-def update_kernel(
-    lay, step_ref, out_in, grad_in, feed_a, feed_b, woq, kv, sorter, sums, *refs
-):
-    masters, results = refs[:12], refs[12:27]
-    out_rows, grad_rows, sem = refs[27:]
-    block_out, token_out, penalty_out = results[:3]
-    moves = []
-    for part in range(2):
-        rows = slice(part * SEQ_LEN // 2, (part + 1) * SEQ_LEN // 2)
-        for which, (source, middle, target) in enumerate(
-            ((out_in, out_rows, block_out), (grad_in, grad_rows, token_out))
-        ):
-            moves.append((
-                pltpu.make_async_copy(source.at[rows], middle.at[rows], sem.at[part, which, 0]),
-                pltpu.make_async_copy(middle.at[rows], target.at[rows], sem.at[part, which, 1]),
-            ))
-    for bring, _ in moves:
-        bring.start()
+    each(tuple(gather) + (scatter_a, scatter_b, total_a, total_b), "close")
+    scatter_kv.fold(3)
+    write_sums[3].start()
+    scatter_sorter.fold(3)
+    write_sums[4].start()
+    each((scatter_woq, scatter_kv, scatter_sorter), "close")
+    for copy in write_sums:
+        copy.wait()
+
+
+def update_kernel(lay, step_ref, *refs):
+    sources, targets, penalty_out, inputs, results = refs[:20], refs[20:34], refs[34], refs[35:55], refs[55:67]
+    in_sems, out_sems = refs[67:]
+    bring = [pltpu.make_async_copy(source, inputs[k], in_sems.at[k]) for k, source in enumerate(sources)]
+    begin(bring[2:] + bring[:2])
+    send = [
+        pltpu.make_async_copy(buffer, targets[k], out_sems.at[k])
+        for k, buffer in enumerate(tuple(inputs[:2]) + tuple(results))
+    ]
+    feed_a, feed_b, woq, kv, sorter, sums = inputs[2:8]
+    masters = inputs[8:]
     step_value = jnp.full((1, 128), step_ref[0], jnp.int32).astype(f32)
     scale_first = 1.0 / (1.0 - jnp.exp(step_value * math.log(beta_first)))[:, 0:1]
     scale_second = 1.0 / (1.0 - jnp.exp(step_value * math.log(beta_second)))[:, 0:1]
@@ -981,33 +1024,39 @@
         moment_new = beta_first * moment + (1.0 - beta_first) * grad
         second_new = beta_second * second + (1.0 - beta_second) * grad * grad
         change = (moment_new * scale_first) / (jnp.sqrt(second_new * scale_second) + adam_eps)
-        outs = results[3 + 3 * which : 6 + 3 * which]
+        outs = results[3 * which : 3 * which + 3]
         outs[0][index] = moment_new
         outs[1][index] = second_new
         outs[2][index] = master - rate * (change + weight_decay * master)
 
-    for j, grad in enumerate((woq[1], kv[0], kv[1], woq[0])):
-        adamw(0, (ALLR, j, ALLR), grad, rate_mixer)
-    for bring, send in moves:
-        bring.wait()
-        send.start()
+    for copy in bring[2:]:
+        copy.wait()
     half = feed_a.shape[2]
     for j in range(2):
         adamw(1, (ALLR, j, slice(0, half)), feed_a[j], rate_feed)
         adamw(1, (ALLR, j, slice(half, 2 * half)), feed_b[j], rate_feed)
+    begin(send[5:8])
+    for copy in bring[:2]:
+        copy.wait()
+    begin(send[:2])
+    for j, grad in enumerate((woq[1], kv[0], kv[1], woq[0])):
+        adamw(0, (ALLR, j, ALLR), grad, rate_mixer)
+    begin(send[2:5])
     r, c = masters[6].shape
     pack = packing(r, c)
     deep = r // pack
     grad = jnp.concatenate([sorter[0][:, k * c : (k + 1) * c] for k in range(pack)], axis=0) if pack > 1 else sorter[0]
     adamw(2, (ALLR, ALLR), grad, rate_sorter)
+    begin(send[8:11])
     rows = jnp.concatenate([joined_row(sums[0:4, :]), joined_row(sums[4:8, :])], axis=0)
     own = spot(masters[9].shape[1])
     grad = sum(mm(part, own, 1, 1) for part in three_parts(rows))
     adamw(3, (ALLR, ALLR), grad, rate_gains)
+    begin(send[11:14])
     entropy = jnp.sum(sums[8:9, :], axis=1, keepdims=True)
     penalty_out[...] = jnp.broadcast_to(entropy / (sums[16:17, 0:1] * HEADS), (1, 128))
-    for _, send in moves:
-        send.wait()
+    for copy in send:
+        copy.wait()
 
 
 def shape(dims, dtype):
@@ -1023,7 +1072,7 @@
     pack = packing(*sorter.shape)
     sorter_item = Item(lay, 1, sorter.shape[0] // pack, sorter.shape[1] * pack)
     feed_item, pair_item = Item(lay, 2, r, half), Item(lay, 2, r, c)
-    gathers = (Item(lay, 3, r, c), sorter_item, Item(lay, 1, r, c), feed_item, feed_item)
+    gathers = (pair_item, sorter_item, pair_item, feed_item, feed_item)
     scatters = (feed_item, feed_item, pair_item, pair_item, sorter_item)
     vm = pltpu.VMEM
     count = 5 * (Gather.count(lay) + Scatter.count(lay)) + 2 * Total.count(lay)
@@ -1039,10 +1088,13 @@
             vm((BLOCKS, PAIRS), f32), vm((BLOCKS, WIDTH), f32), vm((16, WIDTH), f32),
             vm(TOK, bf16), vm((SEQ_LEN, HIDDEN // 2), bf16), vm((SEQ_LEN, HIDDEN // 2), bf16),
         ]
-        + [vm(TOK, f32)] * 4
+        + [vm(TOK, f32)] * 2
         + [vm((lay.mp, 16, 128), f32), vm((lay.dp, 16, 128), f32)] * 2
         + [pltpu.SemaphoreType.DMA((count,))] * 2
-        + [pltpu.SemaphoreType.DMA((5,))]
+        + [pltpu.SemaphoreType.DMA((14,))]
+        + [vm(mixer.shape, f32), vm(feed.shape, f32), vm(sorter.shape, f32)]
+        + [vm(item.shard(), f32) for item in scatters]
+        + [vm((24, 128), f32)]
     )
     for item in scatters:
         scratch += Scatter.buffers(item)
@@ -1053,8 +1105,8 @@
         out_shape=[shape(TOK, bf16), shape(TOK, f32)]
         + [shape(item.shard(), f32) for item in scatters]
         + [shape((24, 128), f32)],
-        in_specs=[outside] * 2 + [inside] * 5,
-        out_specs=[outside] * 2 + [inside] * 6,
+        in_specs=[outside] * 2 + [inside] * 2 + [outside] * 3,
+        out_specs=[outside] * 8,
         scratch_shapes=scratch,
         compiler_params=pltpu.CompilerParams(collective_id=0, has_side_effects=True, vmem_limit_bytes=LIMIT),
         name="step",
@@ -1062,18 +1114,21 @@
 
 
 def run_update(lay, step_count, block_output, token_grad, sums, states):
-    inside = pl.BlockSpec(memory_space=pltpu.VMEM)
     outside = pl.BlockSpec(memory_space=pl.ANY)
-    outs = [shape(TOK, bf16), shape(TOK, f32), shape((1, 128), f32)] + [shape(state.shape, f32) for state in states]
-    return pl.pallas_call(
+    arrays = (block_output, token_grad, *sums, *states)
+    moved = [shape(array.shape, array.dtype) for array in (block_output, token_grad, *states)]
+    *moved, penalty = pl.pallas_call(
         functools.partial(update_kernel, lay),
-        out_shape=outs,
-        in_specs=[pl.BlockSpec(memory_space=pltpu.SMEM)] + [outside] * 2 + [inside] * 18,
-        out_specs=[outside] * 2 + [inside] * 13,
-        scratch_shapes=[pltpu.VMEM(TOK, bf16), pltpu.VMEM(TOK, f32), pltpu.SemaphoreType.DMA((2, 2, 2))],
+        out_shape=moved + [shape((1, 128), f32)],
+        in_specs=[pl.BlockSpec(memory_space=pltpu.SMEM)] + [outside] * len(arrays),
+        out_specs=[outside] * len(moved) + [pl.BlockSpec(memory_space=pltpu.VMEM)],
+        scratch_shapes=[pltpu.VMEM(array.shape, array.dtype) for array in arrays]
+        + [pltpu.VMEM(state.shape, f32) for state in states]
+        + [pltpu.SemaphoreType.DMA((len(arrays),)), pltpu.SemaphoreType.DMA((len(moved),))],
         compiler_params=pltpu.CompilerParams(vmem_limit_bytes=LIMIT),
         name="update",
-    )(step_count, block_output, token_grad, *sums, *states)
+    )(step_count, *arrays)
+    return moved[0], moved[1], penalty, moved[2:]
 
 
 rate_mixer = 0.2
@@ -1113,7 +1168,7 @@
         mixer_weights, mixer_moment, mixer_second, feed_weights, feed_moment, feed_second,
         sorter_weights, sorter_moment, sorter_second, norm_gains, gain_moment, gain_second,
     )
-    block_output, token_grad, penalty, *states = run_update(lay, step_count, block_output, token_grad, sums, states)
+    block_output, token_grad, penalty, states = run_update(lay, step_count, block_output, token_grad, sums, states)
     return (block_output, token_grad, penalty[0, :1], *states)
 
 

time: 126 us -> 102 us (0.81)
  Pallas kernels: 124 us -> 101 us
    pallas_call x1, Pallas kernels: 118 us -> 95.2 us  [run_step(): pl.pallas_call(functools.partial(step_kernel, lay, gathers, scatters, tot...]
where the time goes in v3:
time: 102 us
  Pallas kernels  101 us (99%)
  between operations  1.48 us (1%)
    pallas_call x1, Pallas kernels, run_step(): pl.pallas_call(functools.partial(step_kernel, lay, gathers, scatters, tot...  95.2 us
    pallas_call x1, Pallas kernels, run_update(): pl.pallas_call(functools.partial(update_kernel, lay), out_shape=moved + [...  5.3 us

profile of v3, /device:TPU:0, one launch (start us, length us, event | category | flops | bytes accessed | tf_op | source)
XLA Modules:
  0.0 102.0 jit_solution(3044921813021158787)
XLA Ops:
  1.3 95.2 %step.1 = (bf16[1024,512]{1,0:T(8,128)(2,1)}, f32[1024,512]{1,0:T(8,128)}, f32[2,64,256]{2,1,0:T(8,128)}, f32[2,64,256]{2,1,0:T(8,128)}, f32[2,64,128]{2,1,0:T(8...) custom-call(bf16[1024,512]{1,0:T(8,128)(2,1)} %tokens_ref.1, ...), custom_call_target="tpu_custom_call" | custom-call | tf_op jit(solution)/shard_map/step/pallas_call | solution.py:1103
  96.5 5.3 %update.1 = (bf16[1024,512]{1,0:T(8,128)(2,1)}, f32[1024,512]{1,0:T(8,128)}, f32[64,4,128]{2,1,0:T(4,128)}, f32[64,4,128]{2,1,0:T(4,128)}, f32[64,4,128]{2,1,0:T...) custom-call(s32[1]{0:T(128)S(6)} %copy.31.step_ref, ...), custom_call_target="tpu_custom_call" | custom-call | tf_op jit(solution)/shard_map/update/pallas_call | solution.py:1120

commit v4 on v3

--- a/solution.py
+++ b/solution.py
@@ -23,7 +23,8 @@
 LANES = PACK * HEAD_DIM
 PAIRS = PACK * BLOCK
 PAIR = 2 * HEAD_DIM
-UNROLL = 8
+UNROLL = 32
+ROW_PARTS = 2
 
 norm_eps = 1e-05
 softness_factor = 0.75
@@ -180,11 +181,11 @@
     def full(self):
         return self.dims(self.lay.H, self.lay.L)
 
-    def at(self, lead, m, rows=slice(None)):
+    def at(self, lead, first, count=1, rows=slice(None)):
         if self.direct:
-            cols = slice(None) if m is None else pl.ds(pl.multiple_of(m * self.c, 128), self.c)
-            return (slice(None), *lead, rows, cols)
-        return (slice(None), *lead, slice(None) if m is None else m, rows, slice(None))
+            start = first * self.c if isinstance(first, int) else pl.multiple_of(first * self.c, 128)
+            return (slice(None), *lead, rows, pl.ds(start, count * self.c))
+        return (slice(None), *lead, first if count == 1 else pl.ds(first, count), rows, slice(None))
 
     def rows_a(self):
         return slice(0, self.half)
@@ -198,19 +199,38 @@
 
 class Sems:
     def __init__(self, send, recv):
-        self.send, self.recv, self.used = send, recv, 0
-
-    def copy(self, src, dst, device):
-        index = self.used
-        self.used += 1
-        return pltpu.make_async_remote_copy(
-            src_ref=src,
-            dst_ref=dst,
-            send_sem=self.send.at[index],
-            recv_sem=self.recv.at[index],
-            device_id=device,
-            device_id_type=MESH,
-        )
+        self.send, self.recv = send, recv
+        self.sends, self.recvs = 0, 0
+
+    def lane(self, count):
+        return Lane(self, count)
+
+
+class Lane:
+    def __init__(self, sems, count):
+        self.sems, self.first, self.waiting = sems, sems.sends, []
+        sems.sends += count
+
+    def send(self, copies):
+        self.close()
+        for k, (src, dst, device) in enumerate(copies):
+            self.waiting.append(
+                pltpu.make_async_remote_copy(
+                    src_ref=src,
+                    dst_ref=dst,
+                    send_sem=self.sems.send.at[self.first + k],
+                    recv_sem=self.sems.recv.at[self.sems.recvs + k],
+                    device_id=device,
+                    device_id_type=MESH,
+                )
+            )
+        self.sems.recvs += len(copies)
+        return begin(list(self.waiting))
+
+    def close(self):
+        for copy in self.waiting:
+            copy.wait_send()
+        self.waiting = []
 
 
 def begin(copies):
@@ -225,66 +245,75 @@
 
 
 class Gather:
-    def __init__(self, item, shard, full, sems):
-        self.item, self.shard, self.full, self.sems = item, shard, full, sems
-        self.sent = []
+    def __init__(self, item, shard, full, sems, high_first=True):
+        self.item, self.shard, self.full, self.high_first = item, shard, full, high_first
+        self.lane = sems.lane(self.sends(item.lay))
 
     def stage(self, number):
         item, lay, full = self.item, self.item.lay, self.full
         h, l, x, c = lay.here()
-        mp = x * lay.C + c
         copies = []
 
         def to(hh, ll, xx, cc):
             return (hh * lay.L + ll, xx * lay.C + cc)
 
         def same(index, device):
-            copies.append(self.sems.copy(full.at[index], full.at[index], device))
-
-        if number == 0:
+            copies.append((full.at[index], full.at[index], device))
+
+        mine = c * lay.X + x
+        if number == 0 and not self.high_first:
+            for rows, index, devices in (
+                (item.rows_a(), item.at((h, l), mine, 1, item.rows_a()), [to(h, (l + k) % lay.L, x, c) for k in range(1, lay.L)]),
+                (item.rows_b(), item.at((h, l), mine, 1, item.rows_b()), [to(h, l, (x + k) % lay.X, c) for k in range(1, lay.X)]),
+            ):
+                copies += [(self.shard.at[:, rows], full.at[index], device) for device in devices]
+        if number == 1 and not self.high_first:
             for k in range(1, lay.H):
-                copies.append(
-                    self.sems.copy(self.shard, full.at[item.at((h, l), mp)], to((h + k) % lay.H, l, x, c))
-                )
-        if number == 1:
+                device = to((h + k) % lay.H, l, x, c)
+                same(item.at((h, ALLR), mine, 1, item.rows_a()), device)
+                same(item.at((h, l), c * lay.X, lay.X, item.rows_b()), device)
+        if number == 0 and self.high_first:
+            for k in range(1, lay.H):
+                copies.append((self.shard, full.at[item.at((h, l), mine)], to((h + k) % lay.H, l, x, c)))
+        if number == 1 and self.high_first:
             for k in range(1, lay.L):
-                same(item.at((ALLR, l), mp, item.rows_a()), to(h, (l + k) % lay.L, x, c))
+                same(item.at((ALLR, l), mine, 1, item.rows_a()), to(h, (l + k) % lay.L, x, c))
             for k in range(1, lay.X):
-                same(item.at((ALLR, l), mp, item.rows_b()), to(h, l, (x + k) % lay.X, c))
+                same(item.at((ALLR, l), mine, 1, item.rows_b()), to(h, l, (x + k) % lay.X, c))
         if number == 2:
             for k in range(1, lay.X):
-                same(item.at((ALLR, ALLR), mp, item.rows_a()), to(h, l, (x + k) % lay.X, c))
+                same(item.at((ALLR, ALLR), mine, 1, item.rows_a()), to(h, l, (x + k) % lay.X, c))
             for k in range(1, lay.L):
-                for part in range(lay.X):
-                    same(item.at((ALLR, l), part * lay.C + c, item.rows_b()), to(h, (l + k) % lay.L, x, c))
+                same(item.at((ALLR, l), c * lay.X, lay.X, item.rows_b()), to(h, (l + k) % lay.L, x, c))
         if number == 3:
             for k in range(1, lay.C):
-                for part in range(lay.X):
-                    same(item.at((ALLR, ALLR), part * lay.C + c), to(h, l, x, (c + k) % lay.C))
-        self.sent += begin(copies)
-        self.flying = copies
+                same(item.at((ALLR, ALLR), c * lay.X, lay.X), to(h, l, x, (c + k) % lay.C))
+        self.flying = self.lane.send(copies)
 
     def place(self):
         h, l, x, c = self.item.lay.here()
-        self.full[self.item.at((h, l), x * self.item.lay.C + c)] = self.shard[...]
+        self.full[self.item.at((h, l), c * self.item.lay.X + x)] = self.shard[...]
 
     def landed(self):
         arrive(self.flying)
 
     def close(self):
-        for copy in self.sent:
-            copy.wait_send()
+        self.lane.close()
+
+    @staticmethod
+    def sends(lay):
+        return max(2 * (lay.H - 1), lay.L + lay.X - 2, lay.C - 1)
 
     @staticmethod
     def count(lay):
-        return (lay.H - 1) + (lay.L - 1) + (lay.X - 1) * 2 + (lay.L - 1) * lay.X + (lay.C - 1) * lay.X
+        return 2 * (lay.H - 1) + 2 * (lay.L + lay.X - 2) + (lay.C - 1)
 
 
 class Scatter:
-    def __init__(self, item, full, buffers, out, sems):
-        self.item, self.full, self.out, self.sems = item, full, out, sems
+    def __init__(self, item, full, buffers, write, sems):
+        self.item, self.full, self.write = item, full, write
+        self.lane = sems.lane(self.sends(item.lay))
         self.core, self.one_a, self.one_b, self.two_a, self.two_b, self.top_a, self.top_b = buffers
-        self.sent = []
 
     @staticmethod
     def buffers(item):
@@ -309,30 +338,29 @@
             return (hh * lay.L + ll, xx * lay.C + cc)
 
         def send(src, src_index, dst, dst_index, device):
-            copies.append(self.sems.copy(src.at[src_index], dst.at[dst_index], device))
+            copies.append((src.at[src_index], dst.at[dst_index], device))
 
         if number == 0:
             for k in range(1, lay.C):
                 cc = (c + k) % lay.C
-                for part in range(lay.X):
-                    send(
-                        self.full, item.at((ALLR, ALLR), part * lay.C + cc),
-                        self.core, (k - 1, *item.at((ALLR, ALLR), part)),
-                        to(h, l, x, cc),
-                    )
+                send(
+                    self.full, item.at((ALLR, ALLR), cc * lay.X, lay.X),
+                    self.core, (k - 1, *item.at((ALLR, ALLR), 0, lay.X)),
+                    to(h, l, x, cc),
+                )
         if number == 1:
             for k in range(1, lay.X):
                 xx = (x + k) % lay.X
                 send(
-                    self.core, (0, *item.at((ALLR, ALLR), xx, item.rows_a())),
+                    self.core, (0, *item.at((ALLR, ALLR), xx, 1, item.rows_a())),
                     self.one_a, (k - 1, *item.at((ALLR, ALLR), 0)),
                     to(h, l, xx, c),
                 )
             for k in range(1, lay.L):
                 ll = (l + k) % lay.L
                 send(
-                    self.core, (0, *item.at((ALLR, ll), None, item.rows_b())),
-                    self.one_b, (k - 1, *item.at((ALLR,), None)),
+                    self.core, (0, *item.at((ALLR, ll), 0, lay.X, item.rows_b())),
+                    self.one_b, (k - 1, *item.at((ALLR,), 0, lay.X)),
                     to(h, ll, x, c),
                 )
         if number == 2:
@@ -355,8 +383,7 @@
                 hh = (h + k) % lay.H
                 for src, dst in ((self.two_a, self.top_a), (self.two_b, self.top_b)):
                     send(src, (0, *item.at((hh,), 0)), dst, (k - 1, *item.at((), 0)), to(hh, l, x, c))
-        self.sent += begin(copies)
-        self.flying = copies
+        self.flying = self.lane.send(copies)
 
     def fold(self, number):
         item, lay = self.item, self.item.lay
@@ -380,11 +407,10 @@
 
             def core(high):
                 for low in range(lay.L):
-                    for part in range(lay.X):
-                        add(
-                            self.core, item.at((high, low), part),
-                            self.full, item.at((high, low), part * lay.C + c), lay.C - 1,
-                        )
+                    add(
+                        self.core, item.at((high, low), 0, lay.X),
+                        self.full, item.at((high, low), c * lay.X, lay.X), lay.C - 1,
+                    )
 
             over_high(core)
         if number == 1:
@@ -393,11 +419,11 @@
                 for low in range(lay.L):
                     add(
                         self.one_a, item.at((high, low), 0),
-                        self.core, (0, *item.at((high, low), x, item.rows_a())), lay.X - 1,
+                        self.core, (0, *item.at((high, low), x, 1, item.rows_a())), lay.X - 1,
                     )
                 add(
-                    self.one_b, item.at((high,), None),
-                    self.core, (0, *item.at((high, l), None, item.rows_b())), lay.L - 1,
+                    self.one_b, item.at((high,), 0, lay.X),
+                    self.core, (0, *item.at((high, l), 0, lay.X, item.rows_b())), lay.L - 1,
                 )
 
             over_high(one)
@@ -415,30 +441,33 @@
                 total = mine[(0, *item.at((h,), 0))].astype(f32)
                 for other in range(lay.H - 1):
                     total = total + others[(other, *item.at((), 0))].astype(f32)
-                self.out[:, rows, :] = total
+                total = total.reshape(item.J, item.half, item.c)
+                for j in range(item.J):
+                    self.write(j, rows, total[j])
 
     def close(self):
-        for copy in self.sent:
-            copy.wait_send()
+        self.lane.close()
+
+    @staticmethod
+    def sends(lay):
+        return max(lay.C - 1, lay.X + lay.L - 2, 2 * (lay.H - 1))
 
     @staticmethod
     def count(lay):
-        return (lay.C - 1) * lay.X + (lay.X - 1) * 2 + (lay.L - 1) * 2 + (lay.H - 1) * 2
+        return (lay.C - 1) + 2 * (lay.X + lay.L - 2) + 2 * (lay.H - 1)
 
 
 class Total:
     def __init__(self, lay, near, far, sems):
-        self.lay, self.near, self.far, self.sems = lay, near, far, sems
-        self.sent = []
+        self.lay, self.near, self.far = lay, near, far
+        self.lane = sems.lane(self.sends(lay))
 
     def over_mp(self, value):
         dp, mp = lax.axis_index("dp"), lax.axis_index("mp")
         self.near[mp] = value
-        self.flying = begin([
-            self.sems.copy(self.near.at[mp], self.near.at[mp], (dp, (mp + k) % self.lay.mp))
-            for k in range(1, self.lay.mp)
+        self.flying = self.lane.send([
+            (self.near.at[mp], self.near.at[mp], (dp, (mp + k) % self.lay.mp)) for k in range(1, self.lay.mp)
         ])
-        self.sent += self.flying
 
     def over_dp(self):
         dp, mp = lax.axis_index("dp"), lax.axis_index("mp")
@@ -447,11 +476,9 @@
         for other in range(1, self.lay.mp):
             total = total + self.near[other]
         self.far[dp] = total
-        self.flying = begin([
-            self.sems.copy(self.far.at[dp], self.far.at[dp], ((dp + k) % self.lay.dp, mp))
-            for k in range(1, self.lay.dp)
+        self.flying = self.lane.send([
+            (self.far.at[dp], self.far.at[dp], ((dp + k) % self.lay.dp, mp)) for k in range(1, self.lay.dp)
         ])
-        self.sent += self.flying
 
     def result(self):
         arrive(self.flying)
@@ -461,8 +488,11 @@
         return total
 
     def close(self):
-        for copy in self.sent:
-            copy.wait_send()
+        self.lane.close()
+
+    @staticmethod
+    def sends(lay):
+        return max(lay.mp, lay.dp) - 1
 
     @staticmethod
     def count(lay):
@@ -509,7 +539,7 @@
     tokens_ref, cotangent_ref, segment_ref, gains_in, mixer_hbm, feed_hbm, sorter_hbm,
     out_hbm, grad_hbm, *refs,
 ):
-    sums_hbm, scratch = refs[:6], list(refs[6:])
+    sums_hbm, scratch = refs[:4], list(refs[4:])
 
     def pop(count):
         taken = scratch[:count]
@@ -542,13 +572,47 @@
     fetch_cot.start()
     mp = lax.axis_index("mp")
     greet(lay)
-    gather = [Gather(item, shard, full, sems) for item, shard, full in zip(gathers, shards, weights_full)]
+    gather = [
+        Gather(item, shard, full, sems, k < 4)
+        for k, (item, shard, full) in enumerate(zip(gathers, shards, weights_full))
+    ]
     early = tuple(gather[:2])
     gather_woq, gather_a, gather_b = gather[2:]
     scatters = []
-    *outs, small_out = sums = pop(6)
-    for item, full, out in zip(scatter_items, grads_full, outs):
-        scatters.append(Scatter(item, full, pop(7), out, sems))
+    feed_sum, mixer_sum, sorter_sum, small_out = sums = pop(4)
+    pack = packing(*sorter_sum.shape)
+
+    def write_to(out, places, lane, lanes):
+        def write(j, rows, value):
+            place = places[j]
+            if len(out.shape) == 3:
+                out[rows, place, lane : lane + lanes] = value
+                return
+            tiles = feed_tiles if out is feed_sum else lanes // 128
+            group = len(mixer_order) if out is mixer_sum else 2
+            for tile in range(lanes // 128):
+                start = rows.start * tiles * group + (lane // 128 + tile) * group + place
+                out[pl.ds(start, rows.stop - rows.start, stride=tiles * group), :] = value[:, tile * 128 : (tile + 1) * 128]
+
+        return write
+
+    def write_sorter(j, rows, value):
+        deep, c = sorter_sum.shape[0] // pack, sorter_sum.shape[1]
+        for k in range(pack):
+            sorter_sum[k * deep + rows.start : k * deep + rows.stop, :] = value[:, k * c : (k + 1) * c]
+
+    mixer_order = (3, 0, 1, 2)
+    half_width = scatter_items[0].c
+    feed_tiles = 2 * half_width // 128
+    writers = (
+        write_to(feed_sum, (0, 1), 0, half_width),
+        write_to(feed_sum, (0, 1), half_width, half_width),
+        write_to(mixer_sum, mixer_order[:2], 0, scatter_items[2].c),
+        write_to(mixer_sum, mixer_order[2:], 0, scatter_items[2].c),
+        write_sorter,
+    )
+    for item, full, write in zip(scatter_items, grads_full, writers):
+        scatters.append(Scatter(item, full, pop(7), write, sems))
     write_sums = [
         pltpu.make_async_copy(buffer, target, copy_sems.at[8 + k])
         for k, (buffer, target) in enumerate(zip(sums, sums_hbm))
@@ -579,13 +643,11 @@
         fetch.wait()
     for j, source in enumerate((1, 2)):
         shards[0][j] = mixer_in[:, source, :].astype(bf16)
-    pack = packing(*sorter_in.shape)
     deep = sorter_in.shape[0] // pack
     sorter_shard = sorter_in[...].astype(bf16)
     shards[1][0] = jnp.concatenate([sorter_shard[k * deep : (k + 1) * deep] for k in range(pack)], axis=1)
     for j, source in enumerate((3, 0)):
         shards[2][j] = mixer_in[:, source, :].astype(bf16)
-    half_width = feed_in.shape[2] // 2
     for j in range(2):
         shards[3][j] = feed_in[:, j, :half_width].astype(bf16)
         shards[4][j] = feed_in[:, j, half_width:].astype(bf16)
@@ -597,6 +659,7 @@
     each(early, "stage", 0)
     total_a.over_mp(small)
     gather_woq.stage(0)
+    gather_b.stage(0)
     fetch_x.wait()
 
     def norm_rows(tile, carry):
@@ -627,13 +690,14 @@
     member = (iota((BLOCKS, SEQ_LEN), 0) == iota((BLOCKS, SEQ_LEN), 1) // BLOCK).astype(bf16)
     means = (mm(member, first_ref[...]) / BLOCK).astype(bf16)
     means_ref[...] = means
-    gather_b.stage(0)
     each(early, "landed")
     each(early, "stage", 3)
+    gather_woq.landed()
+    gather_woq.stage(2)
     gather_a.landed()
     gather_a.stage(1)
-    gather_woq.landed()
-    gather_woq.stage(2)
+    gather_b.landed()
+    gather_b.stage(1)
     each(early, "landed")
 
     def weight(ref, j, cols=slice(None)):
@@ -667,6 +731,9 @@
         k_ref[rows, :] = mm(first_ref[rows, :], weight(kv_ref, 0)).astype(bf16)
         v_ref[rows, :] = mm(first_ref[rows, :], weight(kv_ref, 1)).astype(bf16)
 
+    place_k_ref[...] = by_place(k_ref[...])
+    place_v_ref[...] = by_place(v_ref[...])
+
     def store(index, value):
         sink_ref[index] = value
 
@@ -677,10 +744,6 @@
     gather_a.stage(2)
     gather_woq.landed()
     gather_woq.stage(3)
-    gather_b.landed()
-    gather_b.stage(1)
-    place_k_ref[...] = by_place(k_ref[...])
-    place_v_ref[...] = by_place(v_ref[...])
     first_head = iota((SPAN, 2 * PAIR), 1) % PAIR < HEAD_DIM
 
     def rearrange(matrices, keys, values, finish_pair):
@@ -740,8 +803,8 @@
                 mixed_ref[rows, lanes] = own_heads(mm(attention.astype(bf16), values, 0, 0)).astype(bf16)
         return carry
 
-    half = BLOCKS // UNROLL // 2
-    lax.fori_loop(0, 2 * half, attend, 0)
+    steps = BLOCKS // UNROLL
+    lax.fori_loop(0, steps, attend, 0)
     gather_a.landed()
     gather_a.stage(3)
     gather_b.landed()
@@ -797,13 +860,8 @@
         return carry
 
     def feed_weights(dfeed_ref):
-        def run(part, carry):
-            cols = pl.ds(pl.multiple_of(part * WIDTH, WIDTH), WIDTH)
-            keep(dfeed_ref, 0, cols, mm(second_ref[...], pre_ref[:, cols], 0, 0))
-            keep(dfeed_ref, 1, cols, mm(cot_ref[...], act_ref[:, cols], 0, 0))
-            return carry
-
-        lax.fori_loop(0, dfeed_ref.shape[-1] // WIDTH, run, 0)
+        keep(dfeed_ref, 0, slice(None), mm(second_ref[...], pre_ref[...], 0, 0))
+        keep(dfeed_ref, 1, slice(None), mm(cot_ref[...], act_ref[...], 0, 0))
 
     lax.fori_loop(0, TILES, open_rows, 0)
     gather_a.landed()
@@ -865,7 +923,7 @@
             act_ref[rows, WIDTH + at : WIDTH + at + LANES] = value_grad[BLOCK:].astype(bf16)
         return carry
 
-    lax.fori_loop(0, 2 * half, attend_back, 0)
+    lax.fori_loop(0, steps, attend_back, 0)
     scatter_a.fold(2)
     scatter_a.stage(3)
     first = first_ref[...]
@@ -892,8 +950,9 @@
     scatter_b.stage(2)
     scatter_woq.fold(0)
     scatter_woq.stage(1)
-    keep(dkv_ref, 0, slice(None), mm(first, k_ref[...], 0, 0))
-    keep(dkv_ref, 1, slice(None), mm(first, v_ref[...], 0, 0))
+    dkv = mm(first, jnp.concatenate([k_ref[...], v_ref[...]], axis=1), 0, 0)
+    keep(dkv_ref, 0, slice(None), dkv[:, :WIDTH])
+    keep(dkv_ref, 1, slice(None), dkv[:, WIDTH:])
     scatter_kv.stage(0)
     lane_head = iota((SPAN, PAIR), 1) // HEAD_DIM
     diagonal = iota((SPAN, SPAN), 0) // BLOCKS == iota((SPAN, SPAN), 1) // BLOCKS
@@ -983,87 +1042,96 @@
     scatter_sorter.fold(2)
     scatter_sorter.stage(3)
     scatter_a.fold(3)
+    scatter_b.fold(3)
     write_sums[0].start()
-    scatter_b.fold(3)
-    write_sums[1].start()
     small_out[0:16, :] = total_b.result()
     small_out[16:24, :] = summed[8:16]
-    write_sums[5].start()
+    write_sums[3].start()
     scatter_woq.fold(3)
-    write_sums[2].start()
     write_out.wait()
     for copy in writes:
         copy.wait()
     each(tuple(gather) + (scatter_a, scatter_b, total_a, total_b), "close")
     scatter_kv.fold(3)
-    write_sums[3].start()
+    write_sums[1].start()
     scatter_sorter.fold(3)
-    write_sums[4].start()
+    write_sums[2].start()
     each((scatter_woq, scatter_kv, scatter_sorter), "close")
     for copy in write_sums:
         copy.wait()
 
 
 def update_kernel(lay, step_ref, *refs):
-    sources, targets, penalty_out, inputs, results = refs[:20], refs[20:34], refs[34], refs[35:55], refs[55:67]
-    in_sems, out_sems = refs[67:]
-    bring = [pltpu.make_async_copy(source, inputs[k], in_sems.at[k]) for k, source in enumerate(sources)]
-    begin(bring[2:] + bring[:2])
+    sources, targets, penalty_out, inputs, results = refs[:18], refs[18:32], refs[32], refs[33:51], refs[51:63]
+    in_sems, out_sems, row_sems = refs[63:]
+    bring = [pltpu.make_async_copy(source, inputs[k], in_sems.at[k]) for k, source in enumerate(sources) if k > 1]
     send = [
-        pltpu.make_async_copy(buffer, targets[k], out_sems.at[k])
-        for k, buffer in enumerate(tuple(inputs[:2]) + tuple(results))
+        pltpu.make_async_copy(buffer, targets[2 + k], out_sems.at[2 + k]) for k, buffer in enumerate(results)
     ]
-    feed_a, feed_b, woq, kv, sorter, sums = inputs[2:8]
-    masters = inputs[8:]
+    bring_rows, send_rows = [], []
+    for part in range(ROW_PARTS):
+        for which in range(2):
+            rows = slice(part * SEQ_LEN // ROW_PARTS, (part + 1) * SEQ_LEN // ROW_PARTS)
+            sem = row_sems.at[part, which]
+            bring_rows.append(pltpu.make_async_copy(sources[which].at[rows], inputs[which].at[rows], sem.at[0]))
+            send_rows.append(pltpu.make_async_copy(inputs[which].at[rows], targets[which].at[rows], sem.at[1]))
+    begin(bring_rows[:2] + bring + bring_rows[2:])
+    feed_sum, mixer_sum, sorter_sum, sums = inputs[2:6]
+    masters = inputs[6:]
     step_value = jnp.full((1, 128), step_ref[0], jnp.int32).astype(f32)
     scale_first = 1.0 / (1.0 - jnp.exp(step_value * math.log(beta_first)))[:, 0:1]
     scale_second = 1.0 / (1.0 - jnp.exp(step_value * math.log(beta_second)))[:, 0:1]
 
-    def adamw(which, index, grad, rate):
-        master, moment, second = [ref[index] for ref in masters[3 * which : 3 * which + 3]]
+    def adamw(which, grad, rate):
+        master, moment, second = [ref[...] for ref in masters[3 * which : 3 * which + 3]]
         moment_new = beta_first * moment + (1.0 - beta_first) * grad
         second_new = beta_second * second + (1.0 - beta_second) * grad * grad
         change = (moment_new * scale_first) / (jnp.sqrt(second_new * scale_second) + adam_eps)
         outs = results[3 * which : 3 * which + 3]
-        outs[0][index] = moment_new
-        outs[1][index] = second_new
-        outs[2][index] = master - rate * (change + weight_decay * master)
-
-    for copy in bring[2:]:
+        outs[0][...] = moment_new
+        outs[1][...] = second_new
+        outs[2][...] = master - rate * (change + weight_decay * master)
+        begin(send[3 * which : 3 * which + 3])
+
+    for copy, onward in zip(bring_rows[:2], send_rows[:2]):
         copy.wait()
-    half = feed_a.shape[2]
-    for j in range(2):
-        adamw(1, (ALLR, j, slice(0, half)), feed_a[j], rate_feed)
-        adamw(1, (ALLR, j, slice(half, 2 * half)), feed_b[j], rate_feed)
-    begin(send[5:8])
-    for copy in bring[:2]:
+        onward.start()
+    for copy in bring:
         copy.wait()
-    begin(send[:2])
-    for j, grad in enumerate((woq[1], kv[0], kv[1], woq[0])):
-        adamw(0, (ALLR, j, ALLR), grad, rate_mixer)
-    begin(send[2:5])
-    r, c = masters[6].shape
-    pack = packing(r, c)
-    deep = r // pack
-    grad = jnp.concatenate([sorter[0][:, k * c : (k + 1) * c] for k in range(pack)], axis=0) if pack > 1 else sorter[0]
-    adamw(2, (ALLR, ALLR), grad, rate_sorter)
-    begin(send[8:11])
+    adamw(1, feed_sum[...], rate_feed)
+    adamw(0, mixer_sum[...], rate_mixer)
+    adamw(2, sorter_sum[...], rate_sorter)
+    for copy, onward in zip(bring_rows[2:], send_rows[2:]):
+        copy.wait()
+        onward.start()
     rows = jnp.concatenate([joined_row(sums[0:4, :]), joined_row(sums[4:8, :])], axis=0)
     own = spot(masters[9].shape[1])
-    grad = sum(mm(part, own, 1, 1) for part in three_parts(rows))
-    adamw(3, (ALLR, ALLR), grad, rate_gains)
-    begin(send[11:14])
+    adamw(3, sum(mm(part, own, 1, 1) for part in three_parts(rows)), rate_gains)
     entropy = jnp.sum(sums[8:9, :], axis=1, keepdims=True)
     penalty_out[...] = jnp.broadcast_to(entropy / (sums[16:17, 0:1] * HEADS), (1, 128))
-    for copy in send:
+    for copy in send + send_rows:
         copy.wait()
+
+
+def flat_rows(array):
+    if array.ndim != 3 or array.shape[2] % 128:
+        return array
+    rows, parts, width = array.shape
+    return array.reshape(rows, parts, width // 128, 128).transpose(0, 2, 1, 3).reshape(-1, 128)
+
+
+def unflat_rows(flat, like):
+    if flat.shape == like.shape:
+        return flat
+    rows, parts, width = like.shape
+    return flat.reshape(rows, width // 128, parts, 128).transpose(0, 2, 1, 3).reshape(like.shape)
 
 
 def shape(dims, dtype):
     return jax.ShapeDtypeStruct(dims, dtype)
 
 
-LIMIT = 63 * 1024 * 1024
+LIMIT = 65400 * 1024
 TOK = (SEQ_LEN, WIDTH)
 
 
@@ -1074,8 +1142,11 @@
     feed_item, pair_item = Item(lay, 2, r, half), Item(lay, 2, r, c)
     gathers = (pair_item, sorter_item, pair_item, feed_item, feed_item)
     scatters = (feed_item, feed_item, pair_item, pair_item, sorter_item)
+    sums = [shape(jax.eval_shape(flat_rows, array).shape, f32) for array in (feed, mixer, sorter)]
+    sums.append(shape((24, 128), f32))
     vm = pltpu.VMEM
-    count = 5 * (Gather.count(lay) + Scatter.count(lay)) + 2 * Total.count(lay)
+    recvs = 5 * (Gather.count(lay) + Scatter.count(lay)) + 2 * Total.count(lay)
+    sends = 5 * (Gather.sends(lay) + Scatter.sends(lay)) + 2 * Total.sends(lay)
     scratch = (
         [vm(item.shard(), bf16) for item in gathers]
         + [vm(item.full(), bf16) for item in gathers + scatters]
@@ -1090,11 +1161,10 @@
         ]
         + [vm(TOK, f32)] * 2
         + [vm((lay.mp, 16, 128), f32), vm((lay.dp, 16, 128), f32)] * 2
-        + [pltpu.SemaphoreType.DMA((count,))] * 2
+        + [pltpu.SemaphoreType.DMA((sends,)), pltpu.SemaphoreType.DMA((recvs,))]
         + [pltpu.SemaphoreType.DMA((14,))]
         + [vm(mixer.shape, f32), vm(feed.shape, f32), vm(sorter.shape, f32)]
-        + [vm(item.shard(), f32) for item in scatters]
-        + [vm((24, 128), f32)]
+        + [vm(total.shape, f32) for total in sums]
     )
     for item in scatters:
         scratch += Scatter.buffers(item)
@@ -1103,10 +1173,9 @@
     return pl.pallas_call(
         functools.partial(step_kernel, lay, gathers, scatters, total_tokens),
         out_shape=[shape(TOK, bf16), shape(TOK, f32)]
-        + [shape(item.shard(), f32) for item in scatters]
-        + [shape((24, 128), f32)],
+        + sums,
         in_specs=[outside] * 2 + [inside] * 2 + [outside] * 3,
-        out_specs=[outside] * 8,
+        out_specs=[outside] * 6,
         scratch_shapes=scratch,
         compiler_params=pltpu.CompilerParams(collective_id=0, has_side_effects=True, vmem_limit_bytes=LIMIT),
         name="step",
@@ -1124,7 +1193,8 @@
         out_specs=[outside] * len(moved) + [pl.BlockSpec(memory_space=pltpu.VMEM)],
         scratch_shapes=[pltpu.VMEM(array.shape, array.dtype) for array in arrays]
         + [pltpu.VMEM(state.shape, f32) for state in states]
-        + [pltpu.SemaphoreType.DMA((len(arrays),)), pltpu.SemaphoreType.DMA((len(moved),))],
+        + [pltpu.SemaphoreType.DMA((len(arrays),)), pltpu.SemaphoreType.DMA((len(moved),))]
+        + [pltpu.SemaphoreType.DMA((ROW_PARTS, 2, 2))],
         compiler_params=pltpu.CompilerParams(vmem_limit_bytes=LIMIT),
         name="update",
     )(step_count, *arrays)
@@ -1168,7 +1238,9 @@
         mixer_weights, mixer_moment, mixer_second, feed_weights, feed_moment, feed_second,
         sorter_weights, sorter_moment, sorter_second, norm_gains, gain_moment, gain_second,
     )
-    block_output, token_grad, penalty, states = run_update(lay, step_count, block_output, token_grad, sums, states)
+    flat = [flat_rows(state) for state in states]
+    block_output, token_grad, penalty, flat = run_update(lay, step_count, block_output, token_grad, sums, flat)
+    states = [unflat_rows(new, state) for new, state in zip(flat, states)]
     return (block_output, token_grad, penalty[0, :1], *states)
 
 

time: 102 us -> 98.1 us (0.962)
  Pallas kernels: 101 us -> 96.4 us
    pallas_call x1, Pallas kernels: 95.2 us -> 91.5 us  [run_step(): pl.pallas_call(functools.partial(step_kernel, lay, gathers, scatters, tot...]
where the time goes in v4:
time: 98.1 us; the launch traced here: 97.9 us
  Pallas kernels  96.4 us (98%)
  between operations  1.48 us (2%)
    pallas_call x1, Pallas kernels, run_step(): pl.pallas_call(functools.partial(step_kernel, lay, gathers, scatters, tot...  91.5 us
    pallas_call x1, Pallas kernels, run_update(): pl.pallas_call(functools.partial(update_kernel, lay), out_shape=moved + [...  4.83 us

profile of v4, /device:TPU:0, one launch (start us, length us, event | category | flops | bytes accessed | tf_op | source)
XLA Modules:
  0.0 97.9 jit_solution(9195517258845861814)
XLA Ops:
  1.3 91.5 %step.1 = (bf16[1024,512]{1,0:T(8,128)(2,1)}, f32[1024,512]{1,0:T(8,128)}, f32[512,128]{1,0:T(8,128)}, f32[256,128]{1,0:T(8,128)}, f32[64,64]{1,0:T(8,128)}, /*index=5*/f32[24,128]{1,0:T(8,128)}) custom-call(bf16[1024,512]{1,0:T(8,128)(2,1)} %tokens_ref.1, bf16[1024,512]{1,0:T(8,128)(2,1)} %cotangent_ref.1, s32[4,1024]{1,0:T(4,128)} %segment_ref.1, ...), custom_call_target="tpu_custom_call" | custom-call | tf_op jit(solution)/shard_map/step/pallas_call | solution.py:1173
  92.8 4.8 %update.1 = (bf16[1024,512]{1,0:T(8,128)(2,1)}, f32[1024,512]{1,0:T(8,128)}, f32[256,128]{1,0:T(8,128)}, f32[256,128]{1,0:T(8,128)}, f32[256,128]{1,0:T(8,128)},...) custom-call(s32[1]{0:T(128)S(6)} %copy.37.step_ref, ...), custom_call_target="tpu_custom_call" | custom-call | tf_op jit(solution)/shard_map/update/pallas_call | solution.py:1189

commit v5 on v4

--- a/solution.py
+++ b/solution.py
@@ -310,15 +310,22 @@
 
 
 class Scatter:
-    def __init__(self, item, full, buffers, write, sems):
-        self.item, self.full, self.write = item, full, write
+    def __init__(self, item, full, buffers, write, sems, high_last=True):
+        self.item, self.full, self.write, self.high_last = item, full, write, high_last
         self.lane = sems.lane(self.sends(item.lay))
         self.core, self.one_a, self.one_b, self.two_a, self.two_b, self.top_a, self.top_b = buffers
 
     @staticmethod
-    def buffers(item):
+    def buffers(item, high_last=True):
         lay = item.lay
         half = item.half
+        if not high_last:
+            return Scatter.buffers(item)[:3] + [
+                pltpu.VMEM((lay.H - 1, *item.dims(lay.L, rows=half, wide=1)), bf16),
+                pltpu.VMEM((lay.H - 1, *item.dims(rows=half, wide=lay.X)), bf16),
+                pltpu.VMEM((lay.L - 1, *item.dims(rows=half, wide=1)), bf16),
+                pltpu.VMEM((lay.X - 1, *item.dims(rows=half, wide=1)), bf16),
+            ]
         return [
             pltpu.VMEM((lay.C - 1, *item.dims(lay.H, lay.L, wide=lay.X)), bf16),
             pltpu.VMEM((lay.X - 1, *item.dims(lay.H, lay.L, rows=half, wide=1)), bf16),
@@ -363,7 +370,35 @@
                     self.one_b, (k - 1, *item.at((ALLR,), 0, lay.X)),
                     to(h, ll, x, c),
                 )
-        if number == 2:
+        if number == 2 and not self.high_last:
+            for k in range(1, lay.H):
+                hh = (h + k) % lay.H
+                send(
+                    self.one_a, (0, *item.at((hh, ALLR), 0)),
+                    self.two_a, (k - 1, *item.at((ALLR,), 0)),
+                    to(hh, l, x, c),
+                )
+                send(
+                    self.one_b, (0, *item.at((hh,), 0, lay.X)),
+                    self.two_b, (k - 1, *item.at((), 0, lay.X)),
+                    to(hh, l, x, c),
+                )
+        if number == 3 and not self.high_last:
+            for k in range(1, lay.L):
+                ll = (l + k) % lay.L
+                send(
+                    self.two_a, (0, *item.at((ll,), 0)),
+                    self.top_a, (k - 1, *item.at((), 0)),
+                    to(h, ll, x, c),
+                )
+            for k in range(1, lay.X):
+                xx = (x + k) % lay.X
+                send(
+                    self.two_b, (0, *item.at((), xx)),
+                    self.top_b, (k - 1, *item.at((), 0)),
+                    to(h, l, xx, c),
+                )
+        if number == 2 and self.high_last:
             for k in range(1, lay.L):
                 ll = (l + k) % lay.L
                 send(
@@ -378,7 +413,7 @@
                     self.two_b, (k - 1, *item.at((ALLR,), 0)),
                     to(h, l, xx, c),
                 )
-        if number == 3:
+        if number == 3 and self.high_last:
             for k in range(1, lay.H):
                 hh = (h + k) % lay.H
                 for src, dst in ((self.two_a, self.top_a), (self.two_b, self.top_b)):
@@ -427,7 +462,10 @@
                 )
 
             over_high(one)
-        if number == 2:
+        if number == 2 and not self.high_last:
+            add(self.two_a, item.at((ALLR,), 0), self.one_a, (0, *item.at((h, ALLR), 0)), lay.H - 1)
+            add(self.two_b, item.at((), 0, lay.X), self.one_b, (0, *item.at((h,), 0, lay.X)), lay.H - 1)
+        if number == 2 and self.high_last:
 
             def two(high):
                 add(self.two_a, item.at((high,), 0), self.one_a, (0, *item.at((high, l), 0)), lay.L - 1)
@@ -435,11 +473,14 @@
 
             over_high(two)
         if number == 3:
-            for rows, mine, others in (
-                (item.rows_a(), self.two_a, self.top_a), (item.rows_b(), self.two_b, self.top_b),
+            own_a, own_b = item.at((h,), 0), item.at((h,), 0)
+            if not self.high_last:
+                own_a, own_b = item.at((l,), 0), item.at((), x)
+            for rows, mine, own, others in (
+                (item.rows_a(), self.two_a, own_a, self.top_a), (item.rows_b(), self.two_b, own_b, self.top_b),
             ):
-                total = mine[(0, *item.at((h,), 0))].astype(f32)
-                for other in range(lay.H - 1):
+                total = mine[(0, *own)].astype(f32)
+                for other in range(others.shape[0]):
                     total = total + others[(other, *item.at((), 0))].astype(f32)
                 total = total.reshape(item.J, item.half, item.c)
                 for j in range(item.J):
@@ -546,9 +587,9 @@
         del scratch[:count]
         return taken
 
-    shards, weights_full, grads_full = pop(5), pop(5), pop(5)
+    shards, weights_full, grads_full = pop(5), pop(5), pop(6)
     kv_ref, sorter_full, woq_ref, feed_a_ref, feed_b_ref = weights_full
-    dfeed_a_ref, dfeed_b_ref, dwoq_ref, dkv_ref, dsorter_full = grads_full
+    dfeed_a_ref, dfeed_b_ref, dwo_ref, dq_ref, dkv_ref, dsorter_full = grads_full
     x_ref, cot_ref, out_ref, grad_ref = pop(4)
     (
         sorter_ref, first_ref, q_ref, k_ref, v_ref, sk_ref, sv_ref, place_k_ref, place_v_ref,
@@ -576,7 +617,7 @@
         Gather(item, shard, full, sems, k < 4)
         for k, (item, shard, full) in enumerate(zip(gathers, shards, weights_full))
     ]
-    early = tuple(gather[:2])
+    early = (gather[0], gather[1])
     gather_woq, gather_a, gather_b = gather[2:]
     scatters = []
     feed_sum, mixer_sum, sorter_sum, small_out = sums = pop(4)
@@ -607,17 +648,18 @@
     writers = (
         write_to(feed_sum, (0, 1), 0, half_width),
         write_to(feed_sum, (0, 1), half_width, half_width),
-        write_to(mixer_sum, mixer_order[:2], 0, scatter_items[2].c),
+        write_to(mixer_sum, mixer_order[:1], 0, scatter_items[2].c),
+        write_to(mixer_sum, mixer_order[1:2], 0, scatter_items[2].c),
         write_to(mixer_sum, mixer_order[2:], 0, scatter_items[2].c),
         write_sorter,
     )
-    for item, full, write in zip(scatter_items, grads_full, writers):
-        scatters.append(Scatter(item, full, pop(7), write, sems))
+    for k, (item, full, write) in enumerate(zip(scatter_items, grads_full, writers)):
+        scatters.append(Scatter(item, full, pop(7), write, sems, k > 0))
     write_sums = [
         pltpu.make_async_copy(buffer, target, copy_sems.at[8 + k])
         for k, (buffer, target) in enumerate(zip(sums, sums_hbm))
     ]
-    scatter_a, scatter_b, scatter_woq, scatter_kv, scatter_sorter = scatters
+    scatter_a, scatter_b, scatter_wo, scatter_q, scatter_kv, scatter_sorter = scatters
     total_a = Total(lay, near_a, far_a, sems)
     total_b = Total(lay, near_b, far_b, sems)
 
@@ -698,7 +740,7 @@
     gather_a.stage(1)
     gather_b.landed()
     gather_b.stage(1)
-    each(early, "landed")
+    early[1].landed()
 
     def weight(ref, j, cols=slice(None)):
         if len(ref.shape) == 6:
@@ -726,6 +768,13 @@
         for k in range(pack):
             sorter_ref[rows[k], cols] = tile[:, k * c : (k + 1) * c]
     logits = mm(means, sorter_ref[...])
+    def store(index, value):
+        sink_ref[index] = value
+
+    logs, weights = sinkhorn(logits, allowed, group_matrix(), store)
+    logs_ref[...] = logs
+    probs = weights.astype(bf16)
+    early[0].landed()
     for tile in range(TILES):
         rows = slice(tile * ROWS, (tile + 1) * ROWS)
         k_ref[rows, :] = mm(first_ref[rows, :], weight(kv_ref, 0)).astype(bf16)
@@ -733,13 +782,6 @@
 
     place_k_ref[...] = by_place(k_ref[...])
     place_v_ref[...] = by_place(v_ref[...])
-
-    def store(index, value):
-        sink_ref[index] = value
-
-    logs, weights = sinkhorn(logits, allowed, group_matrix(), store)
-    logs_ref[...] = logs
-    probs = weights.astype(bf16)
     gather_a.landed()
     gather_a.stage(2)
     gather_woq.landed()
@@ -879,7 +921,9 @@
     write_out.start()
     feed_weights(dfeed_b_ref)
     scatter_b.stage(0)
-    keep(dwoq_ref, 0, slice(None), mm(grad_ref[...].astype(bf16), mixed_ref[...], 0, 0))
+    keep(dwo_ref, 0, slice(None), mm(grad_ref[...].astype(bf16), mixed_ref[...], 0, 0))
+
+    scatter_wo.stage(0)
 
     def start(tile, carry):
         rows = pl.ds(pl.multiple_of(tile * ROWS, ROWS), ROWS)
@@ -891,6 +935,8 @@
     scatter_a.stage(2)
     scatter_b.fold(0)
     scatter_b.stage(1)
+    scatter_wo.fold(0)
+    scatter_wo.stage(1)
 
     def attend_back(step, carry):
         units = [(step * UNROLL + k, group) for k in range(UNROLL) for group in range(GROUPS)]
@@ -924,12 +970,10 @@
         return carry
 
     lax.fori_loop(0, steps, attend_back, 0)
-    scatter_a.fold(2)
-    scatter_a.stage(3)
     first = first_ref[...]
     q_ref[...] = pre_ref[:, :WIDTH]
-    keep(dwoq_ref, 1, slice(None), mm(first, q_ref[...], 0, 0))
-    scatter_woq.stage(0)
+    keep(dq_ref, 0, slice(None), mm(first, q_ref[...], 0, 0))
+    scatter_q.stage(0)
     weights = sink_ref[2 * SINK_ITERS - 1]
     same_head = iota((LOGITS, LOGITS), 0) // BLOCKS == iota((LOGITS, LOGITS), 1) // BLOCKS
     turned = jnp.where(same_head, jnp.concatenate([weights] * HEADS, axis=0), 0.0).T
@@ -948,12 +992,14 @@
     rearrange(back, sk_ref, sv_ref, add_pair)
     scatter_b.fold(1)
     scatter_b.stage(2)
-    scatter_woq.fold(0)
-    scatter_woq.stage(1)
+    scatter_q.fold(0)
+    scatter_q.stage(1)
     dkv = mm(first, jnp.concatenate([k_ref[...], v_ref[...]], axis=1), 0, 0)
     keep(dkv_ref, 0, slice(None), dkv[:, :WIDTH])
     keep(dkv_ref, 1, slice(None), dkv[:, WIDTH:])
     scatter_kv.stage(0)
+    scatter_wo.fold(1)
+    scatter_wo.stage(2)
     lane_head = iota((SPAN, PAIR), 1) // HEAD_DIM
     diagonal = iota((SPAN, SPAN), 0) // BLOCKS == iota((SPAN, SPAN), 1) // BLOCKS
     folded = []
@@ -989,6 +1035,8 @@
     scatter_sorter.stage(0)
     scatter_b.fold(2)
     scatter_b.stage(3)
+    scatter_a.fold(2)
+    scatter_a.stage(3)
     spread_ref[...] = mm(logit_grad, sorter_ref[...], 1, 1) / BLOCK
     here = ROWS // BLOCK
 
@@ -1017,8 +1065,10 @@
 
     lax.fori_loop(0, TILES // 2, finish, 0)
     write_rows(0)
-    scatter_woq.fold(1)
-    scatter_woq.stage(2)
+    scatter_q.fold(1)
+    scatter_q.stage(2)
+    scatter_wo.fold(2)
+    scatter_wo.stage(3)
     scatter_sorter.fold(0)
     scatter_sorter.stage(1)
     lax.fori_loop(TILES // 2, TILES, finish, 0)
@@ -1032,8 +1082,8 @@
     ], axis=0))
     scatter_kv.fold(1)
     scatter_kv.stage(2)
-    scatter_woq.fold(2)
-    scatter_woq.stage(3)
+    scatter_q.fold(2)
+    scatter_q.stage(3)
     scatter_sorter.fold(1)
     scatter_sorter.stage(2)
     total_b.over_dp()
@@ -1047,16 +1097,17 @@
     small_out[0:16, :] = total_b.result()
     small_out[16:24, :] = summed[8:16]
     write_sums[3].start()
-    scatter_woq.fold(3)
+    scatter_wo.fold(3)
+    scatter_q.fold(3)
     write_out.wait()
     for copy in writes:
         copy.wait()
-    each(tuple(gather) + (scatter_a, scatter_b, total_a, total_b), "close")
+    each(tuple(gather) + (scatter_a, scatter_b, scatter_wo, total_a, total_b), "close")
     scatter_kv.fold(3)
     write_sums[1].start()
     scatter_sorter.fold(3)
     write_sums[2].start()
-    each((scatter_woq, scatter_kv, scatter_sorter), "close")
+    each((scatter_q, scatter_kv, scatter_sorter), "close")
     for copy in write_sums:
         copy.wait()
 
@@ -1139,14 +1190,14 @@
     r, c, half = mixer.shape[0], mixer.shape[2], feed.shape[2] // 2
     pack = packing(*sorter.shape)
     sorter_item = Item(lay, 1, sorter.shape[0] // pack, sorter.shape[1] * pack)
-    feed_item, pair_item = Item(lay, 2, r, half), Item(lay, 2, r, c)
+    feed_item, pair_item, one_item = Item(lay, 2, r, half), Item(lay, 2, r, c), Item(lay, 1, r, c)
     gathers = (pair_item, sorter_item, pair_item, feed_item, feed_item)
-    scatters = (feed_item, feed_item, pair_item, pair_item, sorter_item)
+    scatters = (feed_item, feed_item, one_item, one_item, pair_item, sorter_item)
     sums = [shape(jax.eval_shape(flat_rows, array).shape, f32) for array in (feed, mixer, sorter)]
     sums.append(shape((24, 128), f32))
     vm = pltpu.VMEM
-    recvs = 5 * (Gather.count(lay) + Scatter.count(lay)) + 2 * Total.count(lay)
-    sends = 5 * (Gather.sends(lay) + Scatter.sends(lay)) + 2 * Total.sends(lay)
+    recvs = 5 * Gather.count(lay) + 6 * Scatter.count(lay) + 2 * Total.count(lay)
+    sends = 5 * Gather.sends(lay) + 6 * Scatter.sends(lay) + 2 * Total.sends(lay)
     scratch = (
         [vm(item.shard(), bf16) for item in gathers]
         + [vm(item.full(), bf16) for item in gathers + scatters]
@@ -1166,8 +1217,8 @@
         + [vm(mixer.shape, f32), vm(feed.shape, f32), vm(sorter.shape, f32)]
         + [vm(total.shape, f32) for total in sums]
     )
-    for item in scatters:
-        scratch += Scatter.buffers(item)
+    for k, item in enumerate(scatters):
+        scratch += Scatter.buffers(item, k > 0)
     inside = pl.BlockSpec(memory_space=pltpu.VMEM)
     outside = pl.BlockSpec(memory_space=pl.ANY)
     return pl.pallas_call(

time: 98.1 us -> 96.2 us (0.981)
  Pallas kernels: 96.4 us -> 94.5 us
    pallas_call x1, Pallas kernels: 91.5 us -> 89.6 us  [run_step(): pl.pallas_call(functools.partial(step_kernel, lay, gathers, scatters, tot...]
where the time goes in v5:
time: 96.2 us; the launch traced here: 95.9 us
  Pallas kernels  94.5 us (98%)
  between operations  1.48 us (2%)
    pallas_call x1, Pallas kernels, run_step(): pl.pallas_call(functools.partial(step_kernel, lay, gathers, scatters, tot...  89.6 us
    pallas_call x1, Pallas kernels, run_update(): pl.pallas_call(functools.partial(update_kernel, lay), out_shape=moved + [...  4.83 us

profile of v5, /device:TPU:0, one launch (start us, length us, event | category | flops | bytes accessed | tf_op | source)
XLA Modules:
  0.0 95.9 jit_solution(13645988007534965731)
XLA Ops:
  1.3 89.6 %step.1 = (bf16[1024,512]{1,0:T(8,128)(2,1)}, f32[1024,512]{1,0:T(8,128)}, f32[512,128]{1,0:T(8,128)}, f32[256,128]{1,0:T(8,128)}, f32[64,64]{1,0:T(8,128)}, /*index=5*/f32[24,128]{1,0:T(8,128)}) custom-call(bf16[1024,512]{1,0:T(8,128)(2,1)} %tokens_ref.1, bf16[1024,512]{1,0:T(8,128)(2,1)} %cotangent_ref.1, s32[4,1024]{1,0:T(4,128)} %segment_ref.1, ...), custom_call_target="tpu_custom_call" | custom-call | tf_op jit(solution)/shard_map/step/pallas_call | solution.py:1224
  90.9 4.8 %update.1 = (bf16[1024,512]{1,0:T(8,128)(2,1)}, f32[1024,512]{1,0:T(8,128)}, f32[256,128]{1,0:T(8,128)}, f32[256,128]{1,0:T(8,128)}, f32[256,128]{1,0:T(8,128)},...) custom-call(s32[1]{0:T(128)S(6)} %copy.37.step_ref, ...), custom_call_target="tpu_custom_call" | custom-call | tf_op jit(solution)/shard_map/update/pallas_call | solution.py:1240

commit v6 on v5

--- a/solution.py
+++ b/solution.py
@@ -247,7 +247,7 @@
 class Gather:
     def __init__(self, item, shard, full, sems, high_first=True):
         self.item, self.shard, self.full, self.high_first = item, shard, full, high_first
-        self.lane = sems.lane(self.sends(item.lay))
+        self.lane = sems.lane(self.sends(item.lay, high_first))
 
     def stage(self, number):
         item, lay, full = self.item, self.item.lay, self.full
@@ -301,12 +301,12 @@
         self.lane.close()
 
     @staticmethod
-    def sends(lay):
-        return max(2 * (lay.H - 1), lay.L + lay.X - 2, lay.C - 1)
+    def sends(lay, high_first):
+        return max((lay.H - 1) * (1 if high_first else 2), lay.L + lay.X - 2, lay.C - 1)
 
     @staticmethod
-    def count(lay):
-        return 2 * (lay.H - 1) + 2 * (lay.L + lay.X - 2) + (lay.C - 1)
+    def count(lay, high_first):
+        return (lay.H - 1) * (1 if high_first else 2) + 2 * (lay.L + lay.X - 2) + (lay.C - 1)
 
 
 class Scatter:
@@ -1196,8 +1196,8 @@
     sums = [shape(jax.eval_shape(flat_rows, array).shape, f32) for array in (feed, mixer, sorter)]
     sums.append(shape((24, 128), f32))
     vm = pltpu.VMEM
-    recvs = 5 * Gather.count(lay) + 6 * Scatter.count(lay) + 2 * Total.count(lay)
-    sends = 5 * Gather.sends(lay) + 6 * Scatter.sends(lay) + 2 * Total.sends(lay)
+    recvs = 4 * Gather.count(lay, True) + Gather.count(lay, False) + 6 * Scatter.count(lay) + 2 * Total.count(lay)
+    sends = 4 * Gather.sends(lay, True) + Gather.sends(lay, False) + 6 * Scatter.sends(lay) + 2 * Total.sends(lay)
     scratch = (
         [vm(item.shard(), bf16) for item in gathers]
         + [vm(item.full(), bf16) for item in gathers + scatters]

time: 96.2 us -> 96 us (level)
  no operation moved by 1% of the time
where the time goes in v6:
time: 96 us; the launch traced here: 95.7 us
  Pallas kernels  94.3 us (98%)
  between operations  1.48 us (2%)
    pallas_call x1, Pallas kernels, run_step(): pl.pallas_call(functools.partial(step_kernel, lay, gathers, scatters, tot...  89.4 us
    pallas_call x1, Pallas kernels, run_update(): pl.pallas_call(functools.partial(update_kernel, lay), out_shape=moved + [...  4.83 us

profile of v6, /device:TPU:0, one launch (start us, length us, event | category | flops | bytes accessed | tf_op | source)
XLA Modules:
  0.0 95.7 jit_solution(4624098121730554400)
XLA Ops:
  1.3 89.4 %step.1 = (bf16[1024,512]{1,0:T(8,128)(2,1)}, f32[1024,512]{1,0:T(8,128)}, f32[512,128]{1,0:T(8,128)}, f32[256,128]{1,0:T(8,128)}, f32[64,64]{1,0:T(8,128)}, /*index=5*/f32[24,128]{1,0:T(8,128)}) custom-call(bf16[1024,512]{1,0:T(8,128)(2,1)} %tokens_ref.1, bf16[1024,512]{1,0:T(8,128)(2,1)} %cotangent_ref.1, s32[4,1024]{1,0:T(4,128)} %segment_ref.1, ...), custom_call_target="tpu_custom_call" | custom-call | tf_op jit(solution)/shard_map/step/pallas_call | solution.py:1224
  90.7 4.8 %update.1 = (bf16[1024,512]{1,0:T(8,128)(2,1)}, f32[1024,512]{1,0:T(8,128)}, f32[256,128]{1,0:T(8,128)}, f32[256,128]{1,0:T(8,128)}, f32[256,128]{1,0:T(8,128)},...) custom-call(s32[1]{0:T(128)S(6)} %copy.37.step_ref, ...), custom_call_target="tpu_custom_call" | custom-call | tf_op jit(solution)/shard_map/update/pallas_call | solution.py:1240
